TPU v7x, 32 devices: a whole 2x2x4 slice. The times are simulated.
32 devices in a mesh: image: 4 (over z), space: 8 (over y, x, core).
Axes of the slice: x: 2, y: 2, z: 4, core: 2. Of those that a mesh axis runs over, the one named last changes fastest.
Arguments:
- field: float32 [4, 32, 256, 512], P('image', 'space'), may hold values from -2.5 to 2.5
- mobility: float32 [32, 256, 512], P('space'), may hold values from 0.2 to 1
- fractions: float32 [4], P('image'), may hold values from 0.3 to 0.5
- sides: int32 [4], P('image'), may hold values from 0 to 1, as said below
Outputs:
- blended: float32 [4, 32, 256, 512], P('image', 'space')
Inputs may be any that keep to these rules, and one draw needn't show every extreme that they name: `sides`: the first image always names the next one (1), the last image the previous one (0); the others name either.
All inputs are finite; a program needn't handle non-finite values.
Results may differ from a plain program's by a relative error of at most 0.00002.
Values sent between devices are 32-bit elements; how exact they have to be, the bound alone decides.
No kernel may reach another device: no remote copies, remote signals or barrier semaphores. Data moves between devices by JAX's collectives and lax.ppermute only.
A program may use at most 128 MiB of HBM per device.

v0:
```python
import jax
import jax.numpy as jnp
from jax import lax
from jax.sharding import PartitionSpec as P

STEPS = 4


DT = 0.1
EPS2 = 1.5


def with_halo(cells, sides, width):
    for axis, dim in sides:
        count = lax.axis_size(axis)
        ends = count - 1
        head = lax.slice_in_dim(cells, 0, width, axis=dim)
        tail = lax.slice_in_dim(cells, cells.shape[dim] - width, cells.shape[dim], axis=dim)
        cells = jnp.concatenate(
            [
                lax.ppermute(tail, axis, [(i, (i + 1) % count) for i in range(ends)]),
                cells,
                lax.ppermute(head, axis, [((i + 1) % count, i) for i in range(ends)]),
            ],
            axis=dim,
        )
    return cells


def passed_along(x, axis, by):
    devices = lax.axis_size(axis)
    pairs = [(i, i + by) for i in range(devices) if 0 <= i + by < devices]
    return lax.ppermute(x, axis, pairs)


def advance(phi, xpad, mob):
    padded = jnp.pad(xpad, ((0, 0), (1, 1), (1, 1)))
    beside = padded[2:, 1:-1, 1:-1] + padded[:-2, 1:-1, 1:-1]
    beside = beside + padded[1:-1, 2:, 1:-1] + padded[1:-1, :-2, 1:-1]
    beside = beside + padded[1:-1, 1:-1, 2:] + padded[1:-1, 1:-1, :-2]
    return phi + DT * mob * (EPS2 * (beside - 6.0 * phi) + phi - phi * phi * phi)


def local(field, mobility, fractions, sides):
    phi = field[0]
    for step in range(STEPS):
        xpad = with_halo(phi, (("space", 0),), 1)
        phi = advance(phi, xpad, mobility)
    upper = passed_along(phi, "image", -1)
    lower = passed_along(phi, "image", 1)
    neighbour = jnp.where(sides[0] == 1, upper, lower)
    blended = phi + fractions[0] * (neighbour - phi)
    return blended[None]


def solution(mesh):
    return jax.shard_map(
        local,
        mesh=mesh,
        in_specs=(P("image", "space", None, None), P("space", None, None), P("image"), P("image")),
        out_specs=P("image", "space", None, None),
        check_vma=False,
    )
```

profile of v0, /device:TPU:29, one launch (start us, length us, event | category | flops | bytes accessed | tf_op | source)
XLA Modules:
  0.0 131.7 jit_solution(966505212961937680)
XLA Ops:
  0.0 0.0 copy-start.1
  0.0 1.4 %slice_bitcast_fusion = (f32[1,256,512]{2,1,0:T(8,128)S(1)}, f32[1,256,512]{2,1,0:T(8,128)S(1)}) fusion(f32[1,4,256,512]{3,2,1,0:T(8,128)} %param.4), kind=kLoop, calls=%fused_computation.72 | loop fusion | bytes 2097152 | tf_op jit(solution)/shard_map/slice | solution.py:18
  1.4 2.6 %collective-permute-start = (f32[1,256,512]{2,1,0:T(8,128)S(1)}, f32[1,256,512]{2,1,0:T(8,128)S(1)}, u32[]{:S(2)}, u32[]{:S(2)}) collective-permute-start(f32[1,256,512]{2,1,0:T(8,128)S(1)} %get-tuple-element.12), channel_id=1, source_target_pairs={{1,0},{2,1},{3,2},{4,3},{5,4},{6,5},{7,6},{9,8},{10,9},{11,10},{12... | collective-permute-start | bytes 1572872 | tf_op jit(solution)/shard_map/ppermute | solution.py:23
  4.0 3.0 %collective-permute-start.1 = (f32[1,256,512]{2,1,0:T(8,128)S(1)}, f32[1,256,512]{2,1,0:T(8,128)S(1)}, u32[]{:S(2)}, u32[]{:S(2)}) collective-permute-start(f32[1,256,512]{2,1,0:T(8,128)S(1)} %get-tuple-element.11), channel_id=1, source_target_pairs={{0,1},{1,2},{2,3},{3,4},{4,5},{5,6},{6,7},{8,9},{9,10},{10,11},{11... | collective-permute-start | bytes 1572872 | tf_op jit(solution)/shard_map/ppermute | solution.py:21
  7.0 5.2 %collective-permute-done = f32[1,256,512]{2,1,0:T(8,128)S(1)} collective-permute-done((f32[1,256,512]{2,1,0:T(8,128)S(1)}, f32[1,256,512]{2,1,0:T(8,128)S(1)}, u32[]{:S(2)}, u32[]{:S(2)}) %collective-permute-start) | collective-permute-done | bytes 524320 | tf_op jit(solution)/shard_map/ppermute | solution.py:23
  12.3 4.5 %collective-permute-done.1 = f32[1,256,512]{2,1,0:T(8,128)S(1)} collective-permute-done((f32[1,256,512]{2,1,0:T(8,128)S(1)}, f32[1,256,512]{2,1,0:T(8,128)S(1)}, u32[]{:S(2)}, u32[]{:S(2)}) %collective-permute-start.1) | collective-permute-done | bytes 524320 | tf_op jit(solution)/shard_map/ppermute | solution.py:21
  16.8 0.0 copy-done.1
  16.8 0.0 copy-start
  16.8 2.3 %select_maximum_fusion.6 = f32[6,258,514]{2,1,0:T(8,128)S(1)} fusion(f32[1,256,512]{2,1,0:T(8,128)S(1)} %collective-permute-done, f32[4,256,512]{2,1,0:T(8,128)S(1)} %bitcast.10, f32[1,256,512]{2,1,0:T(8,128)S(1)} %collective-permute-done.1), kind=kLoop, calls=%fused_computation.10 | loop fusion | flops 11935080 | bytes 6328416 | tf_op jit(solution)/shard_map/concatenate | solution.py:19
  19.1 0.0 copy-done
  19.1 2.3 %fusion.5 = f32[4,256,512]{2,1,0:T(8,128)S(1)} fusion(f32[4,256,512]{2,1,0:T(8,128)S(1)} %bitcast.11, f32[6,258,514]{2,1,0:T(8,128)S(1)} %select_maximum_fusion.6, f32[1,256,512]{2,1,0:T(8,128)S(1)} %collective-permute-done.1, f32[1,256,512]{2,1,0:T(8,128)S(1)} %collective-permute-done, f32[4,256,512]{2,1,0:T(8,128)S(1)} %copy-done), kind=kLoop, calls=%fused_computation.21 | loop fusion | flops 8912896 | bytes 15728640 | tf_op jit(solution)/shard_map/add | solution.py:41
  21.4 0.1 fusion.33
  21.4 3.3 %collective-permute-start.2 = (f32[1,256,512]{2,1,0:T(8,128)S(1)}, f32[1,256,512]{2,1,0:T(8,128)S(1)}, u32[]{:S(2)}, u32[]{:S(2)}) collective-permute-start(f32[1,256,512]{2,1,0:T(8,128)S(1)} %get-tuple-element.10), channel_id=1, source_target_pairs={{1,0},{2,1},{3,2},{4,3},{5,4},{6,5},{7,6},{9,8},{10,9},{11,10},{12... | collective-permute-start | bytes 1572872 | tf_op jit(solution)/shard_map/ppermute | solution.py:23
  24.8 3.0 %collective-permute-start.3 = (f32[1,256,512]{2,1,0:T(8,128)S(1)}, f32[1,256,512]{2,1,0:T(8,128)S(1)}, u32[]{:S(2)}, u32[]{:S(2)}) collective-permute-start(f32[1,256,512]{2,1,0:T(8,128)S(1)} %get-tuple-element.9), channel_id=1, source_target_pairs={{0,1},{1,2},{2,3},{3,4},{4,5},{5,6},{6,7},{8,9},{9,10},{10,11},{11... | collective-permute-start | bytes 1572872 | tf_op jit(solution)/shard_map/ppermute | solution.py:21
  27.8 5.2 %collective-permute-done.2 = f32[1,256,512]{2,1,0:T(8,128)S(1)} collective-permute-done((f32[1,256,512]{2,1,0:T(8,128)S(1)}, f32[1,256,512]{2,1,0:T(8,128)S(1)}, u32[]{:S(2)}, u32[]{:S(2)}) %collective-permute-start.2) | collective-permute-done | bytes 524320 | tf_op jit(solution)/shard_map/ppermute | solution.py:23
  33.0 3.7 %collective-permute-done.3 = f32[1,256,512]{2,1,0:T(8,128)S(1)} collective-permute-done((f32[1,256,512]{2,1,0:T(8,128)S(1)}, f32[1,256,512]{2,1,0:T(8,128)S(1)}, u32[]{:S(2)}, u32[]{:S(2)}) %collective-permute-start.3) | collective-permute-done | bytes 524320 | tf_op jit(solution)/shard_map/ppermute | solution.py:21
  36.7 2.3 %select_maximum_fusion.4 = f32[6,258,514]{2,1,0:T(8,128)S(1)} fusion(f32[1,256,512]{2,1,0:T(8,128)S(1)} %collective-permute-done.2, f32[4,256,512]{2,1,0:T(8,128)S(1)} %fusion.5, f32[1,256,512]{2,1,0:T(8,128)S(1)} %collective-permute-done.3), kind=kLoop, calls=%fused_computation.8 | loop fusion | flops 11935080 | bytes 6328416 | tf_op jit(solution)/shard_map/concatenate | solution.py:19
  39.0 2.3 %fusion.8 = f32[4,256,512]{2,1,0:T(8,128)S(1)} fusion(f32[4,256,512]{2,1,0:T(8,128)S(1)} %fusion.5, f32[6,258,514]{2,1,0:T(8,128)S(1)} %select_maximum_fusion.4, f32[1,256,512]{2,1,0:T(8,128)S(1)} %collective-permute-done.3, f32[1,256,512]{2,1,0:T(8,128)S(1)} %collective-permute-done.2, f32[4,256,512]{2,1,0:T(8,128)S(1)} %copy-done), kind=kLoop, calls=%fused_computation.24 | loop fusion | flops 8912896 | bytes 15728640 | tf_op jit(solution)/shard_map/add | solution.py:41
  41.2 0.1 fusion.32
  41.3 1.9 %collective-permute-start.4 = (f32[1,256,512]{2,1,0:T(8,128)S(1)}, f32[1,256,512]{2,1,0:T(8,128)S(1)}, u32[]{:S(2)}, u32[]{:S(2)}) collective-permute-start(f32[1,256,512]{2,1,0:T(8,128)S(1)} %get-tuple-element.8), channel_id=1, source_target_pairs={{1,0},{2,1},{3,2},{4,3},{5,4},{6,5},{7,6},{9,8},{10,9},{11,10},{12... | collective-permute-start | bytes 1572872 | tf_op jit(solution)/shard_map/ppermute | solution.py:23
  43.2 4.4 %collective-permute-start.5 = (f32[1,256,512]{2,1,0:T(8,128)S(1)}, f32[1,256,512]{2,1,0:T(8,128)S(1)}, u32[]{:S(2)}, u32[]{:S(2)}) collective-permute-start(f32[1,256,512]{2,1,0:T(8,128)S(1)} %get-tuple-element.7), channel_id=1, source_target_pairs={{0,1},{1,2},{2,3},{3,4},{4,5},{5,6},{6,7},{8,9},{9,10},{10,11},{11... | collective-permute-start | bytes 1572872 | tf_op jit(solution)/shard_map/ppermute | solution.py:21
  47.6 5.2 %collective-permute-done.4 = f32[1,256,512]{2,1,0:T(8,128)S(1)} collective-permute-done((f32[1,256,512]{2,1,0:T(8,128)S(1)}, f32[1,256,512]{2,1,0:T(8,128)S(1)}, u32[]{:S(2)}, u32[]{:S(2)}) %collective-permute-start.4) | collective-permute-done | bytes 524320 | tf_op jit(solution)/shard_map/ppermute | solution.py:23
  52.9 2.7 %collective-permute-done.5 = f32[1,256,512]{2,1,0:T(8,128)S(1)} collective-permute-done((f32[1,256,512]{2,1,0:T(8,128)S(1)}, f32[1,256,512]{2,1,0:T(8,128)S(1)}, u32[]{:S(2)}, u32[]{:S(2)}) %collective-permute-start.5) | collective-permute-done | bytes 524320 | tf_op jit(solution)/shard_map/ppermute | solution.py:21
  55.5 2.3 %select_maximum_fusion.2 = f32[6,258,514]{2,1,0:T(8,128)S(1)} fusion(f32[1,256,512]{2,1,0:T(8,128)S(1)} %collective-permute-done.4, f32[4,256,512]{2,1,0:T(8,128)S(1)} %fusion.8, f32[1,256,512]{2,1,0:T(8,128)S(1)} %collective-permute-done.5), kind=kLoop, calls=%fused_computation.6 | loop fusion | flops 11935080 | bytes 6328416 | tf_op jit(solution)/shard_map/concatenate | solution.py:19
  57.8 2.3 %fusion.11 = f32[4,256,512]{2,1,0:T(8,128)S(1)} fusion(f32[4,256,512]{2,1,0:T(8,128)S(1)} %fusion.8, f32[6,258,514]{2,1,0:T(8,128)S(1)} %select_maximum_fusion.2, f32[1,256,512]{2,1,0:T(8,128)S(1)} %collective-permute-done.5, f32[1,256,512]{2,1,0:T(8,128)S(1)} %collective-permute-done.4, f32[4,256,512]{2,1,0:T(8,128)S(1)} %copy-done), kind=kLoop, calls=%fused_computation.27 | loop fusion | flops 8912896 | bytes 15728640 | tf_op jit(solution)/shard_map/add | solution.py:41
  60.1 0.1 fusion.31
  60.2 1.9 %collective-permute-start.6 = (f32[1,256,512]{2,1,0:T(8,128)S(1)}, f32[1,256,512]{2,1,0:T(8,128)S(1)}, u32[]{:S(2)}, u32[]{:S(2)}) collective-permute-start(f32[1,256,512]{2,1,0:T(8,128)S(1)} %get-tuple-element.6), channel_id=1, source_target_pairs={{1,0},{2,1},{3,2},{4,3},{5,4},{6,5},{7,6},{9,8},{10,9},{11,10},{12... | collective-permute-start | bytes 1572872 | tf_op jit(solution)/shard_map/ppermute | solution.py:23
  62.1 4.4 %collective-permute-start.7 = (f32[1,256,512]{2,1,0:T(8,128)S(1)}, f32[1,256,512]{2,1,0:T(8,128)S(1)}, u32[]{:S(2)}, u32[]{:S(2)}) collective-permute-start(f32[1,256,512]{2,1,0:T(8,128)S(1)} %get-tuple-element.5), channel_id=1, source_target_pairs={{0,1},{1,2},{2,3},{3,4},{4,5},{5,6},{6,7},{8,9},{9,10},{10,11},{11... | collective-permute-start | bytes 1572872 | tf_op jit(solution)/shard_map/ppermute | solution.py:21
  66.5 5.2 %collective-permute-done.6 = f32[1,256,512]{2,1,0:T(8,128)S(1)} collective-permute-done((f32[1,256,512]{2,1,0:T(8,128)S(1)}, f32[1,256,512]{2,1,0:T(8,128)S(1)}, u32[]{:S(2)}, u32[]{:S(2)}) %collective-permute-start.6) | collective-permute-done | bytes 524320 | tf_op jit(solution)/shard_map/ppermute | solution.py:23
  71.7 1.8 %collective-permute-done.7 = f32[1,256,512]{2,1,0:T(8,128)S(1)} collective-permute-done((f32[1,256,512]{2,1,0:T(8,128)S(1)}, f32[1,256,512]{2,1,0:T(8,128)S(1)}, u32[]{:S(2)}, u32[]{:S(2)}) %collective-permute-start.7) | collective-permute-done | bytes 524320 | tf_op jit(solution)/shard_map/ppermute | solution.py:21
  73.5 2.3 %select_maximum_fusion = f32[6,258,514]{2,1,0:T(8,128)S(1)} fusion(f32[1,256,512]{2,1,0:T(8,128)S(1)} %collective-permute-done.6, f32[4,256,512]{2,1,0:T(8,128)S(1)} %fusion.11, f32[1,256,512]{2,1,0:T(8,128)S(1)} %collective-permute-done.7), kind=kLoop, calls=%fused_computation.4 | loop fusion | flops 11935080 | bytes 6328416 | tf_op jit(solution)/shard_map/concatenate | solution.py:19
  75.8 2.3 %fusion.14 = f32[4,256,512]{2,1,0:T(8,128)S(1)} fusion(f32[4,256,512]{2,1,0:T(8,128)S(1)} %fusion.11, f32[6,258,514]{2,1,0:T(8,128)S(1)} %select_maximum_fusion, f32[1,256,512]{2,1,0:T(8,128)S(1)} %collective-permute-done.7, f32[1,256,512]{2,1,0:T(8,128)S(1)} %collective-permute-done.6, f32[4,256,512]{2,1,0:T(8,128)S(1)} %copy-done), kind=kLoop, calls=%fused_computation.30 | loop fusion | flops 8912896 | bytes 15728640 | tf_op jit(solution)/shard_map/add | solution.py:41
  78.1 2.2 %collective-permute-start.8 = (f32[4,256,512]{2,1,0:T(8,128)S(1)}, f32[4,256,512]{2,1,0:T(8,128)S(1)}, u32[]{:S(2)}, u32[]{:S(2)}) collective-permute-start(f32[4,256,512]{2,1,0:T(8,128)S(1)} %fusion.14), channel_id=1, source_target_pairs={{8,0},{16,8},{24,16},{9,1},{17,9},{25,17},{10,2},{18,10},{26,18},{... | collective-permute-start | bytes 6291464 | tf_op jit(solution)/shard_map/ppermute | solution.py:33
  80.3 1.3 collective-permute-start.9
  82.9 42.7 %collective-permute-done.8 = f32[4,256,512]{2,1,0:T(8,128)S(1)} collective-permute-done((f32[4,256,512]{2,1,0:T(8,128)S(1)}, f32[4,256,512]{2,1,0:T(8,128)S(1)}, u32[]{:S(2)}, u32[]{:S(2)}) %collective-permute-start.8) | collective-permute-done | bytes 2097184 | tf_op jit(solution)/shard_map/ppermute | solution.py:33
  125.6 4.0 %collective-permute-done.9 = f32[4,256,512]{2,1,0:T(8,128)S(1)} collective-permute-done((f32[4,256,512]{2,1,0:T(8,128)S(1)}, f32[4,256,512]{2,1,0:T(8,128)S(1)}, u32[]{:S(2)}, u32[]{:S(2)}) %collective-permute-start.9) | collective-permute-done | bytes 2097184 | tf_op jit(solution)/shard_map/ppermute | solution.py:33
  129.6 2.1 %add_bitcast_fusion = f32[1,4,256,512]{3,2,1,0:T(8,128)} fusion(f32[4,256,512]{2,1,0:T(8,128)S(1)} %fusion.14, f32[4,256,512]{2,1,0:T(8,128)S(1)} %collective-permute-done.8, f32[4,256,512]{2,1,0:T(8,128)S(1)} %collective-permute-done.9, f32[]{:T(128)} %bitcast.9, pred[]{:T(512)} %bitcast.4), kind=kLoop, calls=%fused_computation.71 | loop fusion | flops 2097152 | bytes 8388613 | tf_op jit(solution)/shard_map/broadcast_in_dim | solution.py:53
Async XLA Ops:
  0.0 16.8 %copy-start.1 = (f32[1,4,256,512]{3,2,1,0:T(8,128)S(1)}, f32[1,4,256,512]{3,2,1,0:T(8,128)}, u32[]{:S(2)}) copy-start(f32[1,4,256,512]{3,2,1,0:T(8,128)} %param.4) | copy-start | bytes 6291460
  1.4 10.8 %collective-permute-start = (f32[1,256,512]{2,1,0:T(8,128)S(1)}, f32[1,256,512]{2,1,0:T(8,128)S(1)}, u32[]{:S(2)}, u32[]{:S(2)}) collective-permute-start(f32[1,256,512]{2,1,0:T(8,128)S(1)} %get-tuple-element.12), channel_id=1, source_target_pairs={{1,0},{2,1},{3,2},{4,3},{5,4},{6,5},{7,6},{9,8},{10,9},{11,10},{12... | collective-permute-start | bytes 1572872 | tf_op jit(solution)/shard_map/ppermute | solution.py:23
  4.0 12.8 %collective-permute-start.1 = (f32[1,256,512]{2,1,0:T(8,128)S(1)}, f32[1,256,512]{2,1,0:T(8,128)S(1)}, u32[]{:S(2)}, u32[]{:S(2)}) collective-permute-start(f32[1,256,512]{2,1,0:T(8,128)S(1)} %get-tuple-element.11), channel_id=1, source_target_pairs={{0,1},{1,2},{2,3},{3,4},{4,5},{5,6},{6,7},{8,9},{9,10},{10,11},{11... | collective-permute-start | bytes 1572872 | tf_op jit(solution)/shard_map/ppermute | solution.py:21
  16.8 2.3 %copy-start = (f32[4,256,512]{2,1,0:T(8,128)S(1)}, f32[4,256,512]{2,1,0:T(8,128)}, u32[]{:S(2)}) copy-start(f32[4,256,512]{2,1,0:T(8,128)} %param.5) | copy-start | bytes 6291460
  21.4 11.5 %collective-permute-start.2 = (f32[1,256,512]{2,1,0:T(8,128)S(1)}, f32[1,256,512]{2,1,0:T(8,128)S(1)}, u32[]{:S(2)}, u32[]{:S(2)}) collective-permute-start(f32[1,256,512]{2,1,0:T(8,128)S(1)} %get-tuple-element.10), channel_id=1, source_target_pairs={{1,0},{2,1},{3,2},{4,3},{5,4},{6,5},{7,6},{9,8},{10,9},{11,10},{12... | collective-permute-start | bytes 1572872 | tf_op jit(solution)/shard_map/ppermute | solution.py:23
  24.8 11.9 %collective-permute-start.3 = (f32[1,256,512]{2,1,0:T(8,128)S(1)}, f32[1,256,512]{2,1,0:T(8,128)S(1)}, u32[]{:S(2)}, u32[]{:S(2)}) collective-permute-start(f32[1,256,512]{2,1,0:T(8,128)S(1)} %get-tuple-element.9), channel_id=1, source_target_pairs={{0,1},{1,2},{2,3},{3,4},{4,5},{5,6},{6,7},{8,9},{9,10},{10,11},{11... | collective-permute-start | bytes 1572872 | tf_op jit(solution)/shard_map/ppermute | solution.py:21
  41.3 11.5 %collective-permute-start.4 = (f32[1,256,512]{2,1,0:T(8,128)S(1)}, f32[1,256,512]{2,1,0:T(8,128)S(1)}, u32[]{:S(2)}, u32[]{:S(2)}) collective-permute-start(f32[1,256,512]{2,1,0:T(8,128)S(1)} %get-tuple-element.8), channel_id=1, source_target_pairs={{1,0},{2,1},{3,2},{4,3},{5,4},{6,5},{7,6},{9,8},{10,9},{11,10},{12... | collective-permute-start | bytes 1572872 | tf_op jit(solution)/shard_map/ppermute | solution.py:23
  43.2 12.3 %collective-permute-start.5 = (f32[1,256,512]{2,1,0:T(8,128)S(1)}, f32[1,256,512]{2,1,0:T(8,128)S(1)}, u32[]{:S(2)}, u32[]{:S(2)}) collective-permute-start(f32[1,256,512]{2,1,0:T(8,128)S(1)} %get-tuple-element.7), channel_id=1, source_target_pairs={{0,1},{1,2},{2,3},{3,4},{4,5},{5,6},{6,7},{8,9},{9,10},{10,11},{11... | collective-permute-start | bytes 1572872 | tf_op jit(solution)/shard_map/ppermute | solution.py:21
  60.2 11.5 %collective-permute-start.6 = (f32[1,256,512]{2,1,0:T(8,128)S(1)}, f32[1,256,512]{2,1,0:T(8,128)S(1)}, u32[]{:S(2)}, u32[]{:S(2)}) collective-permute-start(f32[1,256,512]{2,1,0:T(8,128)S(1)} %get-tuple-element.6), channel_id=1, source_target_pairs={{1,0},{2,1},{3,2},{4,3},{5,4},{6,5},{7,6},{9,8},{10,9},{11,10},{12... | collective-permute-start | bytes 1572872 | tf_op jit(solution)/shard_map/ppermute | solution.py:23
  62.1 11.4 %collective-permute-start.7 = (f32[1,256,512]{2,1,0:T(8,128)S(1)}, f32[1,256,512]{2,1,0:T(8,128)S(1)}, u32[]{:S(2)}, u32[]{:S(2)}) collective-permute-start(f32[1,256,512]{2,1,0:T(8,128)S(1)} %get-tuple-element.5), channel_id=1, source_target_pairs={{0,1},{1,2},{2,3},{3,4},{4,5},{5,6},{6,7},{8,9},{9,10},{10,11},{11... | collective-permute-start | bytes 1572872 | tf_op jit(solution)/shard_map/ppermute | solution.py:21
  78.1 47.5 %collective-permute-start.8 = (f32[4,256,512]{2,1,0:T(8,128)S(1)}, f32[4,256,512]{2,1,0:T(8,128)S(1)}, u32[]{:S(2)}, u32[]{:S(2)}) collective-permute-start(f32[4,256,512]{2,1,0:T(8,128)S(1)} %fusion.14), channel_id=1, source_target_pairs={{8,0},{16,8},{24,16},{9,1},{17,9},{25,17},{10,2},{18,10},{26,18},{... | collective-permute-start | bytes 6291464 | tf_op jit(solution)/shard_map/ppermute | solution.py:33
  80.3 49.3 %collective-permute-start.9 = (f32[4,256,512]{2,1,0:T(8,128)S(1)}, f32[4,256,512]{2,1,0:T(8,128)S(1)}, u32[]{:S(2)}, u32[]{:S(2)}) collective-permute-start(f32[4,256,512]{2,1,0:T(8,128)S(1)} %fusion.14), channel_id=1, source_target_pairs={{0,8},{8,16},{16,24},{1,9},{9,17},{17,25},{2,10},{10,18},{18,26},{... | collective-permute-start | bytes 6291464 | tf_op jit(solution)/shard_map/ppermute | solution.py:33
where the time goes:
time: 132 us
  waiting for transfers between devices  80.3 us (61%)
  starting transfers between devices  28 us (21%)
  other arithmetic  20.2 us (15%)
  local copies, waits for them, and re-layouts  1.64 us (1%)
  between operations  1.48 us (1%)
    ppermute x2, waiting for transfers between devices, passed_along(): return lax.ppermute(x, axis, pairs)  46.7 us
    ppermute x4, waiting for transfers between devices, with_halo(): lax.ppermute(head, axis, [((i + 1) % count, i) for i in range(ends)])  20.9 us
    ppermute x4, starting transfers between devices, with_halo(): lax.ppermute(tail, axis, [(i, (i + 1) % count) for i in range(ends)])  14.8 us
    ppermute x4, waiting for transfers between devices, with_halo(): lax.ppermute(tail, axis, [(i, (i + 1) % count) for i in range(ends)])  12.7 us
    ppermute x4, starting transfers between devices, with_halo(): lax.ppermute(head, axis, [((i + 1) % count, i) for i in range(ends)])  9.76 us
    add x4, other arithmetic, advance(): phi + DT * mob * (EPS2 * (beside - 6.0 * phi) + phi - phi * phi * phi)  9.1 us
    concatenate x4, other arithmetic, with_halo(): jnp.concatenate([lax.ppermute(tail, axis, [(i, (i + 1) % count) for i in...  9.04 us
    ppermute x2, starting transfers between devices, passed_along(): return lax.ppermute(x, axis, pairs)  3.5 us
  transfers between devices with their start and end apart: 10, of which 10 were waited for; matrix products, arithmetic and copies ran while one was open for 0% of the time, Pallas kernels for 0%

commit v1 on v0

v1 whole, which is shorter than its diff:
```python
import functools

import jax
import jax.numpy as jnp
from jax import lax
from jax.experimental import pallas as pl
from jax.experimental.pallas import tpu as pltpu
from jax.sharding import PartitionSpec as P

STEPS = 4
DT = 0.1
EPS2 = 1.5
TILE = 8
LANES = 128
BLOCK = 32

VMEM = pl.BlockSpec(memory_space=pltpu.VMEM)
SMEM = pl.BlockSpec(memory_space=pltpu.SMEM)
ANY = pl.BlockSpec(memory_space=pl.ANY)
HBM = pl.BlockSpec(memory_space=pltpu.HBM)

SHARES = (4, 8, 8, 6)
ORDER = (
    "E O01 ZA Cf",
    "Cm O11 O31 O21",
    "K01 O02 K11 O12",
    "K21 O22 K02 O03",
    "K12 O13 K31 K22",
    "O23 K03 O04 N",
    "O32 K13 CN O14",
    "OA1 K04 Z0 K23",
    "O24 K32 K14 O33",
    "Z1 KA1 OA2 K24",
    "K33 O34 Z2 KA2",
    "OA3 K34 Z3 KA3",
    "OA4 B0 KA4 B1",
)
BLENDS = ((0, 1, 2), (3,))


def swap(x, odd):
    count = lax.axis_size("space")
    assert count % 2 == 0
    pairs = [((i + odd) % count, (i + 1 + odd) % count) for i in range(0, count, 2)]
    return lax.ppermute(x, "space", pairs + [(b, a) for a, b in pairs])


def swap_images(x, odd):
    images, count = lax.axis_size("image"), lax.axis_size("space")
    assert images % 2 == 0
    pairs = []
    for s in range(count):
        pairs += [(i * count + s, (i + 1) * count + s) for i in range(odd, images - 1, 2)]
    if odd:
        for i in (0, images - 1):
            pairs += [(i * count + s, i * count + s + 1) for s in range(0, count, 2)]
    return lax.ppermute(x, ("image", "space"), pairs + [(b, a) for a, b in pairs])


def cuts(ny):
    bounds = [0]
    for share in SHARES:
        bounds.append(bounds[-1] + share * ny // 32)
    return bounds


def span(bounds, c, s):
    lo = 0 if c == 0 else bounds[c] + TILE * (STEPS - s)
    if c == len(bounds) - 2:
        return lo, bounds[c + 1] + (TILE if s < STEPS else 0)
    return lo, bounds[c + 1] + TILE * (STEPS - s)


def layer_index(layer, layers):
    odd = lax.rem(lax.axis_index("space"), 2)
    return odd * (layers - 1) + layer * (1 - 2 * odd)


def at(first, rows=TILE):
    return pl.ds(first if isinstance(first, int) else pl.multiple_of(first, TILE), rows)


def params(mib):
    return pltpu.CompilerParams(vmem_limit_bytes=(mib + 11) << 20)


def edge_kernel(spans, start, field_ref, *refs):
    outs, raw, sems = refs[:-2], refs[-2], refs[-1]
    layers = field_ref.shape[1]
    copies = [
        pltpu.make_async_copy(field_ref.at[0, layer_index(0, layers), lo:hi], out, sems.at[i])
        for i, ((lo, hi), out) in enumerate(zip(spans, outs))
    ]
    copies.append(pltpu.make_async_copy(field_ref.at[0, :, start:], raw, sems.at[len(spans)]))
    for copy in copies:
        copy.start()
    for copy in copies:
        copy.wait()


def first_edges(field, bounds):
    layers, ny, nz = field.shape[1:]
    spans = [span(bounds, c, 1) for c in range(len(bounds) - 1)]
    start = bounds[-1] - TILE
    shapes = [(hi - lo, nz) for lo, hi in spans] + [(layers, ny - start, nz)]
    return pl.pallas_call(
        functools.partial(edge_kernel, spans, start),
        out_shape=[jax.ShapeDtypeStruct(shape, field.dtype) for shape in shapes],
        in_specs=[HBM],
        out_specs=[VMEM] * len(shapes),
        scratch_shapes=[pltpu.SemaphoreType.DMA((len(shapes),))],
        compiler_params=params(1),
        name="edges",
    )(field)


def towards_even():
    image_odd = lax.rem(lax.axis_index("image"), 2)
    return lambda side: side != image_odd


def pick_kernel(sides_ref, own_ref, even_ref, odd_ref, out_ref, edge_ref):
    layers, rows, _ = out_ref.shape
    first = layer_index(0, layers)
    with_even = towards_even()(sides_ref[0])

    def take(src_ref):
        @pl.loop(0, rows // TILE)
        def _(i):
            for layer in range(layers):
                out_ref[layer, at(i * TILE), :] = src_ref[layer, at(i * TILE), :]
            edge_ref[0, at(i * TILE), :] = own_ref[first, at(i * TILE), :]
            edge_ref[1, at(i * TILE), :] = src_ref[first, at(i * TILE), :]

    pl.when(with_even)(lambda: take(even_ref))
    pl.when(jnp.logical_not(with_even))(lambda: take(odd_ref))


def pick(sides, own, even, odd):
    _, rows, nz = own.shape
    return pl.pallas_call(
        pick_kernel,
        out_shape=[
            jax.ShapeDtypeStruct(own.shape, own.dtype),
            jax.ShapeDtypeStruct((2, rows, nz), own.dtype),
        ],
        in_specs=[SMEM, VMEM, VMEM, VMEM],
        out_specs=[VMEM, VMEM],
        cost_estimate=pl.CostEstimate(flops=0, bytes_accessed=8 * own.size, transcendentals=0),
        compiler_params=params(1),
        name="pick",
    )(sides, own, even, odd)


def relax_rows(cells, mobility, outer, store, n_out, first, final, top, bottom, alone, nz):
    def block(r, rows, top, bottom):
        lane = lax.broadcasted_iota(jnp.int32, (rows, LANES), 1)
        none = jnp.zeros((TILE, nz), jnp.float32)
        under = outer(r, rows)
        mid = cells(0, r, rows)
        for layer in range(n_out):
            over = cells(layer + 1, r, rows)
            above = none if top else cells(layer, r - TILE, TILE)
            below = none if bottom else cells(layer, r + rows, TILE)
            wide = jnp.concatenate([above, mid, below], axis=0)
            up, down = wide[TILE - 1 : TILE - 1 + rows], wide[TILE + 1 : TILE + 1 + rows]
            right = pltpu.roll(mid, nz - 1, 1)
            right = jnp.concatenate(
                [right[:, :-LANES], jnp.where(lane == LANES - 1, 0.0, right[:, -LANES:])], axis=1
            )
            left = pltpu.roll(mid, 1, 1)
            left = jnp.concatenate([jnp.where(lane == 0, 0.0, left[:, :LANES]), left[:, LANES:]], axis=1)
            beside = (over + under) + (down + up) + (right + left)
            rate = DT * mobility(layer, r, rows)
            store(layer, r, rows, mid + rate * (EPS2 * beside - mid * (6.0 * EPS2 - 1.0 + mid * mid)))
            under, mid = mid, over

    last = final
    if top:
        block(first, TILE, True, False)
        first += TILE
    if bottom or alone:
        last -= TILE
    body = (last - first) // BLOCK
    for r in range(first + body * BLOCK, last, TILE):
        block(r, TILE, False, False)
    if body > 0:
        @pl.loop(0, body)
        def _(i):
            block(first + i * BLOCK, BLOCK, False, False)
    if last < final:
        block(last, TILE, False, bottom)


def outside():
    me, count = lax.axis_index("space"), lax.axis_size("space")
    return jnp.logical_or(me == 0, me == count - 1)


def step_kernel(c, s, bounds, layers, names, *refs):
    ref = dict(zip(names, refs))
    last_chunk = c == len(bounds) - 2
    last_step = s == STEPS
    nz = ref["mob"].shape[-1]
    lo, hi = span(bounds, c, s)
    lead = margin(c, s)
    origin = 0 if s == 1 else span(bounds, c, s - 1)[0] - margin(c, s - 1)
    n_out = layers + STEPS - s
    out = ref["out"]
    no_outer = outside()

    def cells(layer, r, rows):
        if s == 1:
            src = ref["own"] if layer < layers else ref["ghost"]
            return src[layer_index(layer % layers, layers), at(r, rows), :]
        return ref["cells"][layer, at(r - origin, rows), :]

    def mobility(layer, r, rows):
        src = ref["mob"] if layer < layers else ref["ghost_mob"]
        return src[layer_index(layer % layers, layers), at(r, rows), :]

    def outer(r, rows):
        return jnp.where(no_outer, 0.0, ref["beyond"][at(r - lo, rows), :])

    edge_lo, edge_hi = span(bounds, c, s + 1) if not last_step else (0, 0)

    def store(layer, r, rows, new):
        out[layer, at(r - lo + lead, rows), :] = new
        if layer > 0 or last_step:
            return
        if not isinstance(r, int):
            ref["edge"][at(r - edge_lo, rows), :] = new
        elif r < edge_hi:
            kept = min(rows, edge_hi - r)
            ref["edge"][at(r - edge_lo, kept), :] = new[:kept]

    if c > 0 and not last_step:
        rows = ref["above"].shape[1]
        for layer in range(n_out):
            out[layer, 0:lead, :] = ref["above"][layer, rows - lead : rows, :]
        ref["edge"][0:TILE, :] = ref["above"][0, rows - TILE : rows, :]

    relax_rows(cells, mobility, outer, store, n_out, lo, hi, c == 0, last_chunk and s < STEPS, not last_step, nz)


def margin(c, s):
    return 2 * TILE if c > 0 and 0 < s < STEPS else 0


def step(c, s, bounds, layers, arrays, like):
    _, nz = like.shape[1:]
    lo, hi = span(bounds, c, s)
    n_out = layers + STEPS - s
    shapes = {"out": (n_out, margin(c, s) + hi - lo, nz)}
    if s < STEPS:
        edge_lo, edge_hi = span(bounds, c, s + 1)
        shapes["edge"] = (edge_hi - edge_lo, nz)
    cells = n_out * (hi - lo) * nz
    outs = pl.pallas_call(
        functools.partial(step_kernel, c, s, bounds, layers, [*arrays, *shapes]),
        out_shape=[jax.ShapeDtypeStruct(shape, like.dtype) for shape in shapes.values()],
        in_specs=[VMEM] * len(arrays),
        out_specs=[VMEM] * len(shapes),
        cost_estimate=pl.CostEstimate(flops=20 * cells, bytes_accessed=4 * cells, transcendentals=0),
        compiler_params=params(1),
    )(*arrays.values())
    return dict(zip(shapes, outs))


def both_kernel(s, start, layers, names, *refs):
    ref = dict(zip(names, refs))
    last_step = s == STEPS
    ny, nz = ref["mob"].shape[1:]
    n_out = layers + STEPS - s
    no_outer = outside()
    first = start + TILE if last_step else start

    def mobility(layer, r, rows):
        src = ref["mob"] if layer < layers else ref["ghost_mob"]
        return src[layer_index(layer % layers, layers), at(r, rows), :]

    for image in (0, 1):
        def cells(layer, r, rows, image=image):
            if s > 1:
                return ref["cells"][image, layer, at(r - start, rows), :]
            name, skip = ("own", 0) if image == 0 else ("other", start)
            src = ref[name] if layer < layers else ref[name + "_ghost"]
            return src[layer_index(layer % layers, layers), at(r - skip, rows), :]

        def outer(r, rows, image=image):
            return jnp.where(no_outer, 0.0, ref["beyond"][image, at(r - start, rows), :])

        def store(layer, r, rows, new, image=image):
            if last_step:
                here = at(r - first, rows)
                if image == 1:
                    mine = ref["relaxed"][layer, here, :]
                    new = mine + ref["fractions"][0] * (new - mine)
                ref["relaxed"][layer, here, :] = new
                return
            ref["out"][image, layer, at(r - start, rows), :] = new
            if layer == 0:
                ref["edge"][image, at(r - start, rows), :] = new

        relax_rows(cells, mobility, outer, store, n_out, first, ny, not last_step, True, False, nz)

    if last_step:
        copies = [
            pltpu.make_async_copy(
                ref["relaxed"].at[layer], ref["out"].at[0, layer_index(layer, layers), first:ny], ref["sem"].at[layer]
            )
            for layer in range(layers)
        ]
        for copy in copies:
            copy.start()
        for copy in copies:
            copy.wait()


def both_step(s, bounds, layers, arrays, like, out, field):
    ny, nz = like.shape[1:]
    start = bounds[-1] - TILE
    rows = ny - start
    n_out = layers + STEPS - s
    last_step = s == STEPS
    scratch = {}
    if last_step:
        shapes = {"out": field.shape}
        scratch["relaxed"] = pltpu.VMEM((layers, rows - TILE, nz), like.dtype)
        scratch["sem"] = pltpu.SemaphoreType.DMA((layers,))
        specs = [HBM]
    else:
        shapes = {"out": (2, n_out, rows, nz), "edge": (2, rows, nz)}
        specs = [VMEM, VMEM]
    in_specs = [SMEM if name == "fractions" else VMEM for name in arrays]
    aliases = {}
    if last_step and out is not None:
        aliases = {len(arrays): 0}
        arrays = {**arrays, "before": out}
        in_specs.append(HBM)
    cells = 2 * n_out * rows * nz
    outs = pl.pallas_call(
        functools.partial(both_kernel, s, start, layers, [*arrays, *shapes, *scratch]),
        out_shape=[jax.ShapeDtypeStruct(shape, like.dtype) for shape in shapes.values()],
        in_specs=in_specs,
        out_specs=specs,
        scratch_shapes=list(scratch.values()),
        input_output_aliases=aliases,
        cost_estimate=pl.CostEstimate(flops=20 * cells, bytes_accessed=4 * cells, transcendentals=0),
        compiler_params=params(1),
    )(*arrays.values())
    return dict(zip(shapes, outs))


def blend_kernel(spans, aliased, sides_ref, fractions_ref, *refs):
    n = len(spans)
    owns, evens, odds = refs[:n], refs[n : 2 * n], refs[2 * n : 3 * n]
    out_ref, bufs, sem = refs[3 * n + aliased], refs[3 * n + aliased + 1 : -1], refs[-1]
    layers = owns[0].shape[0]
    with_even = towards_even()(sides_ref[0])
    share = fractions_ref[0]
    copies = []
    for k, (lo, hi) in enumerate(spans):
        def mix(other_ref, own_ref=owns[k], buf=bufs[k], rows=hi - lo):
            @pl.loop(0, rows // TILE)
            def _(i):
                for layer in range(layers):
                    mine = own_ref[layer, at(i * TILE), :]
                    buf[layer, at(i * TILE), :] = mine + share * (other_ref[layer, at(i * TILE), :] - mine)

        pl.when(with_even)(functools.partial(mix, evens[k]))
        pl.when(jnp.logical_not(with_even))(functools.partial(mix, odds[k]))
        for layer in range(layers):
            copy = pltpu.make_async_copy(
                bufs[k].at[layer], out_ref.at[0, layer_index(layer, layers), lo:hi], sem.at[k, layer]
            )
            copy.start()
            copies.append(copy)
    for copy in copies:
        copy.wait()


def blend(chunks, bounds, sides, fractions, val, out, like):
    spans = [span(bounds, c, STEPS) for c in chunks]
    owns = [val["K", c, STEPS] for c in chunks]
    layers = owns[0].shape[0]
    operands = [sides, fractions, *owns, *(val["Z", c, name] for name in ("even", "odd") for c in chunks)]
    size = sum(own.size for own in owns)
    return pl.pallas_call(
        functools.partial(blend_kernel, spans, out is not None),
        out_shape=jax.ShapeDtypeStruct(like.shape, like.dtype),
        in_specs=[SMEM, SMEM] + [VMEM] * (3 * len(chunks)) + ([] if out is None else [HBM]),
        out_specs=HBM,
        input_output_aliases={} if out is None else {len(operands): 0},
        scratch_shapes=[pltpu.VMEM(own.shape, own.dtype) for own in owns]
        + [pltpu.SemaphoreType.DMA((len(chunks), layers))],
        cost_estimate=pl.CostEstimate(flops=3 * size, bytes_accessed=12 * size, transcendentals=0),
        compiler_params=params(4),
    )(*operands, *([] if out is None else [out]))


def items():
    return " ".join(ORDER).split()


def local(field, mobility, fractions, sides):
    layers, ny = field.shape[1:3]
    bounds = cuts(ny)
    val = {}
    out = None
    for item in items():
        kind, c, s = item[0], *(item[1:] + "  ")[:2]
        c = int(c) if c.isdigit() else c
        s = int(s) if s.isdigit() else None
        if kind == "E":
            *edges, val["K", "A", STEPS] = first_edges(field, bounds)
            for i, edge in enumerate(edges):
                val["edge", i, 1] = edge
        elif kind == "C":
            source = {"f": field[0], "m": mobility, "N": val.get(("N",))}[c]
            val["C", c] = swap(source, 0)
        elif kind == "N":
            val["N",], val["edge", "A", 1] = pick(
                sides, val["K", "A", STEPS], val["Z", "A", "even"], val["Z", "A", "odd"]
            )
        elif kind == "O":
            val["O", c, s] = swap(val["edge", c, s], 1)
        elif kind == "K":
            arrays = {"mob": mobility, "ghost_mob": val["C", "m"], "beyond": val["O", c, s]}
            if s == 1 and c == "A":
                arrays["own"], arrays["own_ghost"] = field[0], val["C", "f"]
                arrays["other"], arrays["other_ghost"] = val["N",], val["C", "N"]
            elif s == 1:
                arrays["own"], arrays["ghost"] = field[0], val["C", "f"]
            else:
                arrays["cells"] = val["K", c, s - 1]
            if c == "A":
                if s == STEPS:
                    arrays["fractions"] = fractions
                got = both_step(s, bounds, layers, arrays, mobility, out, field)
            else:
                if c > 0 and s < STEPS:
                    arrays["above"] = val["K", c - 1, s]
                got = step(c, s, bounds, layers, arrays, mobility)
            if c == "A" and s == STEPS:
                out = got["out"]
            else:
                val["K", c, s] = got["out"]
            if s < STEPS:
                val["edge", c, s + 1] = got["edge"]
        elif kind == "Z":
            for name, odd in (("even", 0), ("odd", 1)):
                val["Z", c, name] = swap_images(val["K", c, STEPS], odd)
        elif kind == "B":
            out = blend(BLENDS[c], bounds, sides, fractions, val, out, field)
    return out


def solution(mesh):
    return jax.shard_map(
        local,
        mesh=mesh,
        in_specs=(P("image", "space", None, None), P("space", None, None), P("image"), P("image")),
        out_specs=P("image", "space", None, None),
        check_vma=False,
    )
```

time: 132 us -> 116 us (0.88)
  the two profiles are of different devices: /device:TPU:29 before, /device:TPU:0 now
where the time goes in v1:
time: 116 us
  waiting for transfers between devices  55.3 us (48%)
  starting transfers between devices  40.9 us (35%)
  Pallas kernels  14.6 us (13%)
  local copies, waits for them, and re-layouts  3.25 us (3%)
  between operations  1.72 us (1%)
    ppermute x10, waiting for transfers between devices, swap_images(): lax.ppermute(x, ('image', 'space'), pairs + [(b, a) for a, b in pairs])  30.3 us
    ppermute x23, starting transfers between devices, swap(): return lax.ppermute(x, 'space', pairs + [(b, a) for a, b in pairs])  25.6 us
    ppermute x23, waiting for transfers between devices, swap(): return lax.ppermute(x, 'space', pairs + [(b, a) for a, b in pairs])  24.9 us
    ppermute x10, starting transfers between devices, swap_images(): lax.ppermute(x, ('image', 'space'), pairs + [(b, a) for a, b in pairs])  15.3 us
    pallas_call x16, Pallas kernels, step(): pl.pallas_call(functools.partial(step_kernel, c, s, bounds, layers, [*arr...  7.41 us
    pallas_call x4, Pallas kernels, both_step(): pl.pallas_call(functools.partial(both_kernel, s, start, layers, [*arrays,...  4.37 us
    unnamed x6, local copies, waits for them, and re-layouts  3.25 us
  transfers between devices with their start and end apart: 33, of which 14 were waited for; matrix products, arithmetic and copies ran while one was open for 0% of the time, Pallas kernels for 12%

profile of v1, /device:TPU:0, one launch (start us, length us, event | category | flops | bytes accessed | tf_op | source)
XLA Modules:
  0.0 115.7 jit_solution(10346927723883163018)
XLA Ops:
  0.6 1.7 %copy-done.1 = f32[1,4,256,512]{3,2,1,0:T(8,128)S(1)} copy-done((f32[1,4,256,512]{3,2,1,0:T(8,128)S(1)}, f32[1,4,256,512]{3,2,1,0:T(8,128)}, u32[]{:S(2)}) %copy-start.1) | copy-done | bytes 2097176
  2.2 0.7 edges.1
  3.5 4.1 %collective-permute-start.17 = (f32[4,56,512]{2,1,0:T(8,128)S(1)}, f32[4,56,512]{2,1,0:T(8,128)S(1)}, u32[]{:S(2)}, u32[]{:S(2)}) collective-permute-start(f32[4,56,512]{2,1,0:T(8,128)S(1)} %get-tuple-element.67.own_ref), channel_id=1, source_target_pairs={{0,8},{16,24},{1,9},{17,25},{2,10},{18,26},{3,11},{19,27},{4,12},{... | collective-permute-start | bytes 1376264 | tf_op jit(solution)/shard_map/ppermute | solution.py:57
  8.3 9.7 %collective-permute-done.17.even_ref = f32[4,56,512]{2,1,0:T(8,128)S(1)} collective-permute-done((f32[4,56,512]{2,1,0:T(8,128)S(1)}, f32[4,56,512]{2,1,0:T(8,128)S(1)}, u32[]{:S(2)}, u32[]{:S(2)}) %collective-permute-start.17) | collective-permute-done | bytes 458784 | tf_op jit(solution)/shard_map/ppermute | solution.py:57
  18.1 2.5 %collective-permute-start.4 = (f32[64,512]{1,0:T(8,128)S(1)}, f32[64,512]{1,0:T(8,128)S(1)}, u32[]{:S(2)}, u32[]{:S(2)}) collective-permute-start(f32[64,512]{1,0:T(8,128)S(1)} %get-tuple-element.44), channel_id=1, source_target_pairs={{1,2},{3,4},{5,6},{7,0},{2,1},{4,3},{6,5},{0,7},{9,10},{11,12},{13... | collective-permute-start | bytes 393224 | tf_op jit(solution)/shard_map/ppermute | solution.py:45
  20.8 6.2 %collective-permute-done.5.refs_2_ = f32[56,512]{1,0:T(8,128)S(1)} collective-permute-done((f32[56,512]{1,0:T(8,128)S(1)}, f32[56,512]{1,0:T(8,128)S(1)}, u32[]{:S(2)}, u32[]{:S(2)}) %collective-permute-start.5) | collective-permute-done | bytes 114720 | tf_op jit(solution)/shard_map/ppermute | solution.py:45
  27.0 1.6 %copy-done.2 = f32[1,4,256,512]{3,2,1,0:T(8,128)S(1)} copy-done((f32[1,4,256,512]{3,2,1,0:T(8,128)S(1)}, f32[1,4,256,512]{3,2,1,0:T(8,128)}, u32[]{:S(2)}) %copy-start.2) | copy-done | bytes 2097176
  28.6 0.6 shard_map.46
  29.2 0.7 shard_map.47
  29.9 1.3 %collective-permute-start.8 = (f32[64,512]{1,0:T(8,128)S(1)}, f32[64,512]{1,0:T(8,128)S(1)}, u32[]{:S(2)}, u32[]{:S(2)}) collective-permute-start(f32[64,512]{1,0:T(8,128)S(1)} %get-tuple-element.52), channel_id=1, source_target_pairs={{1,2},{3,4},{5,6},{7,0},{2,1},{4,3},{6,5},{0,7},{9,10},{11,12},{13... | collective-permute-start | bytes 393224 | tf_op jit(solution)/shard_map/ppermute | solution.py:45
  31.2 1.4 %collective-permute-start.9 = (f32[48,512]{1,0:T(8,128)S(1)}, f32[48,512]{1,0:T(8,128)S(1)}, u32[]{:S(2)}, u32[]{:S(2)}) collective-permute-start(f32[48,512]{1,0:T(8,128)S(1)} %get-tuple-element.53), channel_id=1, source_target_pairs={{1,2},{3,4},{5,6},{7,0},{2,1},{4,3},{6,5},{0,7},{9,10},{11,12},{13... | collective-permute-start | bytes 294920 | tf_op jit(solution)/shard_map/ppermute | solution.py:45
  32.6 1.2 %collective-permute-start.3 = (f32[64,512]{1,0:T(8,128)S(1)}, f32[64,512]{1,0:T(8,128)S(1)}, u32[]{:S(2)}, u32[]{:S(2)}) collective-permute-start(f32[64,512]{1,0:T(8,128)S(1)} %get-tuple-element.43), channel_id=1, source_target_pairs={{1,2},{3,4},{5,6},{7,0},{2,1},{4,3},{6,5},{0,7},{9,10},{11,12},{13... | collective-permute-start | bytes 393224 | tf_op jit(solution)/shard_map/ppermute | solution.py:45
  33.8 1.4 %collective-permute-start.19 = (f32[2,56,512]{2,1,0:T(8,128)S(1)}, f32[2,56,512]{2,1,0:T(8,128)S(1)}, u32[]{:S(2)}, u32[]{:S(2)}) collective-permute-start(f32[2,56,512]{2,1,0:T(8,128)S(1)} %get-tuple-element.68), channel_id=1, source_target_pairs={{1,2},{3,4},{5,6},{7,0},{2,1},{4,3},{6,5},{0,7},{9,10},{11,12},{13... | collective-permute-start | bytes 688136 | tf_op jit(solution)/shard_map/ppermute | solution.py:45
  35.2 3.5 %collective-permute-done.9.refs_2_ = f32[48,512]{1,0:T(8,128)S(1)} collective-permute-done((f32[48,512]{1,0:T(8,128)S(1)}, f32[48,512]{1,0:T(8,128)S(1)}, u32[]{:S(2)}, u32[]{:S(2)}) %collective-permute-start.9) | collective-permute-done | bytes 98336 | tf_op jit(solution)/shard_map/ppermute | solution.py:45
  39.2 1.3 %collective-permute-start.13 = (f32[40,512]{1,0:T(8,128)S(1)}, f32[40,512]{1,0:T(8,128)S(1)}, u32[]{:S(2)}, u32[]{:S(2)}) collective-permute-start(f32[40,512]{1,0:T(8,128)S(1)} %get-tuple-element.61), channel_id=1, source_target_pairs={{1,2},{3,4},{5,6},{7,0},{2,1},{4,3},{6,5},{0,7},{9,10},{11,12},{13... | collective-permute-start | bytes 245768 | tf_op jit(solution)/shard_map/ppermute | solution.py:45
  40.5 0.6 shard_map.51
  41.1 1.5 %collective-permute-start.12 = (f32[64,512]{1,0:T(8,128)S(1)}, f32[64,512]{1,0:T(8,128)S(1)}, u32[]{:S(2)}, u32[]{:S(2)}) collective-permute-start(f32[64,512]{1,0:T(8,128)S(1)} %get-tuple-element.60), channel_id=1, source_target_pairs={{1,2},{3,4},{5,6},{7,0},{2,1},{4,3},{6,5},{0,7},{9,10},{11,12},{13... | collective-permute-start | bytes 393224 | tf_op jit(solution)/shard_map/ppermute | solution.py:45
  42.6 0.7 shard_map.48
  43.3 1.3 %collective-permute-start.7 = (f32[64,512]{1,0:T(8,128)S(1)}, f32[64,512]{1,0:T(8,128)S(1)}, u32[]{:S(2)}, u32[]{:S(2)}) collective-permute-start(f32[64,512]{1,0:T(8,128)S(1)} %get-tuple-element.51), channel_id=1, source_target_pairs={{1,2},{3,4},{5,6},{7,0},{2,1},{4,3},{6,5},{0,7},{9,10},{11,12},{13... | collective-permute-start | bytes 393224 | tf_op jit(solution)/shard_map/ppermute | solution.py:45
  44.6 3.7 %collective-permute-done.13.refs_2_ = f32[40,512]{1,0:T(8,128)S(1)} collective-permute-done((f32[40,512]{1,0:T(8,128)S(1)}, f32[40,512]{1,0:T(8,128)S(1)}, u32[]{:S(2)}, u32[]{:S(2)}) %collective-permute-start.13) | collective-permute-done | bytes 81952 | tf_op jit(solution)/shard_map/ppermute | solution.py:45
  48.2 1.2 %collective-permute-start.1 = (f32[32,512]{1,0:T(8,128)S(1)}, f32[32,512]{1,0:T(8,128)S(1)}, u32[]{:S(2)}, u32[]{:S(2)}) collective-permute-start(f32[32,512]{1,0:T(8,128)S(1)} %get-tuple-element.42), channel_id=1, source_target_pairs={{1,2},{3,4},{5,6},{7,0},{2,1},{4,3},{6,5},{0,7},{9,10},{11,12},{13... | collective-permute-start | bytes 196616 | tf_op jit(solution)/shard_map/ppermute | solution.py:45
  49.8 1.2 %collective-permute-done.12.refs_2_ = f32[64,512]{1,0:T(8,128)S(1)} collective-permute-done((f32[64,512]{1,0:T(8,128)S(1)}, f32[64,512]{1,0:T(8,128)S(1)}, u32[]{:S(2)}, u32[]{:S(2)}) %collective-permute-start.12) | collective-permute-done | bytes 131104 | tf_op jit(solution)/shard_map/ppermute | solution.py:45
  51.5 1.3 %collective-permute-start.25 = (f32[64,512]{1,0:T(8,128)S(1)}, f32[64,512]{1,0:T(8,128)S(1)}, u32[]{:S(2)}, u32[]{:S(2)}) collective-permute-start(f32[64,512]{1,0:T(8,128)S(1)} %get-tuple-element.77), channel_id=1, source_target_pairs={{1,2},{3,4},{5,6},{7,0},{2,1},{4,3},{6,5},{0,7},{9,10},{11,12},{13... | collective-permute-start | bytes 393224 | tf_op jit(solution)/shard_map/ppermute | solution.py:45
  52.8 2.4 %collective-permute-done.1.refs_2_ = f32[32,512]{1,0:T(8,128)S(1)} collective-permute-done((f32[32,512]{1,0:T(8,128)S(1)}, f32[32,512]{1,0:T(8,128)S(1)}, u32[]{:S(2)}, u32[]{:S(2)}) %collective-permute-start.1) | collective-permute-done | bytes 65568 | tf_op jit(solution)/shard_map/ppermute | solution.py:45
  55.6 0.9 collective-permute-start.6
  56.6 1.2 shard_map.59
  57.7 1.8 %collective-permute-start.21 = (f32[2,56,512]{2,1,0:T(8,128)S(1)}, f32[2,56,512]{2,1,0:T(8,128)S(1)}, u32[]{:S(2)}, u32[]{:S(2)}) collective-permute-start(f32[2,56,512]{2,1,0:T(8,128)S(1)} %get-tuple-element.70), channel_id=1, source_target_pairs={{1,2},{3,4},{5,6},{7,0},{2,1},{4,3},{6,5},{0,7},{9,10},{11,12},{13... | collective-permute-start | bytes 688136 | tf_op jit(solution)/shard_map/ppermute | solution.py:45
  60.2 0.9 collective-permute-start.11
  61.6 1.7 %collective-permute-start.10 = (f32[48,512]{1,0:T(8,128)S(1)}, f32[48,512]{1,0:T(8,128)S(1)}, u32[]{:S(2)}, u32[]{:S(2)}) collective-permute-start(f32[48,512]{1,0:T(8,128)S(1)} %get-tuple-element.57), channel_id=1, source_target_pairs={{1,2},{3,4},{5,6},{7,0},{2,1},{4,3},{6,5},{0,7},{9,10},{11,12},{13... | collective-permute-start | bytes 294920 | tf_op jit(solution)/shard_map/ppermute | solution.py:45
  63.9 1.1 collective-permute-start.24
  64.9 4.5 %collective-permute-done.11.refs_2_ = f32[64,512]{1,0:T(8,128)S(1)} collective-permute-done((f32[64,512]{1,0:T(8,128)S(1)}, f32[64,512]{1,0:T(8,128)S(1)}, u32[]{:S(2)}, u32[]{:S(2)}) %collective-permute-start.11) | collective-permute-done | bytes 131104 | tf_op jit(solution)/shard_map/ppermute | solution.py:45
  69.9 1.1 collective-permute-done.10.refs_2_
  71.4 0.6 collective-permute-start.14
  72.3 2.2 %collective-permute-start.26 = (f32[64,512]{1,0:T(8,128)S(1)}, f32[64,512]{1,0:T(8,128)S(1)}, u32[]{:S(2)}, u32[]{:S(2)}) collective-permute-start(f32[64,512]{1,0:T(8,128)S(1)} %get-tuple-element.78), channel_id=1, source_target_pairs={{1,2},{3,4},{5,6},{7,0},{2,1},{4,3},{6,5},{0,7},{9,10},{11,12},{13... | collective-permute-start | bytes 393224 | tf_op jit(solution)/shard_map/ppermute | solution.py:45
  74.5 1.0 shard_map.60
  75.4 0.6 collective-permute-start.22
  76.4 2.6 %collective-permute-start.28 = (f32[4,64,512]{2,1,0:T(8,128)S(1)}, f32[4,64,512]{2,1,0:T(8,128)S(1)}, u32[]{:S(2)}, u32[]{:S(2)}) collective-permute-start(f32[4,64,512]{2,1,0:T(8,128)S(1)} %shard_map.63.refs_1_), channel_id=1, source_target_pairs={{0,8},{16,24},{1,9},{17,25},{2,10},{18,26},{3,11},{19,27},{4,12},{... | collective-permute-start | bytes 1572872 | tf_op jit(solution)/shard_map/ppermute | solution.py:57
  79.0 2.8 %collective-permute-start.27 = (f32[4,32,512]{2,1,0:T(8,128)S(1)}, f32[4,32,512]{2,1,0:T(8,128)S(1)}, u32[]{:S(2)}, u32[]{:S(2)}) collective-permute-start(f32[4,32,512]{2,1,0:T(8,128)S(1)} %shard_map.62.refs_0_), channel_id=1, source_target_pairs={{0,8},{16,24},{1,9},{17,25},{2,10},{18,26},{3,11},{19,27},{4,12},{... | collective-permute-start | bytes 786440 | tf_op jit(solution)/shard_map/ppermute | solution.py:57
  82.2 1.9 %collective-permute-done.22.refs_2_ = f32[2,56,512]{2,1,0:T(8,128)S(1)} collective-permute-done((f32[2,56,512]{2,1,0:T(8,128)S(1)}, f32[2,56,512]{2,1,0:T(8,128)S(1)}, u32[]{:S(2)}, u32[]{:S(2)}) %collective-permute-start.22) | collective-permute-done | bytes 229408 | tf_op jit(solution)/shard_map/ppermute | solution.py:45
  84.1 2.2 %collective-permute-start.29 = (f32[4,64,512]{2,1,0:T(8,128)S(1)}, f32[4,64,512]{2,1,0:T(8,128)S(1)}, u32[]{:S(2)}, u32[]{:S(2)}) collective-permute-start(f32[4,64,512]{2,1,0:T(8,128)S(1)} %shard_map.64.refs_2_), channel_id=1, source_target_pairs={{0,8},{16,24},{1,9},{17,25},{2,10},{18,26},{3,11},{19,27},{4,12},{... | collective-permute-start | bytes 1572872 | tf_op jit(solution)/shard_map/ppermute | solution.py:57
  86.6 10.7 %collective-permute-done.27.refs_3_ = f32[4,32,512]{2,1,0:T(8,128)S(1)} collective-permute-done((f32[4,32,512]{2,1,0:T(8,128)S(1)}, f32[4,32,512]{2,1,0:T(8,128)S(1)}, u32[]{:S(2)}, u32[]{:S(2)}) %collective-permute-start.27) | collective-permute-done | bytes 262176 | tf_op jit(solution)/shard_map/ppermute | solution.py:57
  97.3 2.9 %collective-permute-start.15 = (f32[4,48,512]{2,1,0:T(8,128)S(1)}, f32[4,48,512]{2,1,0:T(8,128)S(1)}, u32[]{:S(2)}, u32[]{:S(2)}) collective-permute-start(f32[4,48,512]{2,1,0:T(8,128)S(1)} %shard_map.58.refs_0_), channel_id=1, source_target_pairs={{0,8},{16,24},{1,9},{17,25},{2,10},{18,26},{3,11},{19,27},{4,12},{... | collective-permute-start | bytes 1179656 | tf_op jit(solution)/shard_map/ppermute | solution.py:57
  100.3 0.8 shard_map.61
  102.1 6.4 %collective-permute-done.29.refs_5_ = f32[4,64,512]{2,1,0:T(8,128)S(1)} collective-permute-done((f32[4,64,512]{2,1,0:T(8,128)S(1)}, f32[4,64,512]{2,1,0:T(8,128)S(1)}, u32[]{:S(2)}, u32[]{:S(2)}) %collective-permute-start.29) | collective-permute-done | bytes 524320 | tf_op jit(solution)/shard_map/ppermute | solution.py:57
  108.6 1.2 %shard_map.65.refs_5_ = f32[1,4,256,512]{3,2,1,0:T(8,128)} custom-call(s32[1]{0:T(128)S(6)} %copy.10.sides_ref, f32[1]{0:T(128)S(6)} %copy.9.fractions_ref.refs_4_, f32[4,32,512]{2,1,0:T(8,128)S(1)} %shard_map.62.refs_0_, f32[4,64,512]{2,1,0:T(8,128)S(1)} %shard_map.63.refs_1_, f32[4,64,512]{2,1,0:T(8,128)S(1)} %shard_map.64.refs_2_, ...), custom_call_target="tpu_custom_call" | custom-call | flops 983040 | bytes 3932160 | tf_op jit(solution)/shard_map/pallas_call | solution.py:389
  109.8 1.4 %shard_map.66.refs_3_ = f32[1,4,256,512]{3,2,1,0:T(8,128)} custom-call(f32[4,256,512]{2,1,0:T(8,128)S(1)} %copy-done, f32[4,256,512]{2,1,0:T(8,128)S(1)} %collective-permute-done.refs_1_, f32[2,56,512]{2,1,0:T(8,128)S(1)} %collective-permute-done.23.refs_2_, f32[2,5,56,512]{3,2,1,0:T(8,128)S(1)} %get-tuple-element.75.refs_3_, ...), custom_call_target="tpu_custom_call", output_to_operand_aliasing={{}: (5, {})} | custom-call | flops 4587520 | bytes 917504 | tf_op jit(solution)/shard_map/pallas_call | solution.py:342
  111.2 3.4 %collective-permute-done.15.refs_1_ = f32[4,48,512]{2,1,0:T(8,128)S(1)} collective-permute-done((f32[4,48,512]{2,1,0:T(8,128)S(1)}, f32[4,48,512]{2,1,0:T(8,128)S(1)}, u32[]{:S(2)}, u32[]{:S(2)}) %collective-permute-start.15) | collective-permute-done | bytes 393248 | tf_op jit(solution)/shard_map/ppermute | solution.py:57
  114.7 0.9 shard_map.67
  (48 shorter events, 7.3 us)
Async XLA Ops:
  0.0 27.0 %copy-start = (f32[4,256,512]{2,1,0:T(8,128)S(1)}, f32[4,256,512]{2,1,0:T(8,128)}, u32[]{:S(2)}) copy-start(f32[4,256,512]{2,1,0:T(8,128)} %refs_0_.39) | copy-start | bytes 6291460
  0.0 27.0 %collective-permute-start.2 = (f32[4,256,512]{2,1,0:T(8,128)}, f32[4,256,512]{2,1,0:T(8,128)S(1)}, u32[]{:S(2)}, u32[]{:S(2)}) collective-permute-start(f32[4,256,512]{2,1,0:T(8,128)} %bitcast.1), channel_id=1, source_target_pairs={{0,1},{2,3},{4,5},{6,7},{1,0},{3,2},{5,4},{7,6},{8,9},{10,11},{12,... | collective-permute-start | bytes 6291464 | tf_op jit(solution)/shard_map/ppermute | solution.py:45
  0.5 26.5 %collective-permute-start = (f32[4,256,512]{2,1,0:T(8,128)}, f32[4,256,512]{2,1,0:T(8,128)S(1)}, u32[]{:S(2)}, u32[]{:S(2)}) collective-permute-start(f32[4,256,512]{2,1,0:T(8,128)} %refs_0_.39), channel_id=1, source_target_pairs={{0,1},{2,3},{4,5},{6,7},{1,0},{3,2},{5,4},{7,6},{8,9},{10,11},{12,... | collective-permute-start | bytes 6291464 | tf_op jit(solution)/shard_map/ppermute | solution.py:45
  0.6 1.7 %copy-start.1 = (f32[1,4,256,512]{3,2,1,0:T(8,128)S(1)}, f32[1,4,256,512]{3,2,1,0:T(8,128)}, u32[]{:S(2)}) copy-start(f32[1,4,256,512]{3,2,1,0:T(8,128)} %field_ref.1) | copy-start | bytes 6291460
  2.9 5.3 %collective-permute-start.18 = (f32[4,56,512]{2,1,0:T(8,128)S(1)}, f32[4,56,512]{2,1,0:T(8,128)S(1)}, u32[]{:S(2)}, u32[]{:S(2)}) collective-permute-start(f32[4,56,512]{2,1,0:T(8,128)S(1)} %get-tuple-element.67.own_ref), channel_id=1, source_target_pairs={{8,16},{9,17},{10,18},{11,19},{12,20},{13,21},{14,22},{15,23},{0,1... | collective-permute-start | bytes 1376264 | tf_op jit(solution)/shard_map/ppermute | solution.py:57
  3.5 14.5 %collective-permute-start.17 = (f32[4,56,512]{2,1,0:T(8,128)S(1)}, f32[4,56,512]{2,1,0:T(8,128)S(1)}, u32[]{:S(2)}, u32[]{:S(2)}) collective-permute-start(f32[4,56,512]{2,1,0:T(8,128)S(1)} %get-tuple-element.67.own_ref), channel_id=1, source_target_pairs={{0,8},{16,24},{1,9},{17,25},{2,10},{18,26},{3,11},{19,27},{4,12},{... | collective-permute-start | bytes 1376264 | tf_op jit(solution)/shard_map/ppermute | solution.py:57
  18.0 38.5 %collective-permute-start.20 = (f32[4,56,512]{2,1,0:T(8,128)S(1)}, f32[4,56,512]{2,1,0:T(8,128)S(1)}, u32[]{:S(2)}, u32[]{:S(2)}) collective-permute-start(f32[4,56,512]{2,1,0:T(8,128)S(1)} %get-tuple-element.69.refs_5_), channel_id=1, source_target_pairs={{0,1},{2,3},{4,5},{6,7},{1,0},{3,2},{5,4},{7,6},{8,9},{10,11},{12,... | collective-permute-start | bytes 1376264 | tf_op jit(solution)/shard_map/ppermute | solution.py:45
  18.1 11.1 %collective-permute-start.4 = (f32[64,512]{1,0:T(8,128)S(1)}, f32[64,512]{1,0:T(8,128)S(1)}, u32[]{:S(2)}, u32[]{:S(2)}) collective-permute-start(f32[64,512]{1,0:T(8,128)S(1)} %get-tuple-element.44), channel_id=1, source_target_pairs={{1,2},{3,4},{5,6},{7,0},{2,1},{4,3},{6,5},{0,7},{9,10},{11,12},{13... | collective-permute-start | bytes 393224 | tf_op jit(solution)/shard_map/ppermute | solution.py:45
  20.6 6.3 %collective-permute-start.5 = (f32[56,512]{1,0:T(8,128)S(1)}, f32[56,512]{1,0:T(8,128)S(1)}, u32[]{:S(2)}, u32[]{:S(2)}) collective-permute-start(f32[56,512]{1,0:T(8,128)S(1)} %get-tuple-element.45), channel_id=1, source_target_pairs={{1,2},{3,4},{5,6},{7,0},{2,1},{4,3},{6,5},{0,7},{9,10},{11,12},{13... | collective-permute-start | bytes 344072 | tf_op jit(solution)/shard_map/ppermute | solution.py:45
  27.0 1.6 %copy-start.2 = (f32[1,4,256,512]{3,2,1,0:T(8,128)S(1)}, f32[1,4,256,512]{3,2,1,0:T(8,128)}, u32[]{:S(2)}) copy-start(f32[1,4,256,512]{3,2,1,0:T(8,128)} %field_ref.1) | copy-start | bytes 6291460
  29.9 10.6 %collective-permute-start.8 = (f32[64,512]{1,0:T(8,128)S(1)}, f32[64,512]{1,0:T(8,128)S(1)}, u32[]{:S(2)}, u32[]{:S(2)}) collective-permute-start(f32[64,512]{1,0:T(8,128)S(1)} %get-tuple-element.52), channel_id=1, source_target_pairs={{1,2},{3,4},{5,6},{7,0},{2,1},{4,3},{6,5},{0,7},{9,10},{11,12},{13... | collective-permute-start | bytes 393224 | tf_op jit(solution)/shard_map/ppermute | solution.py:45
  31.2 7.6 %collective-permute-start.9 = (f32[48,512]{1,0:T(8,128)S(1)}, f32[48,512]{1,0:T(8,128)S(1)}, u32[]{:S(2)}, u32[]{:S(2)}) collective-permute-start(f32[48,512]{1,0:T(8,128)S(1)} %get-tuple-element.53), channel_id=1, source_target_pairs={{1,2},{3,4},{5,6},{7,0},{2,1},{4,3},{6,5},{0,7},{9,10},{11,12},{13... | collective-permute-start | bytes 294920 | tf_op jit(solution)/shard_map/ppermute | solution.py:45
  32.6 10.0 %collective-permute-start.3 = (f32[64,512]{1,0:T(8,128)S(1)}, f32[64,512]{1,0:T(8,128)S(1)}, u32[]{:S(2)}, u32[]{:S(2)}) collective-permute-start(f32[64,512]{1,0:T(8,128)S(1)} %get-tuple-element.43), channel_id=1, source_target_pairs={{1,2},{3,4},{5,6},{7,0},{2,1},{4,3},{6,5},{0,7},{9,10},{11,12},{13... | collective-permute-start | bytes 393224 | tf_op jit(solution)/shard_map/ppermute | solution.py:45
  33.8 22.7 %collective-permute-start.19 = (f32[2,56,512]{2,1,0:T(8,128)S(1)}, f32[2,56,512]{2,1,0:T(8,128)S(1)}, u32[]{:S(2)}, u32[]{:S(2)}) collective-permute-start(f32[2,56,512]{2,1,0:T(8,128)S(1)} %get-tuple-element.68), channel_id=1, source_target_pairs={{1,2},{3,4},{5,6},{7,0},{2,1},{4,3},{6,5},{0,7},{9,10},{11,12},{13... | collective-permute-start | bytes 688136 | tf_op jit(solution)/shard_map/ppermute | solution.py:45
  39.2 9.0 %collective-permute-start.13 = (f32[40,512]{1,0:T(8,128)S(1)}, f32[40,512]{1,0:T(8,128)S(1)}, u32[]{:S(2)}, u32[]{:S(2)}) collective-permute-start(f32[40,512]{1,0:T(8,128)S(1)} %get-tuple-element.61), channel_id=1, source_target_pairs={{1,2},{3,4},{5,6},{7,0},{2,1},{4,3},{6,5},{0,7},{9,10},{11,12},{13... | collective-permute-start | bytes 245768 | tf_op jit(solution)/shard_map/ppermute | solution.py:45
  41.1 9.9 %collective-permute-start.12 = (f32[64,512]{1,0:T(8,128)S(1)}, f32[64,512]{1,0:T(8,128)S(1)}, u32[]{:S(2)}, u32[]{:S(2)}) collective-permute-start(f32[64,512]{1,0:T(8,128)S(1)} %get-tuple-element.60), channel_id=1, source_target_pairs={{1,2},{3,4},{5,6},{7,0},{2,1},{4,3},{6,5},{0,7},{9,10},{11,12},{13... | collective-permute-start | bytes 393224 | tf_op jit(solution)/shard_map/ppermute | solution.py:45
  43.3 16.3 %collective-permute-start.7 = (f32[64,512]{1,0:T(8,128)S(1)}, f32[64,512]{1,0:T(8,128)S(1)}, u32[]{:S(2)}, u32[]{:S(2)}) collective-permute-start(f32[64,512]{1,0:T(8,128)S(1)} %get-tuple-element.51), channel_id=1, source_target_pairs={{1,2},{3,4},{5,6},{7,0},{2,1},{4,3},{6,5},{0,7},{9,10},{11,12},{13... | collective-permute-start | bytes 393224 | tf_op jit(solution)/shard_map/ppermute | solution.py:45
  48.2 7.0 %collective-permute-start.1 = (f32[32,512]{1,0:T(8,128)S(1)}, f32[32,512]{1,0:T(8,128)S(1)}, u32[]{:S(2)}, u32[]{:S(2)}) collective-permute-start(f32[32,512]{1,0:T(8,128)S(1)} %get-tuple-element.42), channel_id=1, source_target_pairs={{1,2},{3,4},{5,6},{7,0},{2,1},{4,3},{6,5},{0,7},{9,10},{11,12},{13... | collective-permute-start | bytes 196616 | tf_op jit(solution)/shard_map/ppermute | solution.py:45
  51.5 11.8 %collective-permute-start.25 = (f32[64,512]{1,0:T(8,128)S(1)}, f32[64,512]{1,0:T(8,128)S(1)}, u32[]{:S(2)}, u32[]{:S(2)}) collective-permute-start(f32[64,512]{1,0:T(8,128)S(1)} %get-tuple-element.77), channel_id=1, source_target_pairs={{1,2},{3,4},{5,6},{7,0},{2,1},{4,3},{6,5},{0,7},{9,10},{11,12},{13... | collective-permute-start | bytes 393224 | tf_op jit(solution)/shard_map/ppermute | solution.py:45
  55.6 5.6 %collective-permute-start.6 = (f32[40,512]{1,0:T(8,128)S(1)}, f32[40,512]{1,0:T(8,128)S(1)}, u32[]{:S(2)}, u32[]{:S(2)}) collective-permute-start(f32[40,512]{1,0:T(8,128)S(1)} %get-tuple-element.49), channel_id=1, source_target_pairs={{1,2},{3,4},{5,6},{7,0},{2,1},{4,3},{6,5},{0,7},{9,10},{11,12},{13... | collective-permute-start | bytes 245768 | tf_op jit(solution)/shard_map/ppermute | solution.py:45
  57.7 16.7 %collective-permute-start.21 = (f32[2,56,512]{2,1,0:T(8,128)S(1)}, f32[2,56,512]{2,1,0:T(8,128)S(1)}, u32[]{:S(2)}, u32[]{:S(2)}) collective-permute-start(f32[2,56,512]{2,1,0:T(8,128)S(1)} %get-tuple-element.70), channel_id=1, source_target_pairs={{1,2},{3,4},{5,6},{7,0},{2,1},{4,3},{6,5},{0,7},{9,10},{11,12},{13... | collective-permute-start | bytes 688136 | tf_op jit(solution)/shard_map/ppermute | solution.py:45
  60.2 9.2 %collective-permute-start.11 = (f32[64,512]{1,0:T(8,128)S(1)}, f32[64,512]{1,0:T(8,128)S(1)}, u32[]{:S(2)}, u32[]{:S(2)}) collective-permute-start(f32[64,512]{1,0:T(8,128)S(1)} %get-tuple-element.59), channel_id=1, source_target_pairs={{1,2},{3,4},{5,6},{7,0},{2,1},{4,3},{6,5},{0,7},{9,10},{11,12},{13... | collective-permute-start | bytes 393224 | tf_op jit(solution)/shard_map/ppermute | solution.py:45
  61.6 9.4 %collective-permute-start.10 = (f32[48,512]{1,0:T(8,128)S(1)}, f32[48,512]{1,0:T(8,128)S(1)}, u32[]{:S(2)}, u32[]{:S(2)}) collective-permute-start(f32[48,512]{1,0:T(8,128)S(1)} %get-tuple-element.57), channel_id=1, source_target_pairs={{1,2},{3,4},{5,6},{7,0},{2,1},{4,3},{6,5},{0,7},{9,10},{11,12},{13... | collective-permute-start | bytes 294920 | tf_op jit(solution)/shard_map/ppermute | solution.py:45
  63.8 33.6 %collective-permute-start.31 = (f32[4,64,512]{2,1,0:T(8,128)S(1)}, f32[4,64,512]{2,1,0:T(8,128)S(1)}, u32[]{:S(2)}, u32[]{:S(2)}) collective-permute-start(f32[4,64,512]{2,1,0:T(8,128)S(1)} %shard_map.63.refs_1_), channel_id=1, source_target_pairs={{8,16},{9,17},{10,18},{11,19},{12,20},{13,21},{14,22},{15,23},{0,1... | collective-permute-start | bytes 1572872 | tf_op jit(solution)/shard_map/ppermute | solution.py:57
  63.9 8.1 %collective-permute-start.24 = (f32[32,512]{1,0:T(8,128)S(1)}, f32[32,512]{1,0:T(8,128)S(1)}, u32[]{:S(2)}, u32[]{:S(2)}) collective-permute-start(f32[32,512]{1,0:T(8,128)S(1)} %get-tuple-element.76), channel_id=1, source_target_pairs={{1,2},{3,4},{5,6},{7,0},{2,1},{4,3},{6,5},{0,7},{9,10},{11,12},{13... | collective-permute-start | bytes 196616 | tf_op jit(solution)/shard_map/ppermute | solution.py:45
  71.4 5.0 %collective-permute-start.14 = (f32[48,512]{1,0:T(8,128)S(1)}, f32[48,512]{1,0:T(8,128)S(1)}, u32[]{:S(2)}, u32[]{:S(2)}) collective-permute-start(f32[48,512]{1,0:T(8,128)S(1)} %get-tuple-element.65), channel_id=1, source_target_pairs={{1,2},{3,4},{5,6},{7,0},{2,1},{4,3},{6,5},{0,7},{9,10},{11,12},{13... | collective-permute-start | bytes 294920 | tf_op jit(solution)/shard_map/ppermute | solution.py:45
  72.2 11.9 %collective-permute-start.30 = (f32[4,32,512]{2,1,0:T(8,128)S(1)}, f32[4,32,512]{2,1,0:T(8,128)S(1)}, u32[]{:S(2)}, u32[]{:S(2)}) collective-permute-start(f32[4,32,512]{2,1,0:T(8,128)S(1)} %shard_map.62.refs_0_), channel_id=1, source_target_pairs={{8,16},{9,17},{10,18},{11,19},{12,20},{13,21},{14,22},{15,23},{0,1... | collective-permute-start | bytes 786440 | tf_op jit(solution)/shard_map/ppermute | solution.py:57
  72.3 6.7 %collective-permute-start.26 = (f32[64,512]{1,0:T(8,128)S(1)}, f32[64,512]{1,0:T(8,128)S(1)}, u32[]{:S(2)}, u32[]{:S(2)}) collective-permute-start(f32[64,512]{1,0:T(8,128)S(1)} %get-tuple-element.78), channel_id=1, source_target_pairs={{1,2},{3,4},{5,6},{7,0},{2,1},{4,3},{6,5},{0,7},{9,10},{11,12},{13... | collective-permute-start | bytes 393224 | tf_op jit(solution)/shard_map/ppermute | solution.py:45
  75.4 8.7 %collective-permute-start.22 = (f32[2,56,512]{2,1,0:T(8,128)S(1)}, f32[2,56,512]{2,1,0:T(8,128)S(1)}, u32[]{:S(2)}, u32[]{:S(2)}) collective-permute-start(f32[2,56,512]{2,1,0:T(8,128)S(1)} %get-tuple-element.72), channel_id=1, source_target_pairs={{1,2},{3,4},{5,6},{7,0},{2,1},{4,3},{6,5},{0,7},{9,10},{11,12},{13... | collective-permute-start | bytes 688136 | tf_op jit(solution)/shard_map/ppermute | solution.py:45
  76.4 24.7 %collective-permute-start.28 = (f32[4,64,512]{2,1,0:T(8,128)S(1)}, f32[4,64,512]{2,1,0:T(8,128)S(1)}, u32[]{:S(2)}, u32[]{:S(2)}) collective-permute-start(f32[4,64,512]{2,1,0:T(8,128)S(1)} %shard_map.63.refs_1_), channel_id=1, source_target_pairs={{0,8},{16,24},{1,9},{17,25},{2,10},{18,26},{3,11},{19,27},{4,12},{... | collective-permute-start | bytes 1572872 | tf_op jit(solution)/shard_map/ppermute | solution.py:57
  79.0 18.4 %collective-permute-start.27 = (f32[4,32,512]{2,1,0:T(8,128)S(1)}, f32[4,32,512]{2,1,0:T(8,128)S(1)}, u32[]{:S(2)}, u32[]{:S(2)}) collective-permute-start(f32[4,32,512]{2,1,0:T(8,128)S(1)} %shard_map.62.refs_0_), channel_id=1, source_target_pairs={{0,8},{16,24},{1,9},{17,25},{2,10},{18,26},{3,11},{19,27},{4,12},{... | collective-permute-start | bytes 786440 | tf_op jit(solution)/shard_map/ppermute | solution.py:57
  84.1 18.0 %collective-permute-start.32 = (f32[4,64,512]{2,1,0:T(8,128)S(1)}, f32[4,64,512]{2,1,0:T(8,128)S(1)}, u32[]{:S(2)}, u32[]{:S(2)}) collective-permute-start(f32[4,64,512]{2,1,0:T(8,128)S(1)} %shard_map.64.refs_2_), channel_id=1, source_target_pairs={{8,16},{9,17},{10,18},{11,19},{12,20},{13,21},{14,22},{15,23},{0,1... | collective-permute-start | bytes 1572872 | tf_op jit(solution)/shard_map/ppermute | solution.py:57
  84.1 24.5 %collective-permute-start.29 = (f32[4,64,512]{2,1,0:T(8,128)S(1)}, f32[4,64,512]{2,1,0:T(8,128)S(1)}, u32[]{:S(2)}, u32[]{:S(2)}) collective-permute-start(f32[4,64,512]{2,1,0:T(8,128)S(1)} %shard_map.64.refs_2_), channel_id=1, source_target_pairs={{0,8},{16,24},{1,9},{17,25},{2,10},{18,26},{3,11},{19,27},{4,12},{... | collective-permute-start | bytes 1572872 | tf_op jit(solution)/shard_map/ppermute | solution.py:57
  97.3 13.9 %collective-permute-start.16 = (f32[4,48,512]{2,1,0:T(8,128)S(1)}, f32[4,48,512]{2,1,0:T(8,128)S(1)}, u32[]{:S(2)}, u32[]{:S(2)}) collective-permute-start(f32[4,48,512]{2,1,0:T(8,128)S(1)} %shard_map.58.refs_0_), channel_id=1, source_target_pairs={{8,16},{9,17},{10,18},{11,19},{12,20},{13,21},{14,22},{15,23},{0,1... | collective-permute-start | bytes 1179656 | tf_op jit(solution)/shard_map/ppermute | solution.py:57
  97.3 17.4 %collective-permute-start.15 = (f32[4,48,512]{2,1,0:T(8,128)S(1)}, f32[4,48,512]{2,1,0:T(8,128)S(1)}, u32[]{:S(2)}, u32[]{:S(2)}) collective-permute-start(f32[4,48,512]{2,1,0:T(8,128)S(1)} %shard_map.58.refs_0_), channel_id=1, source_target_pairs={{0,8},{16,24},{1,9},{17,25},{2,10},{18,26},{3,11},{19,27},{4,12},{... | collective-permute-start | bytes 1179656 | tf_op jit(solution)/shard_map/ppermute | solution.py:57
  101.1 8.7 %collective-permute-start.23 = (f32[2,56,512]{2,1,0:T(8,128)S(1)}, f32[2,56,512]{2,1,0:T(8,128)S(1)}, u32[]{:S(2)}, u32[]{:S(2)}) collective-permute-start(f32[2,56,512]{2,1,0:T(8,128)S(1)} %get-tuple-element.74), channel_id=1, source_target_pairs={{1,2},{3,4},{5,6},{7,0},{2,1},{4,3},{6,5},{0,7},{9,10},{11,12},{13... | collective-permute-start | bytes 688136 | tf_op jit(solution)/shard_map/ppermute | solution.py:45

commit v2 on v1

v2 whole, which is shorter than its diff:
```python
import functools

import jax
import jax.numpy as jnp
from jax import lax
from jax.experimental import pallas as pl
from jax.experimental.pallas import tpu as pltpu
from jax.sharding import PartitionSpec as P

STEPS = 4
DT = 0.1
EPS2 = 1.5
TILE = 8
LANES = 128
BLOCK = 32
TOGETHER = 2

VMEM = pl.BlockSpec(memory_space=pltpu.VMEM)
SMEM = pl.BlockSpec(memory_space=pltpu.SMEM)
ANY = pl.BlockSpec(memory_space=pl.ANY)
HBM = pl.BlockSpec(memory_space=pltpu.HBM)

SHARES = (4, 8, 7, 5)
ORDER = (
    "E G O01 Cf",
    "L O11 Co Cn",
    "Cm ZA K01 O02",
    "O31 K11 O12 K02",
    "O03 K21 O22 K12",
    "O13 K03 N CN",
    "O04 OA1 K31 K22",
    "K13 O14 O23 K04",
    "Z0 O32 KA1 OA2",
    "K14 Z1 K23 O24",
    "K32 O33 KA2 OA3",
    "K24 Z2 K33 O34",
    "KA3 K34 OA4 Z3",
    "B0 KA4 B1",
)
BLENDS = ((0, 1, 2), (3,))


def swap(x, odd):
    count = lax.axis_size("space")
    assert count % 2 == 0
    pairs = [((i + odd) % count, (i + 1 + odd) % count) for i in range(0, count, 2)]
    return lax.ppermute(x, "space", pairs + [(b, a) for a, b in pairs])


def swap_images(x, odd):
    images, count = lax.axis_size("image"), lax.axis_size("space")
    assert images % 2 == 0
    pairs = []
    for s in range(count):
        pairs += [(i * count + s, (i + 1) * count + s) for i in range(odd, images - 1, 2)]
    if odd:
        for i in (0, images - 1):
            pairs += [(i * count + s, i * count + s + 1) for s in range(0, count, 2)]
    return lax.ppermute(x, ("image", "space"), pairs + [(b, a) for a, b in pairs])


def cuts(ny):
    bounds = [0]
    for share in SHARES:
        bounds.append(bounds[-1] + share * ny // 32)
    assert bounds[-1] < ny
    return bounds + [ny]


def span(bounds, c, s):
    moved = TILE * (STEPS - s)
    return (0 if c == 0 else bounds[c] + moved), (bounds[-1] if c == len(bounds) - 2 else bounds[c + 1] + moved)


def raw_group(bounds, c):
    first, last = (1, TOGETHER) if 1 <= c <= TOGETHER else (c, c)
    return span(bounds, first, 1)[0], span(bounds, last, 1)[1]


def layer_index(layer, layers):
    odd = lax.rem(lax.axis_index("space"), 2)
    return odd * (layers - 1) + layer * (1 - 2 * odd)


def at(first, rows=TILE):
    return pl.ds(first if isinstance(first, int) else pl.multiple_of(first, TILE), rows)


def params(mib):
    return pltpu.CompilerParams(vmem_limit_bytes=mib << 20)


def move(moves, sems):
    copies = [pltpu.make_async_copy(src, dst, sems.at[i]) for i, (src, dst) in enumerate(moves)]
    for copy in copies:
        copy.start()
    for copy in copies:
        copy.wait()


def first_edge(field, bounds):
    layers, _, nz = field.shape[1:]
    rows = span(bounds, 0, 1)[1]
    return lax.dynamic_slice(field, (0, layer_index(0, layers), 0, 0), (1, 1, rows, nz)).reshape(rows, nz)


def near_kernel(near, field_ref, ghost, sems):
    layers = field_ref.shape[1]
    move([(field_ref.at[0, layer_index(layers - 1 - k, layers), :near], ghost.at[k]) for k in range(layers)], sems)


def near_ghosts(field, bounds):
    layers, _, nz = field.shape[1:]
    near = span(bounds, 0, 0)[1]
    return pl.pallas_call(
        functools.partial(near_kernel, near),
        out_shape=jax.ShapeDtypeStruct((layers, near, nz), field.dtype),
        in_specs=[ANY],
        out_specs=VMEM,
        scratch_shapes=[pltpu.SemaphoreType.DMA((layers,))],
        compiler_params=params(12),
        name="near",
    )(field)


def later_kernel(spans, start, near, field_ref, mob_ref, ghost, raw, *refs):
    *edges, sems = refs
    layers = field_ref.shape[1]
    moves = []
    for k in range(layers - 1):
        moves.append((mob_ref.at[layer_index(layers - 1 - k, layers), :near], ghost.at[k]))
    moves.append((field_ref.at[0, :, start:], raw))
    moves += [(field_ref.at[0, layer_index(0, layers), lo:hi], edge) for (lo, hi), edge in zip(spans, edges)]
    move(moves, sems)


def later_edges(field, mobility, bounds):
    layers, ny, nz = field.shape[1:]
    spans = [raw_group(bounds, c) for c in (1, *range(TOGETHER + 1, len(bounds) - 2))]
    start, near = bounds[-2] - TILE, span(bounds, 0, 0)[1]
    shapes = [(layers - 1, near, nz), (layers, ny - start, nz)] + [(hi - lo, nz) for lo, hi in spans]
    return pl.pallas_call(
        functools.partial(later_kernel, spans, start, near),
        out_shape=[jax.ShapeDtypeStruct(shape, field.dtype) for shape in shapes],
        in_specs=[ANY, ANY],
        out_specs=[VMEM] * len(shapes),
        scratch_shapes=[pltpu.SemaphoreType.DMA((layers + len(spans),))],
        compiler_params=params(12),
        name="later",
    )(field, mobility)


def towards_even():
    image_odd = lax.rem(lax.axis_index("image"), 2)
    return lambda side: side != image_odd


def pick_kernel(skip, ahead, sides_ref, own_ref, even_ref, odd_ref, *refs):
    out_ref, edge_ref = refs[-2:]
    layers, rows, _ = out_ref.shape
    first = layer_index(0, layers)
    with_even = towards_even()(sides_ref[0])
    if ahead:
        edge_ref[:ahead, :] = refs[0][...]
    edge_ref[ahead : ahead + rows - skip, :] = own_ref[first, skip:, :]

    def take(src_ref):
        @pl.loop(0, rows // TILE)
        def _(i):
            for layer in range(layers):
                out_ref[layer, at(i * TILE), :] = src_ref[layer, at(i * TILE), :]
            edge_ref[at(i * TILE + ahead + rows - skip), :] = src_ref[first, at(i * TILE), :]

    pl.when(with_even)(lambda: take(even_ref))
    pl.when(jnp.logical_not(with_even))(lambda: take(odd_ref))


def pick(bounds, sides, own, even, odd, before):
    _, rows, nz = own.shape
    skip = span(bounds, len(bounds) - 2, 1)[0] - (bounds[-2] - TILE)
    ahead = 0 if before is None else before.shape[0]
    return pl.pallas_call(
        functools.partial(pick_kernel, skip, ahead),
        out_shape=[
            jax.ShapeDtypeStruct(own.shape, own.dtype),
            jax.ShapeDtypeStruct((ahead + 2 * rows - skip, nz), own.dtype),
        ],
        in_specs=[SMEM] + [VMEM] * (4 if ahead else 3),
        out_specs=[VMEM, VMEM],
        cost_estimate=pl.CostEstimate(flops=0, bytes_accessed=8 * own.size, transcendentals=0),
        compiler_params=params(12),
        name="pick",
    )(sides, own, even, odd, *([before] if ahead else []))


def relax_rows(cells, mobility, outer, store, n_out, first, final, top, bottom, nz):
    def block(r, rows, top, bottom):
        lane = lax.broadcasted_iota(jnp.int32, (rows, LANES), 1)
        none = jnp.zeros((TILE, nz), jnp.float32)
        under = outer(r, rows)
        mid = cells(0, r, rows)
        for layer in range(n_out):
            over = cells(layer + 1, r, rows)
            above = none if top else cells(layer, r - TILE, TILE)
            below = none if bottom else cells(layer, r + rows, TILE)
            wide = jnp.concatenate([above, mid, below], axis=0)
            up, down = wide[TILE - 1 : TILE - 1 + rows], wide[TILE + 1 : TILE + 1 + rows]
            right = pltpu.roll(mid, nz - 1, 1)
            right = jnp.concatenate(
                [right[:, :-LANES], jnp.where(lane == LANES - 1, 0.0, right[:, -LANES:])], axis=1
            )
            left = pltpu.roll(mid, 1, 1)
            left = jnp.concatenate([jnp.where(lane == 0, 0.0, left[:, :LANES]), left[:, LANES:]], axis=1)
            beside = (over + under) + (down + up) + (right + left)
            rate = DT * mobility(layer, r, rows)
            store(layer, r, rows, mid + rate * (EPS2 * beside - mid * (6.0 * EPS2 - 1.0 + mid * mid)))
            under, mid = mid, over

    for r in range(first, final, BLOCK):
        rows = min(BLOCK, final - r)
        block(r, rows, top and r == first, bottom and r + rows == final)


def outside():
    me, count = lax.axis_index("space"), lax.axis_size("space")
    return jnp.logical_or(me == 0, me == count - 1)


def margin(c, s):
    return 2 * TILE if c > 0 and 0 < s < STEPS else 0


def copy_ahead(ref):
    if "edge_before" not in ref:
        return 0
    rows = ref["edge_before"].shape[0]
    ref["edge"][:rows, :] = ref["edge_before"][...]
    return rows


def step_kernel(c, s, skip, bounds, layers, names, *refs):
    ref = dict(zip(names, refs))
    both = c == len(bounds) - 2
    last_step = s == STEPS
    ny, nz = ref["mob"].shape[1:]
    lo, hi = span(bounds, c, s)
    lead = margin(c, s)
    origin = 0 if s == 1 else span(bounds, c, s - 1)[0] - margin(c, s - 1)
    n_out = layers + STEPS - s
    no_outer = outside()

    def ghost_at(name, k, r, rows):
        return ref[name][k if c == 0 else layer_index(k, layers), at(r, rows), :]

    def cells(layer, r, rows):
        if s > 1:
            return ref["cells"][layer, at(r - origin, rows), :]
        if layer < layers:
            return ref["own"][layer_index(layer, layers), at(r, rows), :]
        return ghost_at("ghost", layer - layers, r, rows)

    def mobility(layer, r, rows):
        if layer < layers:
            return ref["mob"][layer_index(layer, layers), at(r, rows), :]
        return ghost_at("ghost_mob", layer - layers, r, rows)

    def outer(r, rows):
        return jnp.where(no_outer, 0.0, ref["beyond"][at(r - lo + skip, rows), :])

    edge_lo, edge_hi = span(bounds, c, s + 1) if not last_step else (0, 0)
    ahead = copy_ahead(ref)
    out = ref["own_out"]

    def store(layer, r, rows, new):
        out[layer, at(r - lo + lead, rows), :] = new
        if layer > 0 or last_step:
            return
        if r < edge_hi:
            kept = min(rows, edge_hi - r)
            ref["edge"][at(r - edge_lo + ahead, kept), :] = new[:kept]

    if c > 0 and not last_step:
        rows = ref["above"].shape[1]
        for layer in range(n_out):
            out[layer, 0:lead, :] = ref["above"][layer, rows - lead : rows, :]
        ref["edge"][ahead : ahead + TILE, :] = ref["above"][0, rows - TILE : rows, :]

    relax_rows(cells, mobility, outer, store, n_out, lo, hi, c == 0, both, nz)
    if not both:
        return

    start = lo_other = bounds[-2] - TILE
    if last_step:
        lo_other += TILE
    sent, kept = hi - lo, edge_hi - edge_lo

    def other_cells(layer, r, rows):
        if s > 1:
            return ref["other"][layer, at(r - start, rows), :]
        src = ref["other"] if layer < layers else ref["other_ghost"]
        return src[layer_index(layer % layers, layers), at(r - start, rows), :]

    def other_outer(r, rows):
        return jnp.where(no_outer, 0.0, ref["beyond"][at(r - start + sent + skip, rows), :])

    def other_store(layer, r, rows, new):
        if last_step:
            mine = out[layer, at(r - lo, rows), :]
            out[layer, at(r - lo, rows), :] = mine + ref["fractions"][0] * (new - mine)
            return
        ref["other_out"][layer, at(r - start, rows), :] = new
        if layer == 0:
            ref["edge"][at(r - start + kept + ahead, rows), :] = new

    relax_rows(
        other_cells, mobility, other_outer, other_store, n_out, lo_other, ny, not last_step, True, nz
    )
    if last_step:
        copies = [
            pltpu.make_async_copy(
                out.at[layer], ref["out"].at[0, layer_index(layer, layers), lo:hi], ref["sem"].at[layer]
            )
            for layer in range(layers)
        ]
        for copy in copies:
            copy.start()
        for copy in copies:
            copy.wait()


def step(c, s, skip, bounds, layers, arrays, like, field, before):
    ny, nz = like.shape[1:]
    lo, hi = span(bounds, c, s)
    both = c == len(bounds) - 2
    n_out = layers + STEPS - s
    rows = ny - bounds[-2] + TILE
    own = (n_out, margin(c, s) + hi - lo, nz)
    last_both = both and s == STEPS
    in_specs = [SMEM if name == "fractions" else VMEM for name in arrays]
    shapes, scratch, aliases = {}, {}, {}
    if last_both:
        shapes["out"] = field.shape
        scratch = {"own_out": pltpu.VMEM(own, like.dtype), "sem": pltpu.SemaphoreType.DMA((layers,))}
        if before is not None:
            aliases = {len(arrays): 0}
            arrays = {**arrays, "before": before}
            in_specs.append(ANY)
    else:
        shapes["own_out"] = own
        if both:
            shapes["other_out"] = (n_out, rows, nz)
        if s < STEPS:
            edge_lo, edge_hi = span(bounds, c, s + 1)
            ahead = arrays["edge_before"].shape[0] if "edge_before" in arrays else 0
            shapes["edge"] = (ahead + edge_hi - edge_lo + (rows if both else 0), nz)
    cells = n_out * (hi - lo + (rows if both else 0)) * nz
    outs = pl.pallas_call(
        functools.partial(step_kernel, c, s, skip, bounds, layers, [*arrays, *shapes, *scratch]),
        out_shape=[jax.ShapeDtypeStruct(shape, like.dtype) for shape in shapes.values()],
        in_specs=in_specs,
        out_specs=[ANY] if last_both else [VMEM] * len(shapes),
        scratch_shapes=list(scratch.values()),
        input_output_aliases=aliases,
        cost_estimate=pl.CostEstimate(flops=20 * cells, bytes_accessed=4 * cells, transcendentals=0),
        compiler_params=params(12),
    )(*arrays.values())
    return dict(zip(shapes, outs))


def blend_kernel(spans, aliased, sides_ref, fractions_ref, *refs):
    n = len(spans)
    owns, evens, odds = refs[:n], refs[n : 2 * n], refs[2 * n : 3 * n]
    out_ref, bufs, sem = refs[3 * n + aliased], refs[3 * n + aliased + 1 : -1], refs[-1]
    layers = owns[0].shape[0]
    with_even = towards_even()(sides_ref[0])
    share = fractions_ref[0]
    copies = []
    for k, (lo, hi) in enumerate(spans):
        def mix(other_ref, own_ref=owns[k], buf=bufs[k], rows=hi - lo):
            @pl.loop(0, rows // TILE)
            def _(i):
                for layer in range(layers):
                    mine = own_ref[layer, at(i * TILE), :]
                    buf[layer, at(i * TILE), :] = mine + share * (other_ref[layer, at(i * TILE), :] - mine)

        pl.when(with_even)(functools.partial(mix, evens[k]))
        pl.when(jnp.logical_not(with_even))(functools.partial(mix, odds[k]))
        for layer in range(layers):
            copy = pltpu.make_async_copy(
                bufs[k].at[layer], out_ref.at[0, layer_index(layer, layers), lo:hi], sem.at[k, layer]
            )
            copy.start()
            copies.append(copy)
    for copy in copies:
        copy.wait()


def blend(chunks, bounds, sides, fractions, val, out, like):
    spans = [span(bounds, c, STEPS) for c in chunks]
    owns = [val["K", c, STEPS] for c in chunks]
    layers = owns[0].shape[0]
    operands = [sides, fractions, *owns, *(val["Z", c, name] for name in ("even", "odd") for c in chunks)]
    size = sum(own.size for own in owns)
    return pl.pallas_call(
        functools.partial(blend_kernel, spans, out is not None),
        out_shape=jax.ShapeDtypeStruct(like.shape, like.dtype),
        in_specs=[SMEM, SMEM] + [VMEM] * (3 * len(chunks)) + ([] if out is None else [HBM]),
        out_specs=HBM,
        input_output_aliases={} if out is None else {len(operands): 0},
        scratch_shapes=[pltpu.VMEM(own.shape, own.dtype) for own in owns]
        + [pltpu.SemaphoreType.DMA((len(chunks), layers))],
        cost_estimate=pl.CostEstimate(flops=3 * size, bytes_accessed=12 * size, transcendentals=0),
        compiler_params=params(12),
    )(*operands, *([] if out is None else [out]))


def items():
    return " ".join(ORDER).split()


def chunk_of(name):
    return len(SHARES) if name == "A" else int(name)


def swaps():
    ahead = {}
    for item in items():
        members = [(chunk_of(m[0]), int(m[1])) for m in item[1:].split("_")] if item[0] == "O" else []
        ahead.update(zip(members[1:], members))
    return ahead


def local(field, mobility, fractions, sides):
    layers, ny = field.shape[1:3]
    bounds = cuts(ny)
    last = len(bounds) - 2
    ahead = swaps()
    val = {}
    out = None

    def before(c, s):
        return val["edge", ahead[c, s]] if (c, s) in ahead else None

    for item in items():
        kind = item[0]
        if kind == "E":
            val["edge", (0, 1)] = first_edge(field, bounds)
        elif kind == "G":
            val["near"] = near_ghosts(field, bounds)
        elif kind == "L":
            val["near_mob"], val["K", last, STEPS], *edges = later_edges(field, mobility, bounds)
            for i, edge in zip((1, *range(TOGETHER + 1, last)), edges):
                val["edge", (i, 1)] = edge
        elif kind == "C":
            sources = {"n": "near", "o": "near_mob", "N": "N", "f": field[0], "m": mobility}
            source = sources[item[1]]
            val["C", item[1]] = swap(val[source] if isinstance(source, str) else source, 0)
        elif kind == "N":
            val["N"], val["edge", (last, 1)] = pick(
                bounds,
                sides,
                val["K", last, STEPS],
                val["Z", last, "even"],
                val["Z", last, "odd"],
                before(last, 1),
            )
        elif kind == "O":
            members = [(chunk_of(m[0]), int(m[1])) for m in item[1:].split("_")]
            got = swap(val["edge", members[-1]], 1)
            skip = 0
            for c, s in members:
                val["O", c, s] = got, skip
                lo, hi = raw_group(bounds, c) if s == 1 else span(bounds, c, s)
                if (c, s) == (1, 1):
                    for i in range(2, TOGETHER + 1):
                        val["O", i, 1] = got, skip + span(bounds, i, 1)[0] - lo
                skip += hi - lo + (ny - bounds[-2] + TILE if c == last else 0)
        elif kind == "K":
            c, s = chunk_of(item[1]), int(item[2])
            beyond, skip = val["O", c, s]
            arrays = {"mob": mobility, "beyond": beyond}
            arrays["ghost_mob"] = val["C", "m" if c > 0 else "o"]
            if s == 1:
                arrays["ghost"] = val["C", "f" if c > 0 else "n"]
                arrays["own"] = field[0]
            else:
                arrays["cells"] = val["K", c, s - 1]
            if c > 0 and s < STEPS:
                arrays["above"] = val["K", c - 1, s]
            if c == last:
                arrays["other"] = val["N"] if s == 1 else val["other", s - 1]
                if s == 1:
                    arrays["other_ghost"] = val["C", "N"]
                if s == STEPS:
                    arrays["fractions"] = fractions
            if before(c, s + 1) is not None:
                arrays["edge_before"] = before(c, s + 1)
            got = step(c, s, skip, bounds, layers, arrays, mobility, field, out)
            if "out" in got:
                out = got["out"]
            else:
                val["K", c, s] = got["own_out"]
            val["other", s] = got.get("other_out", val.get(("other", s)))
            val["edge", (c, s + 1)] = got.get("edge")
        elif kind == "Z":
            c = chunk_of(item[1])
            for name, odd in (("even", 0), ("odd", 1)):
                val["Z", c, name] = swap_images(val["K", c, STEPS], odd)
        elif kind == "B":
            out = blend(BLENDS[int(item[1])], bounds, sides, fractions, val, out, field)
    return out


def solution(mesh):
    return jax.shard_map(
        local,
        mesh=mesh,
        in_specs=(P("image", "space", None, None), P("space", None, None), P("image"), P("image")),
        out_specs=P("image", "space", None, None),
        check_vma=False,
    )
```

time: 116 us -> 107 us (0.922)
  waiting for transfers between devices: 55.3 us -> 37.1 us
  Pallas kernels: 14.6 us -> 23.1 us
  local copies, waits for them, and re-layouts: 3.25 us -> 7.2 us
  starting transfers between devices: 40.9 us -> 37.4 us
    ppermute x10, waiting for transfers between devices: 30.3 us -> 11.6 us  [swap_images(): lax.ppermute(x, ('image', 'space'), pairs + [(b, a) for a, b in pairs])]
    pallas_call x22 -> x23, Pallas kernels: 12.5 us -> 21.1 us  [the longest x20 18.3 us: step(): pl.pallas_call(functools.partial(step_kernel, c, s, skip, bounds, layers,...]
    ppermute x10, starting transfers between devices: 15.3 us -> 11.7 us  [swap_images(): lax.ppermute(x, ('image', 'space'), pairs + [(b, a) for a, b in pairs])]
    unnamed x6 -> x16, local copies, waits for them, and re-layouts: 3.25 us -> 6.3 us
    ppermute x23 -> x24, waiting for transfers between devices: 24.9 us -> 25.5 us  [swap(): return lax.ppermute(x, 'space', pairs + [(b, a) for a, b in pairs])]
    ppermute x23 -> x24, starting transfers between devices: 25.6 us -> 25.7 us  [swap(): return lax.ppermute(x, 'space', pairs + [(b, a) for a, b in pairs])]
  transfers between devices with their start and end apart: 33 -> 34, of which waited for: 14 -> 13; matrix products, arithmetic and copies ran while one was open for 0% -> 1% of each run, Pallas kernels for 12% -> 21%
where the time goes in v2:
time: 107 us; the launch traced here: 106 us
  starting transfers between devices  37.4 us (35%)
  waiting for transfers between devices  37.1 us (35%)
  Pallas kernels  23.1 us (22%)
  local copies, waits for them, and re-layouts  7.2 us (7%)
  between operations  1.64 us (2%)
    ppermute x24, starting transfers between devices, swap(): return lax.ppermute(x, 'space', pairs + [(b, a) for a, b in pairs])  25.7 us
    ppermute x24, waiting for transfers between devices, swap(): return lax.ppermute(x, 'space', pairs + [(b, a) for a, b in pairs])  25.5 us
    pallas_call x20, Pallas kernels, step(): pl.pallas_call(functools.partial(step_kernel, c, s, skip, bounds, layers,...  18.3 us
    ppermute x10, starting transfers between devices, swap_images(): lax.ppermute(x, ('image', 'space'), pairs + [(b, a) for a, b in pairs])  11.7 us
    ppermute x10, waiting for transfers between devices, swap_images(): lax.ppermute(x, ('image', 'space'), pairs + [(b, a) for a, b in pairs])  11.6 us
    unnamed x16, local copies, waits for them, and re-layouts  6.3 us
  transfers between devices with their start and end apart: 34, of which 13 were waited for; matrix products, arithmetic and copies ran while one was open for 1% of the time, Pallas kernels for 21%

profile of v2, /device:TPU:0, one launch (start us, length us, event | category | flops | bytes accessed | tf_op | source)
XLA Modules:
  0.0 106.5 jit_solution(1819506628633536802)
XLA Ops:
  0.5 1.6 %copy-done = f32[4,256,512]{2,1,0:T(8,128)S(1)} copy-done((f32[4,256,512]{2,1,0:T(8,128)S(1)}, f32[4,256,512]{2,1,0:T(8,128)}, u32[]{:S(2)}) %copy-start) | copy-done | bytes 2097176
  2.1 1.6 %copy-done.2 = f32[1,4,256,512]{3,2,1,0:T(8,128)S(1)} copy-done((f32[1,4,256,512]{3,2,1,0:T(8,128)S(1)}, f32[1,4,256,512]{3,2,1,0:T(8,128)}, u32[]{:S(2)}) %copy-start.2) | copy-done | bytes 2097176
  3.7 1.0 later.1
  6.6 4.1 %collective-permute-start.18 = (f32[4,72,512]{2,1,0:T(8,128)S(1)}, f32[4,72,512]{2,1,0:T(8,128)}, u32[]{:S(2)}, u32[]{:S(2)}) collective-permute-start(f32[4,72,512]{2,1,0:T(8,128)S(1)} %get-tuple-element.68.own_ref), channel_id=1, source_target_pairs={{0,8},{16,24},{1,9},{17,25},{2,10},{18,26},{3,11},{19,27},{4,12},{... | collective-permute-start | bytes 1769480 | tf_op jit(solution)/shard_map/ppermute | solution.py:59
  10.7 0.9 dynamic-slice_bitcast_fusion
  11.6 1.6 %collective-permute-start.4 = (f32[56,512]{1,0:T(8,128)S(1)}, f32[56,512]{1,0:T(8,128)S(1)}, u32[]{:S(2)}, u32[]{:S(2)}) collective-permute-start(f32[56,512]{1,0:T(8,128)S(1)} %dynamic-slice_bitcast_fusion), channel_id=1, source_target_pairs={{1,2},{3,4},{5,6},{7,0},{2,1},{4,3},{6,5},{0,7},{9,10},{11,12},{13... | collective-permute-start | bytes 344072 | tf_op jit(solution)/shard_map/ppermute | solution.py:47
  13.2 4.7 %collective-permute-done.4.refs_1_ = f32[56,512]{1,0:T(8,128)S(1)} collective-permute-done((f32[56,512]{1,0:T(8,128)S(1)}, f32[56,512]{1,0:T(8,128)S(1)}, u32[]{:S(2)}, u32[]{:S(2)}) %collective-permute-start.4) | collective-permute-done | bytes 114720 | tf_op jit(solution)/shard_map/ppermute | solution.py:47
  17.9 1.7 %copy-done.3 = f32[1,4,256,512]{3,2,1,0:T(8,128)S(1)} copy-done((f32[1,4,256,512]{3,2,1,0:T(8,128)S(1)}, f32[1,4,256,512]{3,2,1,0:T(8,128)}, u32[]{:S(2)}) %copy-start.3) | copy-done | bytes 2097176
  20.8 3.2 %collective-permute-done.18.even_ref = f32[4,72,512]{2,1,0:T(8,128)} collective-permute-done((f32[4,72,512]{2,1,0:T(8,128)S(1)}, f32[4,72,512]{2,1,0:T(8,128)}, u32[]{:S(2)}, u32[]{:S(2)}) %collective-permute-start.18) | collective-permute-done | bytes 589856 | tf_op jit(solution)/shard_map/ppermute | solution.py:59
  24.0 1.2 %collective-permute-start.3 = (f32[120,512]{1,0:T(8,128)S(1)}, f32[120,512]{1,0:T(8,128)S(1)}, u32[]{:S(2)}, u32[]{:S(2)}) collective-permute-start(f32[120,512]{1,0:T(8,128)S(1)} %get-tuple-element.45), channel_id=1, source_target_pairs={{1,2},{3,4},{5,6},{7,0},{2,1},{4,3},{6,5},{0,7},{9,10},{11,12},{13... | collective-permute-start | bytes 737288 | tf_op jit(solution)/shard_map/ppermute | solution.py:47
  25.9 1.1 %pick.1 = (f32[4,72,512]{2,1,0:T(8,128)S(1)}, f32[112,512]{1,0:T(8,128)S(1)}) custom-call(s32[1]{0:T(128)S(6)} %copy.10.sides_ref, f32[4,72,512]{2,1,0:T(8,128)S(1)} %get-tuple-element.68.own_ref, f32[4,72,512]{2,1,0:T(8,128)} %collective-permute-done.18.even_ref, f32[4,72,512]{2,1,0:T(8,128)S(1)} %collective-permute-done.19.odd_ref), custom_call_target="tpu_custom_call" | custom-call | bytes 1179648 | tf_op jit(solution)/shard_map/pick/pallas_call | solution.py:182
  28.2 1.1 %collective-permute-start.10 = (f32[48,512]{1,0:T(8,128)S(1)}, f32[48,512]{1,0:T(8,128)S(1)}, u32[]{:S(2)}, u32[]{:S(2)}) collective-permute-start(f32[48,512]{1,0:T(8,128)S(1)} %get-tuple-element.54), channel_id=1, source_target_pairs={{1,2},{3,4},{5,6},{7,0},{2,1},{4,3},{6,5},{0,7},{9,10},{11,12},{13... | collective-permute-start | bytes 294920 | tf_op jit(solution)/shard_map/ppermute | solution.py:47
  29.3 3.8 %collective-permute-done.3.refs_1_ = f32[120,512]{1,0:T(8,128)S(1)} collective-permute-done((f32[120,512]{1,0:T(8,128)S(1)}, f32[120,512]{1,0:T(8,128)S(1)}, u32[]{:S(2)}, u32[]{:S(2)}) %collective-permute-start.3) | collective-permute-done | bytes 245792 | tf_op jit(solution)/shard_map/ppermute | solution.py:47
  33.1 2.3 %shard_map.47 = (f32[7,80,512]{2,1,0:T(8,128)S(1)}, f32[64,512]{1,0:T(8,128)S(1)}) custom-call(f32[4,256,512]{2,1,0:T(8,128)S(1)} %copy-done.1, f32[120,512]{1,0:T(8,128)S(1)} %collective-permute-done.3.refs_1_, f32[4,256,512]{2,1,0:T(8,128)S(1)} %collective-permute-done.1.refs_2_, f32[4,256,512]{2,1,0:T(8,128)} %collective-permute-done.2.refs_3_, ...), custom_call_target="tpu_custom_call" | custom-call | flops 4587520 | bytes 917504 | tf_op jit(solution)/shard_map/pallas_call | solution.py:357
  35.4 1.4 %collective-permute-start.9 = (f32[64,512]{1,0:T(8,128)S(1)}, f32[64,512]{1,0:T(8,128)S(1)}, u32[]{:S(2)}, u32[]{:S(2)}) collective-permute-start(f32[64,512]{1,0:T(8,128)S(1)} %get-tuple-element.53), channel_id=1, source_target_pairs={{1,2},{3,4},{5,6},{7,0},{2,1},{4,3},{6,5},{0,7},{9,10},{11,12},{13... | collective-permute-start | bytes 393224 | tf_op jit(solution)/shard_map/ppermute | solution.py:47
  37.2 1.4 %collective-permute-start.14 = (f32[40,512]{1,0:T(8,128)S(1)}, f32[40,512]{1,0:T(8,128)S(1)}, u32[]{:S(2)}, u32[]{:S(2)}) collective-permute-start(f32[40,512]{1,0:T(8,128)S(1)} %get-tuple-element.62), channel_id=1, source_target_pairs={{1,2},{3,4},{5,6},{7,0},{2,1},{4,3},{6,5},{0,7},{9,10},{11,12},{13... | collective-permute-start | bytes 245768 | tf_op jit(solution)/shard_map/ppermute | solution.py:47
  38.6 2.2 %shard_map.48 = (f32[7,72,512]{2,1,0:T(8,128)S(1)}, f32[56,512]{1,0:T(8,128)S(1)}) custom-call(f32[4,256,512]{2,1,0:T(8,128)S(1)} %copy-done.1, f32[120,512]{1,0:T(8,128)S(1)} %collective-permute-done.3.refs_1_, f32[4,256,512]{2,1,0:T(8,128)S(1)} %collective-permute-done.1.refs_2_, f32[4,256,512]{2,1,0:T(8,128)} %collective-permute-done.2.refs_3_, ...), custom_call_target="tpu_custom_call" | custom-call | flops 4014080 | bytes 802816 | tf_op jit(solution)/shard_map/pallas_call | solution.py:357
  40.8 1.4 %collective-permute-start.8 = (f32[56,512]{1,0:T(8,128)S(1)}, f32[56,512]{1,0:T(8,128)S(1)}, u32[]{:S(2)}, u32[]{:S(2)}) collective-permute-start(f32[56,512]{1,0:T(8,128)S(1)} %get-tuple-element.52), channel_id=1, source_target_pairs={{1,2},{3,4},{5,6},{7,0},{2,1},{4,3},{6,5},{0,7},{9,10},{11,12},{13... | collective-permute-start | bytes 344072 | tf_op jit(solution)/shard_map/ppermute | solution.py:47
  42.8 1.4 %collective-permute-start.13 = (f32[64,512]{1,0:T(8,128)S(1)}, f32[64,512]{1,0:T(8,128)S(1)}, u32[]{:S(2)}, u32[]{:S(2)}) collective-permute-start(f32[64,512]{1,0:T(8,128)S(1)} %get-tuple-element.61), channel_id=1, source_target_pairs={{1,2},{3,4},{5,6},{7,0},{2,1},{4,3},{6,5},{0,7},{9,10},{11,12},{13... | collective-permute-start | bytes 393224 | tf_op jit(solution)/shard_map/ppermute | solution.py:47
  44.2 1.3 %collective-permute-start.20 = (f32[112,512]{1,0:T(8,128)S(1)}, f32[112,512]{1,0:T(8,128)S(1)}, u32[]{:S(2)}, u32[]{:S(2)}) collective-permute-start(f32[112,512]{1,0:T(8,128)S(1)} %get-tuple-element.69), channel_id=1, source_target_pairs={{1,2},{3,4},{5,6},{7,0},{2,1},{4,3},{6,5},{0,7},{9,10},{11,12},{13... | collective-permute-start | bytes 688136 | tf_op jit(solution)/shard_map/ppermute | solution.py:47
  45.8 1.4 %collective-permute-start.25 = (f32[32,512]{1,0:T(8,128)S(1)}, f32[32,512]{1,0:T(8,128)S(1)}, u32[]{:S(2)}, u32[]{:S(2)}) collective-permute-start(f32[32,512]{1,0:T(8,128)S(1)} %get-tuple-element.80), channel_id=1, source_target_pairs={{1,2},{3,4},{5,6},{7,0},{2,1},{4,3},{6,5},{0,7},{9,10},{11,12},{13... | collective-permute-start | bytes 196616 | tf_op jit(solution)/shard_map/ppermute | solution.py:47
  47.8 1.4 %collective-permute-start.12 = (f32[56,512]{1,0:T(8,128)S(1)}, f32[56,512]{1,0:T(8,128)S(1)}, u32[]{:S(2)}, u32[]{:S(2)}) collective-permute-start(f32[56,512]{1,0:T(8,128)S(1)} %get-tuple-element.60), channel_id=1, source_target_pairs={{1,2},{3,4},{5,6},{7,0},{2,1},{4,3},{6,5},{0,7},{9,10},{11,12},{13... | collective-permute-start | bytes 344072 | tf_op jit(solution)/shard_map/ppermute | solution.py:47
  49.1 6.7 %collective-permute-done.25.refs_1_ = f32[32,512]{1,0:T(8,128)S(1)} collective-permute-done((f32[32,512]{1,0:T(8,128)S(1)}, f32[32,512]{1,0:T(8,128)S(1)}, u32[]{:S(2)}, u32[]{:S(2)}) %collective-permute-start.25) | collective-permute-done | bytes 65568 | tf_op jit(solution)/shard_map/ppermute | solution.py:47
  58.0 1.9 %collective-permute-start.27 = (f32[56,512]{1,0:T(8,128)S(1)}, f32[56,512]{1,0:T(8,128)S(1)}, u32[]{:S(2)}, u32[]{:S(2)}) collective-permute-start(f32[56,512]{1,0:T(8,128)S(1)} %get-tuple-element.82), channel_id=1, source_target_pairs={{1,2},{3,4},{5,6},{7,0},{2,1},{4,3},{6,5},{0,7},{9,10},{11,12},{13... | collective-permute-start | bytes 344072 | tf_op jit(solution)/shard_map/ppermute | solution.py:47
  59.9 1.3 %collective-permute-done.refs_1_ = f32[40,512]{1,0:T(8,128)S(1)} collective-permute-done((f32[40,512]{1,0:T(8,128)S(1)}, f32[40,512]{1,0:T(8,128)S(1)}, u32[]{:S(2)}, u32[]{:S(2)}) %collective-permute-start) | collective-permute-done | bytes 81952 | tf_op jit(solution)/shard_map/ppermute | solution.py:47
  61.2 2.0 %shard_map.49 = (f32[7,56,512]{2,1,0:T(8,128)S(1)}, f32[40,512]{1,0:T(8,128)S(1)}) custom-call(f32[4,256,512]{2,1,0:T(8,128)S(1)} %copy-done.1, f32[40,512]{1,0:T(8,128)S(1)} %collective-permute-done.refs_1_, f32[4,256,512]{2,1,0:T(8,128)S(1)} %collective-permute-done.1.refs_2_, f32[4,256,512]{2,1,0:T(8,128)} %collective-permute-done.2.refs_3_, ...), custom_call_target="tpu_custom_call" | custom-call | flops 2867200 | bytes 573440 | tf_op jit(solution)/shard_map/pallas_call | solution.py:357
  63.3 1.1 %collective-permute-start.7 = (f32[40,512]{1,0:T(8,128)S(1)}, f32[40,512]{1,0:T(8,128)S(1)}, u32[]{:S(2)}, u32[]{:S(2)}) collective-permute-start(f32[40,512]{1,0:T(8,128)S(1)} %get-tuple-element.50), channel_id=1, source_target_pairs={{1,2},{3,4},{5,6},{7,0},{2,1},{4,3},{6,5},{0,7},{9,10},{11,12},{13... | collective-permute-start | bytes 245768 | tf_op jit(solution)/shard_map/ppermute | solution.py:47
  64.4 2.8 %shard_map.59 = (f32[7,56,512]{2,1,0:T(8,128)S(1)}, f32[7,72,512]{2,1,0:T(8,128)S(1)}, f32[120,512]{1,0:T(8,128)S(1)}) custom-call(f32[4,256,512]{2,1,0:T(8,128)S(1)} %copy-done.1, f32[112,512]{1,0:T(8,128)S(1)} %collective-permute-done.20.refs_1_, f32[4,256,512]{2,1,0:T(8,128)S(1)} %collective-permute-done.1.refs_2_, ...), custom_call_target="tpu_custom_call" | custom-call | flops 8028160 | bytes 1605632 | tf_op jit(solution)/shard_map/pallas_call | solution.py:357
  67.1 1.7 %collective-permute-start.22 = (f32[120,512]{1,0:T(8,128)S(1)}, f32[120,512]{1,0:T(8,128)S(1)}, u32[]{:S(2)}, u32[]{:S(2)}) collective-permute-start(f32[120,512]{1,0:T(8,128)S(1)} %get-tuple-element.71), channel_id=1, source_target_pairs={{1,2},{3,4},{5,6},{7,0},{2,1},{4,3},{6,5},{0,7},{9,10},{11,12},{13... | collective-permute-start | bytes 737288 | tf_op jit(solution)/shard_map/ppermute | solution.py:47
  69.3 1.0 collective-permute-start.11
  70.3 2.5 %collective-permute-start.28 = (f32[4,32,512]{2,1,0:T(8,128)S(1)}, f32[4,32,512]{2,1,0:T(8,128)S(1)}, u32[]{:S(2)}, u32[]{:S(2)}) collective-permute-start(f32[4,32,512]{2,1,0:T(8,128)S(1)} %shard_map.62.refs_0_), channel_id=1, source_target_pairs={{0,8},{16,24},{1,9},{17,25},{2,10},{18,26},{3,11},{19,27},{4,12},{... | collective-permute-start | bytes 786440 | tf_op jit(solution)/shard_map/ppermute | solution.py:59
  73.2 1.8 %collective-permute-start.30 = (f32[4,56,512]{2,1,0:T(8,128)S(1)}, f32[4,56,512]{2,1,0:T(8,128)S(1)}, u32[]{:S(2)}, u32[]{:S(2)}) collective-permute-start(f32[4,56,512]{2,1,0:T(8,128)S(1)} %shard_map.64.refs_2_), channel_id=1, source_target_pairs={{0,8},{16,24},{1,9},{17,25},{2,10},{18,26},{3,11},{19,27},{4,12},{... | collective-permute-start | bytes 1376264 | tf_op jit(solution)/shard_map/ppermute | solution.py:59
  75.1 2.1 %collective-permute-done.11.refs_1_ = f32[40,512]{1,0:T(8,128)S(1)} collective-permute-done((f32[40,512]{1,0:T(8,128)S(1)}, f32[40,512]{1,0:T(8,128)S(1)}, u32[]{:S(2)}, u32[]{:S(2)}) %collective-permute-start.11) | collective-permute-done | bytes 81952 | tf_op jit(solution)/shard_map/ppermute | solution.py:47
  77.2 1.1 collective-permute-start.26
  78.6 1.7 %collective-permute-start.15 = (f32[40,512]{1,0:T(8,128)S(1)}, f32[40,512]{1,0:T(8,128)S(1)}, u32[]{:S(2)}, u32[]{:S(2)}) collective-permute-start(f32[40,512]{1,0:T(8,128)S(1)} %get-tuple-element.66), channel_id=1, source_target_pairs={{1,2},{3,4},{5,6},{7,0},{2,1},{4,3},{6,5},{0,7},{9,10},{11,12},{13... | collective-permute-start | bytes 245768 | tf_op jit(solution)/shard_map/ppermute | solution.py:47
  80.2 1.1 shard_map.60
  81.3 1.9 %collective-permute-done.26.refs_1_ = f32[64,512]{1,0:T(8,128)S(1)} collective-permute-done((f32[64,512]{1,0:T(8,128)S(1)}, f32[64,512]{1,0:T(8,128)S(1)}, u32[]{:S(2)}, u32[]{:S(2)}) %collective-permute-start.26) | collective-permute-done | bytes 131104 | tf_op jit(solution)/shard_map/ppermute | solution.py:47
  84.3 1.6 %collective-permute-start.29 = (f32[4,64,512]{2,1,0:T(8,128)S(1)}, f32[4,64,512]{2,1,0:T(8,128)S(1)}, u32[]{:S(2)}, u32[]{:S(2)}) collective-permute-start(f32[4,64,512]{2,1,0:T(8,128)S(1)} %shard_map.63.refs_1_), channel_id=1, source_target_pairs={{0,8},{16,24},{1,9},{17,25},{2,10},{18,26},{3,11},{19,27},{4,12},{... | collective-permute-start | bytes 1572872 | tf_op jit(solution)/shard_map/ppermute | solution.py:59
  86.2 3.7 %collective-permute-done.23.refs_1_ = f32[128,512]{1,0:T(8,128)S(1)} collective-permute-done((f32[128,512]{1,0:T(8,128)S(1)}, f32[128,512]{1,0:T(8,128)S(1)}, u32[]{:S(2)}, u32[]{:S(2)}) %collective-permute-start.23) | collective-permute-done | bytes 262176 | tf_op jit(solution)/shard_map/ppermute | solution.py:47
  89.9 0.9 collective-permute-start.16
  90.8 0.9 shard_map.61
  91.8 1.0 collective-permute-start.24
  93.5 5.7 %collective-permute-done.29.refs_4_ = f32[4,64,512]{2,1,0:T(8,128)S(1)} collective-permute-done((f32[4,64,512]{2,1,0:T(8,128)S(1)}, f32[4,64,512]{2,1,0:T(8,128)S(1)}, u32[]{:S(2)}, u32[]{:S(2)}) %collective-permute-start.29) | collective-permute-done | bytes 524320 | tf_op jit(solution)/shard_map/ppermute | solution.py:59
  99.2 1.2 %shard_map.65.refs_6_ = f32[1,4,256,512]{3,2,1,0:T(8,128)} custom-call(s32[1]{0:T(128)S(6)} %copy.10.sides_ref, f32[1]{0:T(128)S(6)} %copy.9.fractions_ref.refs_5_, f32[4,32,512]{2,1,0:T(8,128)S(1)} %shard_map.62.refs_0_, f32[4,64,512]{2,1,0:T(8,128)S(1)} %shard_map.63.refs_1_, f32[4,56,512]{2,1,0:T(8,128)S(1)} %shard_map.64.refs_2_, ...), custom_call_target="tpu_custom_call" | custom-call | flops 933888 | bytes 3735552 | tf_op jit(solution)/shard_map/pallas_call | solution.py:404
  100.4 0.9 collective-permute-done.24.refs_1_
  101.3 1.6 %shard_map.66.refs_3_ = f32[1,4,256,512]{3,2,1,0:T(8,128)} custom-call(f32[4,256,512]{2,1,0:T(8,128)S(1)} %copy-done.1, f32[136,512]{1,0:T(8,128)S(1)} %collective-permute-done.24.refs_1_, f32[4,256,512]{2,1,0:T(8,128)S(1)} %collective-permute-done.1.refs_2_, f32[5,72,512]{2,1,0:T(8,128)S(1)} %get-tuple-element.78.refs_3_, ...), custom_call_target="tpu_custom_call", output_to_operand_aliasing={{}: (6, {})} | custom-call | flops 5570560 | bytes 1114112 | tf_op jit(solution)/shard_map/pallas_call | solution.py:357
  103.0 2.7 %collective-permute-done.16.refs_1_ = f32[4,40,512]{2,1,0:T(8,128)S(1)} collective-permute-done((f32[4,40,512]{2,1,0:T(8,128)S(1)}, f32[4,40,512]{2,1,0:T(8,128)S(1)}, u32[]{:S(2)}, u32[]{:S(2)}) %collective-permute-start.16) | collective-permute-done | bytes 327712 | tf_op jit(solution)/shard_map/ppermute | solution.py:59
  105.7 0.8 shard_map.67
  (62 shorter events, 11.2 us)
Async XLA Ops:
  0.0 33.1 %collective-permute-start.2 = (f32[4,256,512]{2,1,0:T(8,128)}, f32[4,256,512]{2,1,0:T(8,128)}, u32[]{:S(2)}, u32[]{:S(2)}) collective-permute-start(f32[4,256,512]{2,1,0:T(8,128)} %bitcast.3), channel_id=1, source_target_pairs={{0,1},{2,3},{4,5},{6,7},{1,0},{3,2},{5,4},{7,6},{8,9},{10,11},{12,... | collective-permute-start | bytes 6291464 | tf_op jit(solution)/shard_map/ppermute | solution.py:47
  0.5 32.6 %collective-permute-start.1 = (f32[4,256,512]{2,1,0:T(8,128)}, f32[4,256,512]{2,1,0:T(8,128)S(1)}, u32[]{:S(2)}, u32[]{:S(2)}) collective-permute-start(f32[4,256,512]{2,1,0:T(8,128)} %refs_0_.39), channel_id=1, source_target_pairs={{0,1},{2,3},{4,5},{6,7},{1,0},{3,2},{5,4},{7,6},{8,9},{10,11},{12,... | collective-permute-start | bytes 6291464 | tf_op jit(solution)/shard_map/ppermute | solution.py:47
  0.5 1.6 %copy-start = (f32[4,256,512]{2,1,0:T(8,128)S(1)}, f32[4,256,512]{2,1,0:T(8,128)}, u32[]{:S(2)}) copy-start(f32[4,256,512]{2,1,0:T(8,128)} %refs_0_.39) | copy-start | bytes 6291460
  2.1 1.6 %copy-start.2 = (f32[1,4,256,512]{3,2,1,0:T(8,128)S(1)}, f32[1,4,256,512]{3,2,1,0:T(8,128)}, u32[]{:S(2)}) copy-start(f32[1,4,256,512]{3,2,1,0:T(8,128)} %field_ref.3) | copy-start | bytes 6291460
  4.7 0.6 copy-start.6
  5.3 0.7 copy-start.5
  6.1 14.3 %collective-permute-start.19 = (f32[4,72,512]{2,1,0:T(8,128)S(1)}, f32[4,72,512]{2,1,0:T(8,128)S(1)}, u32[]{:S(2)}, u32[]{:S(2)}) collective-permute-start(f32[4,72,512]{2,1,0:T(8,128)S(1)} %get-tuple-element.68.own_ref), channel_id=1, source_target_pairs={{8,16},{9,17},{10,18},{11,19},{12,20},{13,21},{14,22},{15,23},{0,1... | collective-permute-start | bytes 1769480 | tf_op jit(solution)/shard_map/ppermute | solution.py:59
  6.6 17.5 %collective-permute-start.18 = (f32[4,72,512]{2,1,0:T(8,128)S(1)}, f32[4,72,512]{2,1,0:T(8,128)}, u32[]{:S(2)}, u32[]{:S(2)}) collective-permute-start(f32[4,72,512]{2,1,0:T(8,128)S(1)} %get-tuple-element.68.own_ref), channel_id=1, source_target_pairs={{0,8},{16,24},{1,9},{17,25},{2,10},{18,26},{3,11},{19,27},{4,12},{... | collective-permute-start | bytes 1769480 | tf_op jit(solution)/shard_map/ppermute | solution.py:59
  11.6 6.3 %collective-permute-start.4 = (f32[56,512]{1,0:T(8,128)S(1)}, f32[56,512]{1,0:T(8,128)S(1)}, u32[]{:S(2)}, u32[]{:S(2)}) collective-permute-start(f32[56,512]{1,0:T(8,128)S(1)} %dynamic-slice_bitcast_fusion), channel_id=1, source_target_pairs={{1,2},{3,4},{5,6},{7,0},{2,1},{4,3},{6,5},{0,7},{9,10},{11,12},{13... | collective-permute-start | bytes 344072 | tf_op jit(solution)/shard_map/ppermute | solution.py:47
  17.9 9.6 %copy-start.1 = (f32[4,256,512]{2,1,0:T(8,128)S(1)}, f32[4,256,512]{2,1,0:T(8,128)}, u32[]{:S(2)}) copy-start(f32[4,256,512]{2,1,0:T(8,128)} %refs_0_.39) | copy-start | bytes 6291460
  17.9 9.1 %collective-permute-start.5 = (f32[3,64,512]{2,1,0:T(8,128)}, f32[3,64,512]{2,1,0:T(8,128)S(1)}, u32[]{:S(2)}, u32[]{:S(2)}) collective-permute-start(f32[3,64,512]{2,1,0:T(8,128)} %copy-done.5), channel_id=1, source_target_pairs={{0,1},{2,3},{4,5},{6,7},{1,0},{3,2},{5,4},{7,6},{8,9},{10,11},{12,... | collective-permute-start | bytes 1179656 | tf_op jit(solution)/shard_map/ppermute | solution.py:47
  17.9 1.7 %copy-start.3 = (f32[1,4,256,512]{3,2,1,0:T(8,128)S(1)}, f32[1,4,256,512]{3,2,1,0:T(8,128)}, u32[]{:S(2)}) copy-start(f32[1,4,256,512]{3,2,1,0:T(8,128)} %field_ref.3) | copy-start | bytes 6291460
  19.7 7.9 %copy-start.4 = (f32[1,4,256,512]{3,2,1,0:T(8,128)S(1)}, f32[1,4,256,512]{3,2,1,0:T(8,128)}, u32[]{:S(2)}) copy-start(f32[1,4,256,512]{3,2,1,0:T(8,128)} %field_ref.3) | copy-start | bytes 6291460
  20.4 7.1 %collective-permute-start.6 = (f32[4,64,512]{2,1,0:T(8,128)S(1)}, f32[4,64,512]{2,1,0:T(8,128)S(1)}, u32[]{:S(2)}, u32[]{:S(2)}) collective-permute-start(f32[4,64,512]{2,1,0:T(8,128)S(1)} %near.1), channel_id=1, source_target_pairs={{0,1},{2,3},{4,5},{6,7},{1,0},{3,2},{5,4},{7,6},{8,9},{10,11},{12,... | collective-permute-start | bytes 1572872 | tf_op jit(solution)/shard_map/ppermute | solution.py:47
  24.0 9.1 %collective-permute-start.3 = (f32[120,512]{1,0:T(8,128)S(1)}, f32[120,512]{1,0:T(8,128)S(1)}, u32[]{:S(2)}, u32[]{:S(2)}) collective-permute-start(f32[120,512]{1,0:T(8,128)S(1)} %get-tuple-element.45), channel_id=1, source_target_pairs={{1,2},{3,4},{5,6},{7,0},{2,1},{4,3},{6,5},{0,7},{9,10},{11,12},{13... | collective-permute-start | bytes 737288 | tf_op jit(solution)/shard_map/ppermute | solution.py:47
  27.1 37.3 %collective-permute-start.21 = (f32[4,72,512]{2,1,0:T(8,128)S(1)}, f32[4,72,512]{2,1,0:T(8,128)S(1)}, u32[]{:S(2)}, u32[]{:S(2)}) collective-permute-start(f32[4,72,512]{2,1,0:T(8,128)S(1)} %get-tuple-element.70.refs_6_), channel_id=1, source_target_pairs={{0,1},{2,3},{4,5},{6,7},{1,0},{3,2},{5,4},{7,6},{8,9},{10,11},{12,... | collective-permute-start | bytes 1769480 | tf_op jit(solution)/shard_map/ppermute | solution.py:47
  28.2 8.6 %collective-permute-start.10 = (f32[48,512]{1,0:T(8,128)S(1)}, f32[48,512]{1,0:T(8,128)S(1)}, u32[]{:S(2)}, u32[]{:S(2)}) collective-permute-start(f32[48,512]{1,0:T(8,128)S(1)} %get-tuple-element.54), channel_id=1, source_target_pairs={{1,2},{3,4},{5,6},{7,0},{2,1},{4,3},{6,5},{0,7},{9,10},{11,12},{13... | collective-permute-start | bytes 294920 | tf_op jit(solution)/shard_map/ppermute | solution.py:47
  35.4 6.8 %collective-permute-start.9 = (f32[64,512]{1,0:T(8,128)S(1)}, f32[64,512]{1,0:T(8,128)S(1)}, u32[]{:S(2)}, u32[]{:S(2)}) collective-permute-start(f32[64,512]{1,0:T(8,128)S(1)} %get-tuple-element.53), channel_id=1, source_target_pairs={{1,2},{3,4},{5,6},{7,0},{2,1},{4,3},{6,5},{0,7},{9,10},{11,12},{13... | collective-permute-start | bytes 393224 | tf_op jit(solution)/shard_map/ppermute | solution.py:47
  37.2 8.3 %collective-permute-start.14 = (f32[40,512]{1,0:T(8,128)S(1)}, f32[40,512]{1,0:T(8,128)S(1)}, u32[]{:S(2)}, u32[]{:S(2)}) collective-permute-start(f32[40,512]{1,0:T(8,128)S(1)} %get-tuple-element.62), channel_id=1, source_target_pairs={{1,2},{3,4},{5,6},{7,0},{2,1},{4,3},{6,5},{0,7},{9,10},{11,12},{13... | collective-permute-start | bytes 245768 | tf_op jit(solution)/shard_map/ppermute | solution.py:47
  40.8 6.4 %collective-permute-start.8 = (f32[56,512]{1,0:T(8,128)S(1)}, f32[56,512]{1,0:T(8,128)S(1)}, u32[]{:S(2)}, u32[]{:S(2)}) collective-permute-start(f32[56,512]{1,0:T(8,128)S(1)} %get-tuple-element.52), channel_id=1, source_target_pairs={{1,2},{3,4},{5,6},{7,0},{2,1},{4,3},{6,5},{0,7},{9,10},{11,12},{13... | collective-permute-start | bytes 344072 | tf_op jit(solution)/shard_map/ppermute | solution.py:47
  42.8 13.4 %collective-permute-start.13 = (f32[64,512]{1,0:T(8,128)S(1)}, f32[64,512]{1,0:T(8,128)S(1)}, u32[]{:S(2)}, u32[]{:S(2)}) collective-permute-start(f32[64,512]{1,0:T(8,128)S(1)} %get-tuple-element.61), channel_id=1, source_target_pairs={{1,2},{3,4},{5,6},{7,0},{2,1},{4,3},{6,5},{0,7},{9,10},{11,12},{13... | collective-permute-start | bytes 393224 | tf_op jit(solution)/shard_map/ppermute | solution.py:47
  44.2 20.2 %collective-permute-start.20 = (f32[112,512]{1,0:T(8,128)S(1)}, f32[112,512]{1,0:T(8,128)S(1)}, u32[]{:S(2)}, u32[]{:S(2)}) collective-permute-start(f32[112,512]{1,0:T(8,128)S(1)} %get-tuple-element.69), channel_id=1, source_target_pairs={{1,2},{3,4},{5,6},{7,0},{2,1},{4,3},{6,5},{0,7},{9,10},{11,12},{13... | collective-permute-start | bytes 688136 | tf_op jit(solution)/shard_map/ppermute | solution.py:47
  45.8 10.0 %collective-permute-start.25 = (f32[32,512]{1,0:T(8,128)S(1)}, f32[32,512]{1,0:T(8,128)S(1)}, u32[]{:S(2)}, u32[]{:S(2)}) collective-permute-start(f32[32,512]{1,0:T(8,128)S(1)} %get-tuple-element.80), channel_id=1, source_target_pairs={{1,2},{3,4},{5,6},{7,0},{2,1},{4,3},{6,5},{0,7},{9,10},{11,12},{13... | collective-permute-start | bytes 196616 | tf_op jit(solution)/shard_map/ppermute | solution.py:47
  47.8 8.4 %copy-start.7 = (f32[40,512]{1,0:T(8,128)S(1)}, f32[40,512]{1,0:T(8,128)}, u32[]{:S(2)}) copy-start(f32[40,512]{1,0:T(8,128)} %copy-done.6) | copy-start | bytes 245764
  47.8 9.8 %collective-permute-start.12 = (f32[56,512]{1,0:T(8,128)S(1)}, f32[56,512]{1,0:T(8,128)S(1)}, u32[]{:S(2)}, u32[]{:S(2)}) collective-permute-start(f32[56,512]{1,0:T(8,128)S(1)} %get-tuple-element.60), channel_id=1, source_target_pairs={{1,2},{3,4},{5,6},{7,0},{2,1},{4,3},{6,5},{0,7},{9,10},{11,12},{13... | collective-permute-start | bytes 344072 | tf_op jit(solution)/shard_map/ppermute | solution.py:47
  56.1 17.2 %collective-permute-start.31 = (f32[4,32,512]{2,1,0:T(8,128)S(1)}, f32[4,32,512]{2,1,0:T(8,128)S(1)}, u32[]{:S(2)}, u32[]{:S(2)}) collective-permute-start(f32[4,32,512]{2,1,0:T(8,128)S(1)} %shard_map.62.refs_0_), channel_id=1, source_target_pairs={{8,16},{9,17},{10,18},{11,19},{12,20},{13,21},{14,22},{15,23},{0,1... | collective-permute-start | bytes 786440 | tf_op jit(solution)/shard_map/ppermute | solution.py:59
  56.2 5.0 %collective-permute-start = (f32[40,512]{1,0:T(8,128)S(1)}, f32[40,512]{1,0:T(8,128)S(1)}, u32[]{:S(2)}, u32[]{:S(2)}) collective-permute-start(f32[40,512]{1,0:T(8,128)S(1)} %copy-done.7), channel_id=1, source_target_pairs={{1,2},{3,4},{5,6},{7,0},{2,1},{4,3},{6,5},{0,7},{9,10},{11,12},{13... | collective-permute-start | bytes 245768 | tf_op jit(solution)/shard_map/ppermute | solution.py:47
  58.0 14.8 %collective-permute-start.27 = (f32[56,512]{1,0:T(8,128)S(1)}, f32[56,512]{1,0:T(8,128)S(1)}, u32[]{:S(2)}, u32[]{:S(2)}) collective-permute-start(f32[56,512]{1,0:T(8,128)S(1)} %get-tuple-element.82), channel_id=1, source_target_pairs={{1,2},{3,4},{5,6},{7,0},{2,1},{4,3},{6,5},{0,7},{9,10},{11,12},{13... | collective-permute-start | bytes 344072 | tf_op jit(solution)/shard_map/ppermute | solution.py:47
  63.3 5.6 %collective-permute-start.7 = (f32[40,512]{1,0:T(8,128)S(1)}, f32[40,512]{1,0:T(8,128)S(1)}, u32[]{:S(2)}, u32[]{:S(2)}) collective-permute-start(f32[40,512]{1,0:T(8,128)S(1)} %get-tuple-element.50), channel_id=1, source_target_pairs={{1,2},{3,4},{5,6},{7,0},{2,1},{4,3},{6,5},{0,7},{9,10},{11,12},{13... | collective-permute-start | bytes 245768 | tf_op jit(solution)/shard_map/ppermute | solution.py:47
  67.1 11.4 %collective-permute-start.22 = (f32[120,512]{1,0:T(8,128)S(1)}, f32[120,512]{1,0:T(8,128)S(1)}, u32[]{:S(2)}, u32[]{:S(2)}) collective-permute-start(f32[120,512]{1,0:T(8,128)S(1)} %get-tuple-element.71), channel_id=1, source_target_pairs={{1,2},{3,4},{5,6},{7,0},{2,1},{4,3},{6,5},{0,7},{9,10},{11,12},{13... | collective-permute-start | bytes 737288 | tf_op jit(solution)/shard_map/ppermute | solution.py:47
  69.3 7.9 %collective-permute-start.11 = (f32[40,512]{1,0:T(8,128)S(1)}, f32[40,512]{1,0:T(8,128)S(1)}, u32[]{:S(2)}, u32[]{:S(2)}) collective-permute-start(f32[40,512]{1,0:T(8,128)S(1)} %get-tuple-element.58), channel_id=1, source_target_pairs={{1,2},{3,4},{5,6},{7,0},{2,1},{4,3},{6,5},{0,7},{9,10},{11,12},{13... | collective-permute-start | bytes 245768 | tf_op jit(solution)/shard_map/ppermute | solution.py:47
  70.3 13.9 %collective-permute-start.28 = (f32[4,32,512]{2,1,0:T(8,128)S(1)}, f32[4,32,512]{2,1,0:T(8,128)S(1)}, u32[]{:S(2)}, u32[]{:S(2)}) collective-permute-start(f32[4,32,512]{2,1,0:T(8,128)S(1)} %shard_map.62.refs_0_), channel_id=1, source_target_pairs={{0,8},{16,24},{1,9},{17,25},{2,10},{18,26},{3,11},{19,27},{4,12},{... | collective-permute-start | bytes 786440 | tf_op jit(solution)/shard_map/ppermute | solution.py:59
  73.2 16.8 %collective-permute-start.33 = (f32[4,56,512]{2,1,0:T(8,128)S(1)}, f32[4,56,512]{2,1,0:T(8,128)S(1)}, u32[]{:S(2)}, u32[]{:S(2)}) collective-permute-start(f32[4,56,512]{2,1,0:T(8,128)S(1)} %shard_map.64.refs_2_), channel_id=1, source_target_pairs={{8,16},{9,17},{10,18},{11,19},{12,20},{13,21},{14,22},{15,23},{0,1... | collective-permute-start | bytes 1376264 | tf_op jit(solution)/shard_map/ppermute | solution.py:59
  73.2 18.5 %collective-permute-start.30 = (f32[4,56,512]{2,1,0:T(8,128)S(1)}, f32[4,56,512]{2,1,0:T(8,128)S(1)}, u32[]{:S(2)}, u32[]{:S(2)}) collective-permute-start(f32[4,56,512]{2,1,0:T(8,128)S(1)} %shard_map.64.refs_2_), channel_id=1, source_target_pairs={{0,8},{16,24},{1,9},{17,25},{2,10},{18,26},{3,11},{19,27},{4,12},{... | collective-permute-start | bytes 1376264 | tf_op jit(solution)/shard_map/ppermute | solution.py:59
  77.2 6.0 %collective-permute-start.26 = (f32[64,512]{1,0:T(8,128)S(1)}, f32[64,512]{1,0:T(8,128)S(1)}, u32[]{:S(2)}, u32[]{:S(2)}) collective-permute-start(f32[64,512]{1,0:T(8,128)S(1)} %get-tuple-element.81), channel_id=1, source_target_pairs={{1,2},{3,4},{5,6},{7,0},{2,1},{4,3},{6,5},{0,7},{9,10},{11,12},{13... | collective-permute-start | bytes 393224 | tf_op jit(solution)/shard_map/ppermute | solution.py:47
  78.6 5.7 %collective-permute-start.15 = (f32[40,512]{1,0:T(8,128)S(1)}, f32[40,512]{1,0:T(8,128)S(1)}, u32[]{:S(2)}, u32[]{:S(2)}) collective-permute-start(f32[40,512]{1,0:T(8,128)S(1)} %get-tuple-element.66), channel_id=1, source_target_pairs={{1,2},{3,4},{5,6},{7,0},{2,1},{4,3},{6,5},{0,7},{9,10},{11,12},{13... | collective-permute-start | bytes 245768 | tf_op jit(solution)/shard_map/ppermute | solution.py:47
  83.2 6.7 %collective-permute-start.23 = (f32[128,512]{1,0:T(8,128)S(1)}, f32[128,512]{1,0:T(8,128)S(1)}, u32[]{:S(2)}, u32[]{:S(2)}) collective-permute-start(f32[128,512]{1,0:T(8,128)S(1)} %get-tuple-element.74), channel_id=1, source_target_pairs={{1,2},{3,4},{5,6},{7,0},{2,1},{4,3},{6,5},{0,7},{9,10},{11,12},{13... | collective-permute-start | bytes 786440 | tf_op jit(solution)/shard_map/ppermute | solution.py:47
  84.2 9.2 %collective-permute-start.32 = (f32[4,64,512]{2,1,0:T(8,128)S(1)}, f32[4,64,512]{2,1,0:T(8,128)S(1)}, u32[]{:S(2)}, u32[]{:S(2)}) collective-permute-start(f32[4,64,512]{2,1,0:T(8,128)S(1)} %shard_map.63.refs_1_), channel_id=1, source_target_pairs={{8,16},{9,17},{10,18},{11,19},{12,20},{13,21},{14,22},{15,23},{0,1... | collective-permute-start | bytes 1572872 | tf_op jit(solution)/shard_map/ppermute | solution.py:59
  84.3 14.9 %collective-permute-start.29 = (f32[4,64,512]{2,1,0:T(8,128)S(1)}, f32[4,64,512]{2,1,0:T(8,128)S(1)}, u32[]{:S(2)}, u32[]{:S(2)}) collective-permute-start(f32[4,64,512]{2,1,0:T(8,128)S(1)} %shard_map.63.refs_1_), channel_id=1, source_target_pairs={{0,8},{16,24},{1,9},{17,25},{2,10},{18,26},{3,11},{19,27},{4,12},{... | collective-permute-start | bytes 1572872 | tf_op jit(solution)/shard_map/ppermute | solution.py:59
  89.9 13.0 %collective-permute-start.17 = (f32[4,40,512]{2,1,0:T(8,128)S(1)}, f32[4,40,512]{2,1,0:T(8,128)S(1)}, u32[]{:S(2)}, u32[]{:S(2)}) collective-permute-start(f32[4,40,512]{2,1,0:T(8,128)S(1)} %shard_map.58.refs_0_), channel_id=1, source_target_pairs={{8,16},{9,17},{10,18},{11,19},{12,20},{13,21},{14,22},{15,23},{0,1... | collective-permute-start | bytes 983048 | tf_op jit(solution)/shard_map/ppermute | solution.py:59
  89.9 15.7 %collective-permute-start.16 = (f32[4,40,512]{2,1,0:T(8,128)S(1)}, f32[4,40,512]{2,1,0:T(8,128)S(1)}, u32[]{:S(2)}, u32[]{:S(2)}) collective-permute-start(f32[4,40,512]{2,1,0:T(8,128)S(1)} %shard_map.58.refs_0_), channel_id=1, source_target_pairs={{0,8},{16,24},{1,9},{17,25},{2,10},{18,26},{3,11},{19,27},{4,12},{... | collective-permute-start | bytes 983048 | tf_op jit(solution)/shard_map/ppermute | solution.py:59
  91.8 9.5 %collective-permute-start.24 = (f32[136,512]{1,0:T(8,128)S(1)}, f32[136,512]{1,0:T(8,128)S(1)}, u32[]{:S(2)}, u32[]{:S(2)}) collective-permute-start(f32[136,512]{1,0:T(8,128)S(1)} %get-tuple-element.77), channel_id=1, source_target_pairs={{1,2},{3,4},{5,6},{7,0},{2,1},{4,3},{6,5},{0,7},{9,10},{11,12},{13... | collective-permute-start | bytes 835592 | tf_op jit(solution)/shard_map/ppermute | solution.py:47

commit v3 on v2

--- a/solution.py
+++ b/solution.py
@@ -20,21 +20,22 @@
 ANY = pl.BlockSpec(memory_space=pl.ANY)
 HBM = pl.BlockSpec(memory_space=pltpu.HBM)
 
-SHARES = (4, 8, 7, 5)
+SHARES = (5, 8, 7, 4)
 ORDER = (
     "E G O01 Cf",
     "L O11 Co Cn",
     "Cm ZA K01 O02",
     "O31 K11 O12 K02",
     "O03 K21 O22 K12",
-    "O13 K03 N CN",
-    "O04 OA1 K31 K22",
-    "K13 O14 O23 K04",
-    "Z0 O32 KA1 OA2",
-    "K14 Z1 K23 O24",
-    "K32 O33 KA2 OA3",
-    "K24 Z2 K33 O34",
-    "KA3 K34 OA4 Z3",
+    "O13 K03 O04 N",
+    "CN OA1 K31 K22",
+    "K13 O14 K04 Z0",
+    "O23 O32 JA1 OA2",
+    "KA1 K14 Z1 K23",
+    "O24 K32 O33 JA2",
+    "OA3 KA2 K24 Z2",
+    "K33 O34 JA3 OA4",
+    "K34 Z3 KA3 IA4",
     "B0 KA4 B1",
 )
 BLENDS = ((0, 1, 2), (3,))
@@ -193,13 +194,13 @@
     )(sides, own, even, odd, *([before] if ahead else []))
 
 
-def relax_rows(cells, mobility, outer, store, n_out, first, final, top, bottom, nz):
+def relax_rows(cells, mobility, outer, store, some, first, final, top, bottom, nz):
     def block(r, rows, top, bottom):
         lane = lax.broadcasted_iota(jnp.int32, (rows, LANES), 1)
         none = jnp.zeros((TILE, nz), jnp.float32)
-        under = outer(r, rows)
-        mid = cells(0, r, rows)
-        for layer in range(n_out):
+        under = outer(r, rows) if some[0] == 0 else cells(some[0] - 1, r, rows)
+        mid = cells(some[0], r, rows)
+        for layer in some:
             over = cells(layer + 1, r, rows)
             above = none if top else cells(layer, r - TILE, TILE)
             below = none if bottom else cells(layer, r + rows, TILE)
@@ -212,8 +213,8 @@
             left = pltpu.roll(mid, 1, 1)
             left = jnp.concatenate([jnp.where(lane == 0, 0.0, left[:, :LANES]), left[:, LANES:]], axis=1)
             beside = (over + under) + (down + up) + (right + left)
-            rate = DT * mobility(layer, r, rows)
-            store(layer, r, rows, mid + rate * (EPS2 * beside - mid * (6.0 * EPS2 - 1.0 + mid * mid)))
+            rest = mid * (6.0 - 1.0 / EPS2 + (1.0 / EPS2) * (mid * mid))
+            store(layer, r, rows, mid + (DT * EPS2 * mobility(layer, r, rows)) * (beside - rest))
             under, mid = mid, over
 
     for r in range(first, final, BLOCK):
@@ -238,7 +239,7 @@
     return rows
 
 
-def step_kernel(c, s, skip, bounds, layers, names, *refs):
+def step_kernel(c, s, part, skip, bounds, layers, names, *refs):
     ref = dict(zip(names, refs))
     both = c == len(bounds) - 2
     last_step = s == STEPS
@@ -247,6 +248,9 @@
     lead = margin(c, s)
     origin = 0 if s == 1 else span(bounds, c, s - 1)[0] - margin(c, s - 1)
     n_out = layers + STEPS - s
+    some = {"edge": range(1), "inner": range(1, n_out), "outer": range(1)}.get(part, range(n_out))
+    gives_edge = part in ("all", "edge") and not last_step
+    gives_cells = part != "edge"
     no_outer = outside()
 
     def ghost_at(name, k, r, rows):
@@ -268,12 +272,13 @@
         return jnp.where(no_outer, 0.0, ref["beyond"][at(r - lo + skip, rows), :])
 
     edge_lo, edge_hi = span(bounds, c, s + 1) if not last_step else (0, 0)
-    ahead = copy_ahead(ref)
-    out = ref["own_out"]
+    ahead = copy_ahead(ref) if gives_edge else 0
+    out = ref["own_out"] if gives_cells else None
 
     def store(layer, r, rows, new):
-        out[layer, at(r - lo + lead, rows), :] = new
-        if layer > 0 or last_step:
+        if gives_cells:
+            out[layer - (some[0] if last_step else 0), at(r - lo + lead, rows), :] = new
+        if layer > 0 or not gives_edge:
             return
         if r < edge_hi:
             kept = min(rows, edge_hi - r)
@@ -281,17 +286,18 @@
 
     if c > 0 and not last_step:
         rows = ref["above"].shape[1]
-        for layer in range(n_out):
-            out[layer, 0:lead, :] = ref["above"][layer, rows - lead : rows, :]
-        ref["edge"][ahead : ahead + TILE, :] = ref["above"][0, rows - TILE : rows, :]
-
-    relax_rows(cells, mobility, outer, store, n_out, lo, hi, c == 0, both, nz)
+        if gives_cells:
+            for layer in range(n_out):
+                out[layer, 0:lead, :] = ref["above"][layer, rows - lead : rows, :]
+        if gives_edge:
+            ref["edge"][ahead : ahead + TILE, :] = ref["above"][0, rows - TILE : rows, :]
+
+    relax_rows(cells, mobility, outer, store, some, lo, hi, c == 0, both, nz)
     if not both:
         return
 
-    start = lo_other = bounds[-2] - TILE
-    if last_step:
-        lo_other += TILE
+    start = bounds[-2] - TILE
+    lo_other = other_first(bounds, s)
     sent, kept = hi - lo, edge_hi - edge_lo
 
     def other_cells(layer, r, rows):
@@ -301,34 +307,33 @@
         return src[layer_index(layer % layers, layers), at(r - start, rows), :]
 
     def other_outer(r, rows):
-        return jnp.where(no_outer, 0.0, ref["beyond"][at(r - start + sent + skip, rows), :])
+        return jnp.where(no_outer, 0.0, ref["beyond"][at(r - lo_other + sent + skip, rows), :])
 
     def other_store(layer, r, rows, new):
         if last_step:
-            mine = out[layer, at(r - lo, rows), :]
-            out[layer, at(r - lo, rows), :] = mine + ref["fractions"][0] * (new - mine)
+            here = layer - some[0], at(r - lo, rows), slice(None)
+            mine = out[here]
+            out[here] = mine + ref["fractions"][0] * (new - mine)
             return
-        ref["other_out"][layer, at(r - start, rows), :] = new
-        if layer == 0:
-            ref["edge"][at(r - start + kept + ahead, rows), :] = new
-
-    relax_rows(
-        other_cells, mobility, other_outer, other_store, n_out, lo_other, ny, not last_step, True, nz
-    )
+        if gives_cells:
+            ref["other_out"][layer, at(r - start, rows), :] = new
+        if layer == 0 and gives_edge:
+            cut = max(0, other_first(bounds, s + 1) - r)
+            ref["edge"][at(r + cut - other_first(bounds, s + 1) + kept + ahead, rows - cut), :] = new[cut:]
+
+    relax_rows(other_cells, mobility, other_outer, other_store, some, lo_other, ny, not last_step, True, nz)
     if last_step:
-        copies = [
-            pltpu.make_async_copy(
-                out.at[layer], ref["out"].at[0, layer_index(layer, layers), lo:hi], ref["sem"].at[layer]
-            )
-            for layer in range(layers)
-        ]
-        for copy in copies:
-            copy.start()
-        for copy in copies:
-            copy.wait()
-
-
-def step(c, s, skip, bounds, layers, arrays, like, field, before):
+        move(
+            [(out.at[layer - some[0]], ref["out"].at[0, layer_index(layer, layers), lo:hi]) for layer in some],
+            ref["sem"],
+        )
+
+
+def other_first(bounds, s):
+    return bounds[-2] - (TILE if s < STEPS else 0)
+
+
+def step(c, s, part, skip, bounds, layers, arrays, like, field, before):
     ny, nz = like.shape[1:]
     lo, hi = span(bounds, c, s)
     both = c == len(bounds) - 2
@@ -340,22 +345,24 @@
     shapes, scratch, aliases = {}, {}, {}
     if last_both:
         shapes["out"] = field.shape
+        own = ({"inner": layers - 1, "outer": 1}.get(part, layers), *own[1:])
         scratch = {"own_out": pltpu.VMEM(own, like.dtype), "sem": pltpu.SemaphoreType.DMA((layers,))}
         if before is not None:
             aliases = {len(arrays): 0}
             arrays = {**arrays, "before": before}
             in_specs.append(ANY)
     else:
-        shapes["own_out"] = own
-        if both:
-            shapes["other_out"] = (n_out, rows, nz)
-        if s < STEPS:
+        if part != "edge":
+            shapes["own_out"] = own
+            if both:
+                shapes["other_out"] = (n_out, rows, nz)
+        if s < STEPS and part != "rest":
             edge_lo, edge_hi = span(bounds, c, s + 1)
             ahead = arrays["edge_before"].shape[0] if "edge_before" in arrays else 0
-            shapes["edge"] = (ahead + edge_hi - edge_lo + (rows if both else 0), nz)
+            shapes["edge"] = (ahead + edge_hi - edge_lo + (ny - other_first(bounds, s + 1) if both else 0), nz)
     cells = n_out * (hi - lo + (rows if both else 0)) * nz
     outs = pl.pallas_call(
-        functools.partial(step_kernel, c, s, skip, bounds, layers, [*arrays, *shapes, *scratch]),
+        functools.partial(step_kernel, c, s, part, skip, bounds, layers, [*arrays, *shapes, *scratch]),
         out_shape=[jax.ShapeDtypeStruct(shape, like.dtype) for shape in shapes.values()],
         in_specs=in_specs,
         out_specs=[ANY] if last_both else [VMEM] * len(shapes),
@@ -474,11 +481,17 @@
                 if (c, s) == (1, 1):
                     for i in range(2, TOGETHER + 1):
                         val["O", i, 1] = got, skip + span(bounds, i, 1)[0] - lo
-                skip += hi - lo + (ny - bounds[-2] + TILE if c == last else 0)
-        elif kind == "K":
+                skip += hi - lo + (ny - other_first(bounds, s) if c == last else 0)
+        elif kind in "KJI":
             c, s = chunk_of(item[1]), int(item[2])
-            beyond, skip = val["O", c, s]
-            arrays = {"mob": mobility, "beyond": beyond}
+            split = c == last
+            part = "all"
+            if split:
+                part = {"J": "edge", "I": "inner"}.get(kind, "rest" if s < STEPS else "outer")
+            beyond, skip = val["O", c, s] if part != "inner" else (None, 0)
+            arrays = {"mob": mobility}
+            if beyond is not None:
+                arrays["beyond"] = beyond
             arrays["ghost_mob"] = val["C", "m" if c > 0 else "o"]
             if s == 1:
                 arrays["ghost"] = val["C", "f" if c > 0 else "n"]
@@ -493,15 +506,13 @@
                     arrays["other_ghost"] = val["C", "N"]
                 if s == STEPS:
                     arrays["fractions"] = fractions
-            if before(c, s + 1) is not None:
+            if before(c, s + 1) is not None and part in ("all", "edge"):
                 arrays["edge_before"] = before(c, s + 1)
-            got = step(c, s, skip, bounds, layers, arrays, mobility, field, out)
-            if "out" in got:
-                out = got["out"]
-            else:
-                val["K", c, s] = got["own_out"]
-            val["other", s] = got.get("other_out", val.get(("other", s)))
-            val["edge", (c, s + 1)] = got.get("edge")
+            got = step(c, s, part, skip, bounds, layers, arrays, mobility, field, out)
+            out = got.get("out", out)
+            for name, key in (("own_out", ("K", c, s)), ("other_out", ("other", s)), ("edge", ("edge", (c, s + 1)))):
+                if name in got:
+                    val[key] = got[name]
         elif kind == "Z":
             c = chunk_of(item[1])
             for name, odd in (("even", 0), ("odd", 1)):

time: 107 us -> 129 us (1.21)
  Pallas kernels: 23.1 us -> 55.3 us
  waiting for transfers between devices: 37.1 us -> 26.2 us
    pallas_call x20 -> x24, Pallas kernels: 18.3 us -> 48.3 us  [step(): pl.pallas_call(functools.partial(step_kernel, c, s, part, skip, bounds, l...]
    ppermute x24, waiting for transfers between devices: 25.5 us -> 16.6 us  [swap(): return lax.ppermute(x, 'space', pairs + [(b, a) for a, b in pairs])]
    ppermute x10, waiting for transfers between devices: 11.6 us -> 9.66 us  [swap_images(): lax.ppermute(x, ('image', 'space'), pairs + [(b, a) for a, b in pairs])]
    unnamed x16 -> x14, local copies, waits for them, and re-layouts: 6.3 us -> 6.66 us
  transfers between devices with their start and end apart: 34 -> 34, of which waited for: 13 -> 8; matrix products, arithmetic and copies ran while one was open for 1% -> 1% of each run, Pallas kernels for 21% -> 43%
where the time goes in v3:
time: 129 us; the launch traced here: 128 us
  Pallas kernels  55.3 us (43%)
  starting transfers between devices  37 us (29%)
  waiting for transfers between devices  26.2 us (20%)
  local copies, waits for them, and re-layouts  7.57 us (6%)
  between operations  1.91 us (1%)
    pallas_call x24, Pallas kernels, step(): pl.pallas_call(functools.partial(step_kernel, c, s, part, skip, bounds, l...  48.3 us
    ppermute x24, starting transfers between devices, swap(): return lax.ppermute(x, 'space', pairs + [(b, a) for a, b in pairs])  24.6 us
    ppermute x24, waiting for transfers between devices, swap(): return lax.ppermute(x, 'space', pairs + [(b, a) for a, b in pairs])  16.6 us
    ppermute x10, starting transfers between devices, swap_images(): lax.ppermute(x, ('image', 'space'), pairs + [(b, a) for a, b in pairs])  12.3 us
    ppermute x10, waiting for transfers between devices, swap_images(): lax.ppermute(x, ('image', 'space'), pairs + [(b, a) for a, b in pairs])  9.66 us
    unnamed x14, local copies, waits for them, and re-layouts  6.66 us
  transfers between devices with their start and end apart: 34, of which 8 were waited for; matrix products, arithmetic and copies ran while one was open for 1% of the time, Pallas kernels for 43%

profile of v3, /device:TPU:0, one launch (start us, length us, event | category | flops | bytes accessed | tf_op | source)
XLA Modules:
  0.0 127.9 jit_solution(12177561257346615973)
XLA Ops:
  0.5 1.6 %copy-done = f32[4,256,512]{2,1,0:T(8,128)S(1)} copy-done((f32[4,256,512]{2,1,0:T(8,128)S(1)}, f32[4,256,512]{2,1,0:T(8,128)}, u32[]{:S(2)}) %copy-start) | copy-done | bytes 2097176
  2.1 1.6 %copy-done.2 = f32[1,4,256,512]{3,2,1,0:T(8,128)S(1)} copy-done((f32[1,4,256,512]{3,2,1,0:T(8,128)S(1)}, f32[1,4,256,512]{3,2,1,0:T(8,128)}, u32[]{:S(2)}) %copy-start.2) | copy-done | bytes 2097176
  3.7 2.0 %later.1 = (f32[3,72,512]{2,1,0:T(8,128)}, f32[4,72,512]{2,1,0:T(8,128)}, f32[120,512]{1,0:T(8,128)S(1)}, f32[32,512]{1,0:T(8,128)S(1)}) custom-call(f32[1,4,256,512]{3,2,1,0:T(8,128)S(1)} %copy-done.2, f32[4,256,512]{2,1,0:T(8,128)S(1)} %copy-done), custom_call_target="tpu_custom_call" | custom-call | tf_op jit(solution)/shard_map/later/pallas_call | solution.py:143
  6.3 4.1 %collective-permute-start.18 = (f32[4,72,512]{2,1,0:T(8,128)}, f32[4,72,512]{2,1,0:T(8,128)}, u32[]{:S(2)}, u32[]{:S(2)}) collective-permute-start(f32[4,72,512]{2,1,0:T(8,128)} %get-tuple-element.65.own_ref), channel_id=1, source_target_pairs={{0,8},{16,24},{1,9},{17,25},{2,10},{18,26},{3,11},{19,27},{4,12},{... | collective-permute-start | bytes 1769480 | tf_op jit(solution)/shard_map/ppermute | solution.py:60
  10.4 1.6 %near.1 = f32[4,72,512]{2,1,0:T(8,128)} custom-call(f32[1,4,256,512]{3,2,1,0:T(8,128)S(1)} %copy-done.2), custom_call_target="tpu_custom_call" | custom-call | tf_op jit(solution)/shard_map/near/pallas_call | solution.py:116
  14.4 9.6 %collective-permute-done.18.even_ref = f32[4,72,512]{2,1,0:T(8,128)} collective-permute-done((f32[4,72,512]{2,1,0:T(8,128)}, f32[4,72,512]{2,1,0:T(8,128)}, u32[]{:S(2)}, u32[]{:S(2)}) %collective-permute-start.18) | collective-permute-done | bytes 589856 | tf_op jit(solution)/shard_map/ppermute | solution.py:60
  24.0 1.2 collective-permute-start.4
  26.9 1.3 %pick.1 = (f32[4,72,512]{2,1,0:T(8,128)S(1)}, f32[112,512]{1,0:T(8,128)S(1)}) custom-call(s32[1]{0:T(128)S(6)} %copy.12.sides_ref, f32[4,72,512]{2,1,0:T(8,128)} %get-tuple-element.65.own_ref, f32[4,72,512]{2,1,0:T(8,128)} %collective-permute-done.18.even_ref, f32[4,72,512]{2,1,0:T(8,128)S(1)} %copy-done.6), custom_call_target="tpu_custom_call" | custom-call | bytes 1179648 | tf_op jit(solution)/shard_map/pick/pallas_call | solution.py:183
  28.2 2.3 %collective-permute-done.4.refs_1_ = f32[64,512]{1,0:T(8,128)S(1)} collective-permute-done((f32[64,512]{1,0:T(8,128)S(1)}, f32[64,512]{1,0:T(8,128)S(1)}, u32[]{:S(2)}, u32[]{:S(2)}) %collective-permute-start.4) | collective-permute-done | bytes 131104 | tf_op jit(solution)/shard_map/ppermute | solution.py:48
  31.6 1.6 %copy-done.3 = f32[1,4,256,512]{3,2,1,0:T(8,128)S(1)} copy-done((f32[1,4,256,512]{3,2,1,0:T(8,128)S(1)}, f32[1,4,256,512]{3,2,1,0:T(8,128)}, u32[]{:S(2)}) %copy-start.3) | copy-done | bytes 2097176
  33.9 1.7 %collective-permute-start.10 = (f32[56,512]{1,0:T(8,128)S(1)}, f32[56,512]{1,0:T(8,128)S(1)}, u32[]{:S(2)}, u32[]{:S(2)}) collective-permute-start(f32[56,512]{1,0:T(8,128)S(1)} %get-tuple-element.51), channel_id=1, source_target_pairs={{1,2},{3,4},{5,6},{7,0},{2,1},{4,3},{6,5},{0,7},{9,10},{11,12},{13... | collective-permute-start | bytes 344072 | tf_op jit(solution)/shard_map/ppermute | solution.py:48
  35.6 6.5 %collective-permute-done.10.refs_1_ = f32[56,512]{1,0:T(8,128)S(1)} collective-permute-done((f32[56,512]{1,0:T(8,128)S(1)}, f32[56,512]{1,0:T(8,128)S(1)}, u32[]{:S(2)}, u32[]{:S(2)}) %collective-permute-start.10) | collective-permute-done | bytes 114720 | tf_op jit(solution)/shard_map/ppermute | solution.py:48
  42.7 2.7 %collective-permute-start.14 = (f32[48,512]{1,0:T(8,128)S(1)}, f32[48,512]{1,0:T(8,128)S(1)}, u32[]{:S(2)}, u32[]{:S(2)}) collective-permute-start(f32[48,512]{1,0:T(8,128)S(1)} %get-tuple-element.59), channel_id=1, source_target_pairs={{1,2},{3,4},{5,6},{7,0},{2,1},{4,3},{6,5},{0,7},{9,10},{11,12},{13... | collective-permute-start | bytes 294920 | tf_op jit(solution)/shard_map/ppermute | solution.py:48
  45.4 2.9 %shard_map.47 = (f32[7,80,512]{2,1,0:T(8,128)S(1)}, f32[64,512]{1,0:T(8,128)S(1)}) custom-call(f32[4,256,512]{2,1,0:T(8,128)S(1)} %copy-done.1, f32[120,512]{1,0:T(8,128)S(1)} %collective-permute-done.3.refs_1_, f32[4,256,512]{2,1,0:T(8,128)} %collective-permute-done.1.refs_2_.refs_1_, f32[4,256,512]{2,1,0:T(8,128)} %collective-permute-done.2.refs_3_, ...), custom_call_target="tpu_custom_call" | custom-call | flops 4587520 | bytes 917504 | tf_op jit(solution)/shard_map/pallas_call | solution.py:364
  48.4 2.8 %shard_map.48 = (f32[7,72,512]{2,1,0:T(8,128)S(1)}, f32[56,512]{1,0:T(8,128)S(1)}) custom-call(f32[4,256,512]{2,1,0:T(8,128)S(1)} %copy-done.1, f32[120,512]{1,0:T(8,128)S(1)} %collective-permute-done.3.refs_1_, f32[4,256,512]{2,1,0:T(8,128)} %collective-permute-done.1.refs_2_.refs_1_, f32[4,256,512]{2,1,0:T(8,128)} %collective-permute-done.2.refs_3_, ...), custom_call_target="tpu_custom_call" | custom-call | flops 4014080 | bytes 802816 | tf_op jit(solution)/shard_map/pallas_call | solution.py:364
  51.2 2.7 %collective-permute-start.8 = (f32[56,512]{1,0:T(8,128)S(1)}, f32[56,512]{1,0:T(8,128)S(1)}, u32[]{:S(2)}, u32[]{:S(2)}) collective-permute-start(f32[56,512]{1,0:T(8,128)S(1)} %get-tuple-element.49), channel_id=1, source_target_pairs={{1,2},{3,4},{5,6},{7,0},{2,1},{4,3},{6,5},{0,7},{9,10},{11,12},{13... | collective-permute-start | bytes 344072 | tf_op jit(solution)/shard_map/ppermute | solution.py:48
  54.4 1.5 %collective-permute-done.9.refs_1_ = f32[64,512]{1,0:T(8,128)S(1)} collective-permute-done((f32[64,512]{1,0:T(8,128)S(1)}, f32[64,512]{1,0:T(8,128)S(1)}, u32[]{:S(2)}, u32[]{:S(2)}) %collective-permute-start.9) | collective-permute-done | bytes 131104 | tf_op jit(solution)/shard_map/ppermute | solution.py:48
  55.9 1.2 collective-permute-start.25
  57.0 2.2 %shard_map.51 = (f32[6,80,512]{2,1,0:T(8,128)S(1)}, f32[64,512]{1,0:T(8,128)S(1)}) custom-call(f32[4,256,512]{2,1,0:T(8,128)S(1)} %copy-done.1, f32[64,512]{1,0:T(8,128)S(1)} %collective-permute-done.9.refs_1_, f32[4,256,512]{2,1,0:T(8,128)} %collective-permute-done.1.refs_2_.refs_1_, f32[7,80,512]{2,1,0:T(8,128)S(1)} %get-tuple-element.45.refs_5_.refs_3_, ...), custom_call_target="tpu_custom_call" | custom-call | flops 3932160 | bytes 786432 | tf_op jit(solution)/shard_map/pallas_call | solution.py:364
  60.8 2.6 %shard_map.49 = (f32[7,48,512]{2,1,0:T(8,128)S(1)}, f32[32,512]{1,0:T(8,128)S(1)}) custom-call(f32[4,256,512]{2,1,0:T(8,128)S(1)} %copy-done.1, f32[32,512]{1,0:T(8,128)S(1)} %collective-permute-done.refs_1_, f32[4,256,512]{2,1,0:T(8,128)} %collective-permute-done.1.refs_2_.refs_1_, f32[4,256,512]{2,1,0:T(8,128)} %collective-permute-done.2.refs_3_, ...), custom_call_target="tpu_custom_call" | custom-call | flops 2293760 | bytes 458752 | tf_op jit(solution)/shard_map/pallas_call | solution.py:364
  63.4 2.4 %shard_map.59 = f32[120,512]{1,0:T(8,128)S(1)} custom-call(f32[4,256,512]{2,1,0:T(8,128)S(1)} %copy-done.1, f32[112,512]{1,0:T(8,128)S(1)} %collective-permute-done.20.refs_1_, f32[4,256,512]{2,1,0:T(8,128)} %collective-permute-done.1.refs_2_.refs_1_, f32[4,256,512]{2,1,0:T(8,128)} %collective-permute-done.2.refs_3_, f32[4,256,512]{2,1,0:T(8,128)S(1)} %bitcast.8, ...), custom_call_target="tpu_custom_call" | custom-call | flops 8028160 | bytes 1605632 | tf_op jit(solution)/shard_map/pallas_call | solution.py:364
  65.8 1.7 %collective-permute-start.22 = (f32[120,512]{1,0:T(8,128)S(1)}, f32[120,512]{1,0:T(8,128)S(1)}, u32[]{:S(2)}, u32[]{:S(2)}) collective-permute-start(f32[120,512]{1,0:T(8,128)S(1)} %shard_map.59), channel_id=1, source_target_pairs={{1,2},{3,4},{5,6},{7,0},{2,1},{4,3},{6,5},{0,7},{9,10},{11,12},{13... | collective-permute-start | bytes 737288 | tf_op jit(solution)/shard_map/ppermute | solution.py:48
  67.5 2.1 %shard_map.52 = (f32[6,72,512]{2,1,0:T(8,128)S(1)}, f32[56,512]{1,0:T(8,128)S(1)}) custom-call(f32[4,256,512]{2,1,0:T(8,128)S(1)} %copy-done.1, f32[56,512]{1,0:T(8,128)S(1)} %collective-permute-done.8.refs_1_, f32[4,256,512]{2,1,0:T(8,128)} %collective-permute-done.1.refs_2_.refs_1_, f32[7,72,512]{2,1,0:T(8,128)S(1)} %get-tuple-element.46.refs_5_.refs_3_, ...), custom_call_target="tpu_custom_call" | custom-call | flops 3440640 | bytes 688128 | tf_op jit(solution)/shard_map/pallas_call | solution.py:364
  69.6 1.1 collective-permute-start.12
  71.0 3.2 %collective-permute-start.28 = (f32[4,40,512]{2,1,0:T(8,128)S(1)}, f32[4,40,512]{2,1,0:T(8,128)S(1)}, u32[]{:S(2)}, u32[]{:S(2)}) collective-permute-start(f32[4,40,512]{2,1,0:T(8,128)S(1)} %shard_map.65.refs_0_), channel_id=1, source_target_pairs={{0,8},{16,24},{1,9},{17,25},{2,10},{18,26},{3,11},{19,27},{4,12},{... | collective-permute-start | bytes 983048 | tf_op jit(solution)/shard_map/ppermute | solution.py:60
  74.3 2.1 %shard_map.55 = (f32[5,80,512]{2,1,0:T(8,128)S(1)}, f32[64,512]{1,0:T(8,128)S(1)}) custom-call(f32[4,256,512]{2,1,0:T(8,128)S(1)} %copy-done.1, f32[64,512]{1,0:T(8,128)S(1)} %collective-permute-done.13.refs_1_, f32[4,256,512]{2,1,0:T(8,128)} %collective-permute-done.1.refs_2_.refs_1_, f32[6,80,512]{2,1,0:T(8,128)S(1)} %get-tuple-element.53.refs_4_.refs_3_, ...), custom_call_target="tpu_custom_call" | custom-call | flops 3276800 | bytes 655360 | tf_op jit(solution)/shard_map/pallas_call | solution.py:364
  76.4 2.0 %shard_map.56 = (f32[5,72,512]{2,1,0:T(8,128)S(1)}, f32[56,512]{1,0:T(8,128)S(1)}) custom-call(f32[4,256,512]{2,1,0:T(8,128)S(1)} %copy-done.1, f32[56,512]{1,0:T(8,128)S(1)} %collective-permute-done.12.refs_1_, f32[4,256,512]{2,1,0:T(8,128)} %collective-permute-done.1.refs_2_.refs_1_, f32[6,72,512]{2,1,0:T(8,128)S(1)} %get-tuple-element.54.refs_4_.refs_3_, ...), custom_call_target="tpu_custom_call" | custom-call | flops 2867200 | bytes 573440 | tf_op jit(solution)/shard_map/pallas_call | solution.py:364
  79.4 1.8 %collective-permute-start.7 = (f32[32,512]{1,0:T(8,128)S(1)}, f32[32,512]{1,0:T(8,128)S(1)}, u32[]{:S(2)}, u32[]{:S(2)}) collective-permute-start(f32[32,512]{1,0:T(8,128)S(1)} %get-tuple-element.47), channel_id=1, source_target_pairs={{1,2},{3,4},{5,6},{7,0},{2,1},{4,3},{6,5},{0,7},{9,10},{11,12},{13... | collective-permute-start | bytes 196616 | tf_op jit(solution)/shard_map/ppermute | solution.py:48
  81.1 2.8 %collective-permute-done.27.refs_1_ = f32[56,512]{1,0:T(8,128)S(1)} collective-permute-done((f32[56,512]{1,0:T(8,128)S(1)}, f32[56,512]{1,0:T(8,128)S(1)}, u32[]{:S(2)}, u32[]{:S(2)}) %collective-permute-start.27) | collective-permute-done | bytes 114720 | tf_op jit(solution)/shard_map/ppermute | solution.py:48
  84.9 1.9 %shard_map.67.refs_2_ = f32[4,56,512]{2,1,0:T(8,128)S(1)} custom-call(f32[4,256,512]{2,1,0:T(8,128)S(1)} %copy-done.1, f32[56,512]{1,0:T(8,128)S(1)} %collective-permute-done.27.refs_1_, f32[4,256,512]{2,1,0:T(8,128)} %collective-permute-done.1.refs_2_.refs_1_, f32[5,72,512]{2,1,0:T(8,128)S(1)} %get-tuple-element.62.refs_4_.refs_3_), custom_call_target="tpu_custom_call" | custom-call | flops 2293760 | bytes 458752 | tf_op jit(solution)/shard_map/pallas_call | solution.py:364
  86.9 2.2 %collective-permute-start.30 = (f32[4,56,512]{2,1,0:T(8,128)S(1)}, f32[4,56,512]{2,1,0:T(8,128)S(1)}, u32[]{:S(2)}, u32[]{:S(2)}) collective-permute-start(f32[4,56,512]{2,1,0:T(8,128)S(1)} %shard_map.67.refs_2_), channel_id=1, source_target_pairs={{0,8},{16,24},{1,9},{17,25},{2,10},{18,26},{3,11},{19,27},{4,12},{... | collective-permute-start | bytes 1376264 | tf_op jit(solution)/shard_map/ppermute | solution.py:60
  89.1 3.4 %shard_map.60 = (f32[7,56,512]{2,1,0:T(8,128)S(1)}, f32[7,72,512]{2,1,0:T(8,128)S(1)}) custom-call(f32[4,256,512]{2,1,0:T(8,128)S(1)} %copy-done.1, f32[112,512]{1,0:T(8,128)S(1)} %collective-permute-done.20.refs_1_, f32[4,256,512]{2,1,0:T(8,128)} %collective-permute-done.1.refs_2_.refs_1_, f32[4,256,512]{2,1,0:T(8,128)} %collective-permute-done.2.refs_3_, ...), custom_call_target="tpu_custom_call" | custom-call | flops 8028160 | bytes 1605632 | tf_op jit(solution)/shard_map/pallas_call | solution.py:364
  92.5 1.9 %shard_map.53 = (f32[6,48,512]{2,1,0:T(8,128)S(1)}, f32[32,512]{1,0:T(8,128)S(1)}) custom-call(f32[4,256,512]{2,1,0:T(8,128)S(1)} %copy-done.1, f32[32,512]{1,0:T(8,128)S(1)} %collective-permute-done.7.refs_1_, f32[4,256,512]{2,1,0:T(8,128)} %collective-permute-done.1.refs_2_.refs_1_, f32[7,48,512]{2,1,0:T(8,128)S(1)} %get-tuple-element.48.refs_3_.refs_5_, ...), custom_call_target="tpu_custom_call" | custom-call | flops 1966080 | bytes 393216 | tf_op jit(solution)/shard_map/pallas_call | solution.py:364
  94.4 1.8 %shard_map.61 = f32[128,512]{1,0:T(8,128)S(1)} custom-call(f32[4,256,512]{2,1,0:T(8,128)S(1)} %copy-done.1, f32[120,512]{1,0:T(8,128)S(1)} %collective-permute-done.22.refs_1_, f32[4,256,512]{2,1,0:T(8,128)} %collective-permute-done.1.refs_2_.refs_1_, f32[7,56,512]{2,1,0:T(8,128)S(1)} %get-tuple-element.68.refs_3_, ...), custom_call_target="tpu_custom_call" | custom-call | flops 7372800 | bytes 1474560 | tf_op jit(solution)/shard_map/pallas_call | solution.py:364
  96.2 1.1 collective-permute-start.11
  97.3 1.6 %collective-permute-start.23 = (f32[128,512]{1,0:T(8,128)S(1)}, f32[128,512]{1,0:T(8,128)S(1)}, u32[]{:S(2)}, u32[]{:S(2)}) collective-permute-start(f32[128,512]{1,0:T(8,128)S(1)} %shard_map.61), channel_id=1, source_target_pairs={{1,2},{3,4},{5,6},{7,0},{2,1},{4,3},{6,5},{0,7},{9,10},{11,12},{13... | collective-permute-start | bytes 786440 | tf_op jit(solution)/shard_map/ppermute | solution.py:48
  98.9 2.0 %shard_map.66.refs_1_ = f32[4,64,512]{2,1,0:T(8,128)S(1)} custom-call(f32[4,256,512]{2,1,0:T(8,128)S(1)} %copy-done.1, f32[64,512]{1,0:T(8,128)S(1)} %collective-permute-done.26.refs_1_, f32[4,256,512]{2,1,0:T(8,128)} %collective-permute-done.1.refs_2_.refs_1_, f32[5,80,512]{2,1,0:T(8,128)S(1)} %get-tuple-element.61.refs_4_.refs_3_), custom_call_target="tpu_custom_call" | custom-call | flops 2621440 | bytes 524288 | tf_op jit(solution)/shard_map/pallas_call | solution.py:364
  101.6 1.9 %shard_map.57 = (f32[5,48,512]{2,1,0:T(8,128)S(1)}, f32[32,512]{1,0:T(8,128)S(1)}) custom-call(f32[4,256,512]{2,1,0:T(8,128)S(1)} %copy-done.1, f32[32,512]{1,0:T(8,128)S(1)} %collective-permute-done.11.refs_1_, f32[4,256,512]{2,1,0:T(8,128)} %collective-permute-done.1.refs_2_.refs_1_, f32[6,48,512]{2,1,0:T(8,128)S(1)} %get-tuple-element.56.refs_3_.refs_4_, ...), custom_call_target="tpu_custom_call" | custom-call | flops 1638400 | bytes 327680 | tf_op jit(solution)/shard_map/pallas_call | solution.py:364
  103.5 2.3 %collective-permute-done.23.refs_1_ = f32[128,512]{1,0:T(8,128)S(1)} collective-permute-done((f32[128,512]{1,0:T(8,128)S(1)}, f32[128,512]{1,0:T(8,128)S(1)}, u32[]{:S(2)}, u32[]{:S(2)}) %collective-permute-start.23) | collective-permute-done | bytes 262176 | tf_op jit(solution)/shard_map/ppermute | solution.py:48
  105.8 2.6 %shard_map.62 = (f32[6,64,512]{2,1,0:T(8,128)S(1)}, f32[6,72,512]{2,1,0:T(8,128)S(1)}) custom-call(f32[4,256,512]{2,1,0:T(8,128)S(1)} %copy-done.1, f32[120,512]{1,0:T(8,128)S(1)} %collective-permute-done.22.refs_1_, f32[4,256,512]{2,1,0:T(8,128)} %collective-permute-done.1.refs_2_.refs_1_, f32[7,56,512]{2,1,0:T(8,128)S(1)} %get-tuple-element.68.refs_3_, ...), custom_call_target="tpu_custom_call" | custom-call | flops 7372800 | bytes 1474560 | tf_op jit(solution)/shard_map/pallas_call | solution.py:364
  108.5 2.0 %shard_map.63 = f32[128,512]{1,0:T(8,128)S(1)} custom-call(f32[4,256,512]{2,1,0:T(8,128)S(1)} %copy-done.1, f32[128,512]{1,0:T(8,128)S(1)} %collective-permute-done.23.refs_1_, f32[4,256,512]{2,1,0:T(8,128)} %collective-permute-done.1.refs_2_.refs_1_, f32[6,64,512]{2,1,0:T(8,128)S(1)} %get-tuple-element.70.refs_3_, ...), custom_call_target="tpu_custom_call" | custom-call | flops 6553600 | bytes 1310720 | tf_op jit(solution)/shard_map/pallas_call | solution.py:364
  110.5 2.6 %collective-permute-start.24 = (f32[128,512]{1,0:T(8,128)S(1)}, f32[128,512]{1,0:T(8,128)S(1)}, u32[]{:S(2)}, u32[]{:S(2)}) collective-permute-start(f32[128,512]{1,0:T(8,128)S(1)} %shard_map.63), channel_id=1, source_target_pairs={{1,2},{3,4},{5,6},{7,0},{2,1},{4,3},{6,5},{0,7},{9,10},{11,12},{13... | collective-permute-start | bytes 786440 | tf_op jit(solution)/shard_map/ppermute | solution.py:48
  113.1 1.8 %shard_map.58.refs_0_ = f32[4,32,512]{2,1,0:T(8,128)S(1)} custom-call(f32[4,256,512]{2,1,0:T(8,128)S(1)} %copy-done.1, f32[32,512]{1,0:T(8,128)S(1)} %collective-permute-done.15.refs_1_, f32[4,256,512]{2,1,0:T(8,128)} %collective-permute-done.1.refs_2_.refs_1_, f32[5,48,512]{2,1,0:T(8,128)S(1)} %get-tuple-element.64.refs_3_.refs_4_), custom_call_target="tpu_custom_call" | custom-call | flops 1310720 | bytes 262144 | tf_op jit(solution)/shard_map/pallas_call | solution.py:364
  115.0 1.9 %collective-permute-start.16 = (f32[4,32,512]{2,1,0:T(8,128)S(1)}, f32[4,32,512]{2,1,0:T(8,128)S(1)}, u32[]{:S(2)}, u32[]{:S(2)}) collective-permute-start(f32[4,32,512]{2,1,0:T(8,128)S(1)} %shard_map.58.refs_0_), channel_id=1, source_target_pairs={{0,8},{16,24},{1,9},{17,25},{2,10},{18,26},{3,11},{19,27},{4,12},{... | collective-permute-start | bytes 786440 | tf_op jit(solution)/shard_map/ppermute | solution.py:60
  117.6 2.5 %shard_map.64 = (f32[5,72,512]{2,1,0:T(8,128)S(1)}, f32[5,72,512]{2,1,0:T(8,128)S(1)}) custom-call(f32[4,256,512]{2,1,0:T(8,128)S(1)} %copy-done.1, f32[128,512]{1,0:T(8,128)S(1)} %collective-permute-done.23.refs_1_, f32[4,256,512]{2,1,0:T(8,128)} %collective-permute-done.1.refs_2_.refs_1_, f32[6,64,512]{2,1,0:T(8,128)S(1)} %get-tuple-element.70.refs_3_, ...), custom_call_target="tpu_custom_call" | custom-call | flops 6553600 | bytes 1310720 | tf_op jit(solution)/shard_map/pallas_call | solution.py:364
  120.1 3.0 %shard_map.68.refs_9_ = f32[1,4,256,512]{3,2,1,0:T(8,128)} custom-call(f32[4,256,512]{2,1,0:T(8,128)S(1)} %copy-done.1, f32[4,256,512]{2,1,0:T(8,128)} %collective-permute-done.1.refs_2_.refs_1_, f32[5,72,512]{2,1,0:T(8,128)S(1)} %get-tuple-element.72.refs_2_.refs_3_, f32[5,72,512]{2,1,0:T(8,128)S(1)} %get-tuple-element.73.refs_3_.refs_4_, ...), custom_call_target="tpu_custom_call" | custom-call | flops 5570560 | bytes 1114112 | tf_op jit(solution)/shard_map/pallas_call | solution.py:364
  123.1 1.2 shard_map.69.refs_6_
  124.4 2.5 %shard_map.70.refs_3_ = f32[1,4,256,512]{3,2,1,0:T(8,128)} custom-call(f32[4,256,512]{2,1,0:T(8,128)S(1)} %copy-done.1, f32[128,512]{1,0:T(8,128)S(1)} %collective-permute-done.24.refs_1_, f32[4,256,512]{2,1,0:T(8,128)} %collective-permute-done.1.refs_2_.refs_1_, ...), custom_call_target="tpu_custom_call", output_to_operand_aliasing={{}: (6, {})} | custom-call | flops 5570560 | bytes 1114112 | tf_op jit(solution)/shard_map/pallas_call | solution.py:364
  (64 shorter events, 12.7 us)
Async XLA Ops:
  0.0 45.4 %collective-permute-start.2 = (f32[4,256,512]{2,1,0:T(8,128)}, f32[4,256,512]{2,1,0:T(8,128)}, u32[]{:S(2)}, u32[]{:S(2)}) collective-permute-start(f32[4,256,512]{2,1,0:T(8,128)} %bitcast.3), channel_id=1, source_target_pairs={{0,1},{2,3},{4,5},{6,7},{1,0},{3,2},{5,4},{7,6},{8,9},{10,11},{12,... | collective-permute-start | bytes 6291464 | tf_op jit(solution)/shard_map/ppermute | solution.py:48
  0.5 44.9 %collective-permute-start.1 = (f32[4,256,512]{2,1,0:T(8,128)}, f32[4,256,512]{2,1,0:T(8,128)}, u32[]{:S(2)}, u32[]{:S(2)}) collective-permute-start(f32[4,256,512]{2,1,0:T(8,128)} %refs_0_.47), channel_id=1, source_target_pairs={{0,1},{2,3},{4,5},{6,7},{1,0},{3,2},{5,4},{7,6},{8,9},{10,11},{12,... | collective-permute-start | bytes 6291464 | tf_op jit(solution)/shard_map/ppermute | solution.py:48
  0.5 1.6 %copy-start = (f32[4,256,512]{2,1,0:T(8,128)S(1)}, f32[4,256,512]{2,1,0:T(8,128)}, u32[]{:S(2)}) copy-start(f32[4,256,512]{2,1,0:T(8,128)} %refs_0_.47) | copy-start | bytes 6291460
  2.1 1.6 %copy-start.2 = (f32[1,4,256,512]{3,2,1,0:T(8,128)S(1)}, f32[1,4,256,512]{3,2,1,0:T(8,128)}, u32[]{:S(2)}) copy-start(f32[1,4,256,512]{3,2,1,0:T(8,128)} %field_ref.3) | copy-start | bytes 6291460
  5.7 25.9 %copy-start.1 = (f32[4,256,512]{2,1,0:T(8,128)S(1)}, f32[4,256,512]{2,1,0:T(8,128)}, u32[]{:S(2)}) copy-start(f32[4,256,512]{2,1,0:T(8,128)} %refs_0_.47) | copy-start | bytes 6291460
  5.7 6.4 %collective-permute-start.19 = (f32[4,72,512]{2,1,0:T(8,128)}, f32[4,72,512]{2,1,0:T(8,128)S(1)}, u32[]{:S(2)}, u32[]{:S(2)}) collective-permute-start(f32[4,72,512]{2,1,0:T(8,128)} %get-tuple-element.65.own_ref), channel_id=1, source_target_pairs={{8,16},{9,17},{10,18},{11,19},{12,20},{13,21},{14,22},{15,23},{0,1... | collective-permute-start | bytes 1769480 | tf_op jit(solution)/shard_map/ppermute | solution.py:60
  6.3 17.7 %collective-permute-start.18 = (f32[4,72,512]{2,1,0:T(8,128)}, f32[4,72,512]{2,1,0:T(8,128)}, u32[]{:S(2)}, u32[]{:S(2)}) collective-permute-start(f32[4,72,512]{2,1,0:T(8,128)} %get-tuple-element.65.own_ref), channel_id=1, source_target_pairs={{0,8},{16,24},{1,9},{17,25},{2,10},{18,26},{3,11},{19,27},{4,12},{... | collective-permute-start | bytes 1769480 | tf_op jit(solution)/shard_map/ppermute | solution.py:60
  12.0 19.6 %collective-permute-start.6 = (f32[4,72,512]{2,1,0:T(8,128)}, f32[4,72,512]{2,1,0:T(8,128)S(1)}, u32[]{:S(2)}, u32[]{:S(2)}) collective-permute-start(f32[4,72,512]{2,1,0:T(8,128)} %near.1), channel_id=1, source_target_pairs={{0,1},{2,3},{4,5},{6,7},{1,0},{3,2},{5,4},{7,6},{8,9},{10,11},{12,... | collective-permute-start | bytes 1769480 | tf_op jit(solution)/shard_map/ppermute | solution.py:48
  12.1 0.8 copy-start.5
  13.0 17.6 %collective-permute-start.5 = (f32[3,72,512]{2,1,0:T(8,128)}, f32[3,72,512]{2,1,0:T(8,128)S(1)}, u32[]{:S(2)}, u32[]{:S(2)}) collective-permute-start(f32[3,72,512]{2,1,0:T(8,128)} %get-tuple-element.43), channel_id=1, source_target_pairs={{0,1},{2,3},{4,5},{6,7},{1,0},{3,2},{5,4},{7,6},{8,9},{10,11},{12,... | collective-permute-start | bytes 1327112 | tf_op jit(solution)/shard_map/ppermute | solution.py:48
  24.0 6.6 %collective-permute-start.4 = (f32[64,512]{1,0:T(8,128)S(1)}, f32[64,512]{1,0:T(8,128)S(1)}, u32[]{:S(2)}, u32[]{:S(2)}) collective-permute-start(f32[64,512]{1,0:T(8,128)S(1)} %dynamic-slice_bitcast_fusion), channel_id=1, source_target_pairs={{1,2},{3,4},{5,6},{7,0},{2,1},{4,3},{6,5},{0,7},{9,10},{11,12},{13... | collective-permute-start | bytes 393224 | tf_op jit(solution)/shard_map/ppermute | solution.py:48
  25.8 1.1 copy-start.6
  30.6 32.8 %collective-permute-start.21 = (f32[4,72,512]{2,1,0:T(8,128)S(1)}, f32[4,72,512]{2,1,0:T(8,128)S(1)}, u32[]{:S(2)}, u32[]{:S(2)}) collective-permute-start(f32[4,72,512]{2,1,0:T(8,128)S(1)} %get-tuple-element.67.refs_6_), channel_id=1, source_target_pairs={{0,1},{2,3},{4,5},{6,7},{1,0},{3,2},{5,4},{7,6},{8,9},{10,11},{12,... | collective-permute-start | bytes 1769480 | tf_op jit(solution)/shard_map/ppermute | solution.py:48
  30.6 12.1 %collective-permute-start.3 = (f32[120,512]{1,0:T(8,128)S(1)}, f32[120,512]{1,0:T(8,128)S(1)}, u32[]{:S(2)}, u32[]{:S(2)}) collective-permute-start(f32[120,512]{1,0:T(8,128)S(1)} %get-tuple-element.42), channel_id=1, source_target_pairs={{1,2},{3,4},{5,6},{7,0},{2,1},{4,3},{6,5},{0,7},{9,10},{11,12},{13... | collective-permute-start | bytes 737288 | tf_op jit(solution)/shard_map/ppermute | solution.py:48
  31.6 1.6 %copy-start.3 = (f32[1,4,256,512]{3,2,1,0:T(8,128)S(1)}, f32[1,4,256,512]{3,2,1,0:T(8,128)}, u32[]{:S(2)}) copy-start(f32[1,4,256,512]{3,2,1,0:T(8,128)} %field_ref.3) | copy-start | bytes 6291460
  33.9 11.5 %copy-start.4 = (f32[1,4,256,512]{3,2,1,0:T(8,128)S(1)}, f32[1,4,256,512]{3,2,1,0:T(8,128)}, u32[]{:S(2)}) copy-start(f32[1,4,256,512]{3,2,1,0:T(8,128)} %field_ref.3) | copy-start | bytes 6291460
  33.9 8.2 %collective-permute-start.10 = (f32[56,512]{1,0:T(8,128)S(1)}, f32[56,512]{1,0:T(8,128)S(1)}, u32[]{:S(2)}, u32[]{:S(2)}) collective-permute-start(f32[56,512]{1,0:T(8,128)S(1)} %get-tuple-element.51), channel_id=1, source_target_pairs={{1,2},{3,4},{5,6},{7,0},{2,1},{4,3},{6,5},{0,7},{9,10},{11,12},{13... | collective-permute-start | bytes 344072 | tf_op jit(solution)/shard_map/ppermute | solution.py:48
  42.1 21.2 %collective-permute-start.20 = (f32[112,512]{1,0:T(8,128)S(1)}, f32[112,512]{1,0:T(8,128)S(1)}, u32[]{:S(2)}, u32[]{:S(2)}) collective-permute-start(f32[112,512]{1,0:T(8,128)S(1)} %get-tuple-element.66), channel_id=1, source_target_pairs={{1,2},{3,4},{5,6},{7,0},{2,1},{4,3},{6,5},{0,7},{9,10},{11,12},{13... | collective-permute-start | bytes 688136 | tf_op jit(solution)/shard_map/ppermute | solution.py:48
  42.7 11.2 %collective-permute-start.14 = (f32[48,512]{1,0:T(8,128)S(1)}, f32[48,512]{1,0:T(8,128)S(1)}, u32[]{:S(2)}, u32[]{:S(2)}) collective-permute-start(f32[48,512]{1,0:T(8,128)S(1)} %get-tuple-element.59), channel_id=1, source_target_pairs={{1,2},{3,4},{5,6},{7,0},{2,1},{4,3},{6,5},{0,7},{9,10},{11,12},{13... | collective-permute-start | bytes 294920 | tf_op jit(solution)/shard_map/ppermute | solution.py:48
  48.3 7.6 %collective-permute-start.9 = (f32[64,512]{1,0:T(8,128)S(1)}, f32[64,512]{1,0:T(8,128)S(1)}, u32[]{:S(2)}, u32[]{:S(2)}) collective-permute-start(f32[64,512]{1,0:T(8,128)S(1)} %get-tuple-element.50), channel_id=1, source_target_pairs={{1,2},{3,4},{5,6},{7,0},{2,1},{4,3},{6,5},{0,7},{9,10},{11,12},{13... | collective-permute-start | bytes 393224 | tf_op jit(solution)/shard_map/ppermute | solution.py:48
  51.2 16.2 %collective-permute-start.8 = (f32[56,512]{1,0:T(8,128)S(1)}, f32[56,512]{1,0:T(8,128)S(1)}, u32[]{:S(2)}, u32[]{:S(2)}) collective-permute-start(f32[56,512]{1,0:T(8,128)S(1)} %get-tuple-element.49), channel_id=1, source_target_pairs={{1,2},{3,4},{5,6},{7,0},{2,1},{4,3},{6,5},{0,7},{9,10},{11,12},{13... | collective-permute-start | bytes 344072 | tf_op jit(solution)/shard_map/ppermute | solution.py:48
  53.9 5.8 %collective-permute-start = (f32[32,512]{1,0:T(8,128)S(1)}, f32[32,512]{1,0:T(8,128)S(1)}, u32[]{:S(2)}, u32[]{:S(2)}) collective-permute-start(f32[32,512]{1,0:T(8,128)S(1)} %get-tuple-element.41), channel_id=1, source_target_pairs={{1,2},{3,4},{5,6},{7,0},{2,1},{4,3},{6,5},{0,7},{9,10},{11,12},{13... | collective-permute-start | bytes 196616 | tf_op jit(solution)/shard_map/ppermute | solution.py:48
  55.9 14.8 %collective-permute-start.25 = (f32[40,512]{1,0:T(8,128)S(1)}, f32[40,512]{1,0:T(8,128)S(1)}, u32[]{:S(2)}, u32[]{:S(2)}) collective-permute-start(f32[40,512]{1,0:T(8,128)S(1)} %get-tuple-element.74), channel_id=1, source_target_pairs={{1,2},{3,4},{5,6},{7,0},{2,1},{4,3},{6,5},{0,7},{9,10},{11,12},{13... | collective-permute-start | bytes 245768 | tf_op jit(solution)/shard_map/ppermute | solution.py:48
  59.7 14.6 %collective-permute-start.13 = (f32[64,512]{1,0:T(8,128)S(1)}, f32[64,512]{1,0:T(8,128)S(1)}, u32[]{:S(2)}, u32[]{:S(2)}) collective-permute-start(f32[64,512]{1,0:T(8,128)S(1)} %get-tuple-element.58), channel_id=1, source_target_pairs={{1,2},{3,4},{5,6},{7,0},{2,1},{4,3},{6,5},{0,7},{9,10},{11,12},{13... | collective-permute-start | bytes 393224 | tf_op jit(solution)/shard_map/ppermute | solution.py:48
  65.8 21.1 %collective-permute-start.22 = (f32[120,512]{1,0:T(8,128)S(1)}, f32[120,512]{1,0:T(8,128)S(1)}, u32[]{:S(2)}, u32[]{:S(2)}) collective-permute-start(f32[120,512]{1,0:T(8,128)S(1)} %shard_map.59), channel_id=1, source_target_pairs={{1,2},{3,4},{5,6},{7,0},{2,1},{4,3},{6,5},{0,7},{9,10},{11,12},{13... | collective-permute-start | bytes 737288 | tf_op jit(solution)/shard_map/ppermute | solution.py:48
  69.6 6.8 %collective-permute-start.12 = (f32[56,512]{1,0:T(8,128)S(1)}, f32[56,512]{1,0:T(8,128)S(1)}, u32[]{:S(2)}, u32[]{:S(2)}) collective-permute-start(f32[56,512]{1,0:T(8,128)S(1)} %get-tuple-element.57), channel_id=1, source_target_pairs={{1,2},{3,4},{5,6},{7,0},{2,1},{4,3},{6,5},{0,7},{9,10},{11,12},{13... | collective-permute-start | bytes 344072 | tf_op jit(solution)/shard_map/ppermute | solution.py:48
  71.0 25.3 %collective-permute-start.31 = (f32[4,40,512]{2,1,0:T(8,128)S(1)}, f32[4,40,512]{2,1,0:T(8,128)S(1)}, u32[]{:S(2)}, u32[]{:S(2)}) collective-permute-start(f32[4,40,512]{2,1,0:T(8,128)S(1)} %shard_map.65.refs_0_), channel_id=1, source_target_pairs={{8,16},{9,17},{10,18},{11,19},{12,20},{13,21},{14,22},{15,23},{0,1... | collective-permute-start | bytes 983048 | tf_op jit(solution)/shard_map/ppermute | solution.py:60
  71.0 29.9 %collective-permute-start.28 = (f32[4,40,512]{2,1,0:T(8,128)S(1)}, f32[4,40,512]{2,1,0:T(8,128)S(1)}, u32[]{:S(2)}, u32[]{:S(2)}) collective-permute-start(f32[4,40,512]{2,1,0:T(8,128)S(1)} %shard_map.65.refs_0_), channel_id=1, source_target_pairs={{0,8},{16,24},{1,9},{17,25},{2,10},{18,26},{3,11},{19,27},{4,12},{... | collective-permute-start | bytes 983048 | tf_op jit(solution)/shard_map/ppermute | solution.py:60
  78.4 5.5 %collective-permute-start.27 = (f32[56,512]{1,0:T(8,128)S(1)}, f32[56,512]{1,0:T(8,128)S(1)}, u32[]{:S(2)}, u32[]{:S(2)}) collective-permute-start(f32[56,512]{1,0:T(8,128)S(1)} %get-tuple-element.76), channel_id=1, source_target_pairs={{1,2},{3,4},{5,6},{7,0},{2,1},{4,3},{6,5},{0,7},{9,10},{11,12},{13... | collective-permute-start | bytes 344072 | tf_op jit(solution)/shard_map/ppermute | solution.py:48
  79.4 7.5 %collective-permute-start.7 = (f32[32,512]{1,0:T(8,128)S(1)}, f32[32,512]{1,0:T(8,128)S(1)}, u32[]{:S(2)}, u32[]{:S(2)}) collective-permute-start(f32[32,512]{1,0:T(8,128)S(1)} %get-tuple-element.47), channel_id=1, source_target_pairs={{1,2},{3,4},{5,6},{7,0},{2,1},{4,3},{6,5},{0,7},{9,10},{11,12},{13... | collective-permute-start | bytes 196616 | tf_op jit(solution)/shard_map/ppermute | solution.py:48
  83.9 13.4 %collective-permute-start.26 = (f32[64,512]{1,0:T(8,128)S(1)}, f32[64,512]{1,0:T(8,128)S(1)}, u32[]{:S(2)}, u32[]{:S(2)}) collective-permute-start(f32[64,512]{1,0:T(8,128)S(1)} %get-tuple-element.75), channel_id=1, source_target_pairs={{1,2},{3,4},{5,6},{7,0},{2,1},{4,3},{6,5},{0,7},{9,10},{11,12},{13... | collective-permute-start | bytes 393224 | tf_op jit(solution)/shard_map/ppermute | solution.py:48
  86.8 28.1 %collective-permute-start.33 = (f32[4,56,512]{2,1,0:T(8,128)S(1)}, f32[4,56,512]{2,1,0:T(8,128)S(1)}, u32[]{:S(2)}, u32[]{:S(2)}) collective-permute-start(f32[4,56,512]{2,1,0:T(8,128)S(1)} %shard_map.67.refs_2_), channel_id=1, source_target_pairs={{8,16},{9,17},{10,18},{11,19},{12,20},{13,21},{14,22},{15,23},{0,1... | collective-permute-start | bytes 1376264 | tf_op jit(solution)/shard_map/ppermute | solution.py:60
  86.9 28.1 %collective-permute-start.30 = (f32[4,56,512]{2,1,0:T(8,128)S(1)}, f32[4,56,512]{2,1,0:T(8,128)S(1)}, u32[]{:S(2)}, u32[]{:S(2)}) collective-permute-start(f32[4,56,512]{2,1,0:T(8,128)S(1)} %shard_map.67.refs_2_), channel_id=1, source_target_pairs={{0,8},{16,24},{1,9},{17,25},{2,10},{18,26},{3,11},{19,27},{4,12},{... | collective-permute-start | bytes 1376264 | tf_op jit(solution)/shard_map/ppermute | solution.py:60
  96.2 5.4 %collective-permute-start.11 = (f32[32,512]{1,0:T(8,128)S(1)}, f32[32,512]{1,0:T(8,128)S(1)}, u32[]{:S(2)}, u32[]{:S(2)}) collective-permute-start(f32[32,512]{1,0:T(8,128)S(1)} %get-tuple-element.55), channel_id=1, source_target_pairs={{1,2},{3,4},{5,6},{7,0},{2,1},{4,3},{6,5},{0,7},{9,10},{11,12},{13... | collective-permute-start | bytes 196616 | tf_op jit(solution)/shard_map/ppermute | solution.py:48
  97.3 8.4 %collective-permute-start.23 = (f32[128,512]{1,0:T(8,128)S(1)}, f32[128,512]{1,0:T(8,128)S(1)}, u32[]{:S(2)}, u32[]{:S(2)}) collective-permute-start(f32[128,512]{1,0:T(8,128)S(1)} %shard_map.61), channel_id=1, source_target_pairs={{1,2},{3,4},{5,6},{7,0},{2,1},{4,3},{6,5},{0,7},{9,10},{11,12},{13... | collective-permute-start | bytes 786440 | tf_op jit(solution)/shard_map/ppermute | solution.py:48
  100.9 22.2 %collective-permute-start.32 = (f32[4,64,512]{2,1,0:T(8,128)S(1)}, f32[4,64,512]{2,1,0:T(8,128)S(1)}, u32[]{:S(2)}, u32[]{:S(2)}) collective-permute-start(f32[4,64,512]{2,1,0:T(8,128)S(1)} %shard_map.66.refs_1_), channel_id=1, source_target_pairs={{8,16},{9,17},{10,18},{11,19},{12,20},{13,21},{14,22},{15,23},{0,1... | collective-permute-start | bytes 1572872 | tf_op jit(solution)/shard_map/ppermute | solution.py:60
  101.6 21.6 %collective-permute-start.29 = (f32[4,64,512]{2,1,0:T(8,128)S(1)}, f32[4,64,512]{2,1,0:T(8,128)S(1)}, u32[]{:S(2)}, u32[]{:S(2)}) collective-permute-start(f32[4,64,512]{2,1,0:T(8,128)S(1)} %shard_map.66.refs_1_), channel_id=1, source_target_pairs={{0,8},{16,24},{1,9},{17,25},{2,10},{18,26},{3,11},{19,27},{4,12},{... | collective-permute-start | bytes 1572872 | tf_op jit(solution)/shard_map/ppermute | solution.py:60
  105.8 4.7 %collective-permute-start.15 = (f32[32,512]{1,0:T(8,128)S(1)}, f32[32,512]{1,0:T(8,128)S(1)}, u32[]{:S(2)}, u32[]{:S(2)}) collective-permute-start(f32[32,512]{1,0:T(8,128)S(1)} %get-tuple-element.63), channel_id=1, source_target_pairs={{1,2},{3,4},{5,6},{7,0},{2,1},{4,3},{6,5},{0,7},{9,10},{11,12},{13... | collective-permute-start | bytes 196616 | tf_op jit(solution)/shard_map/ppermute | solution.py:48
  110.5 13.9 %collective-permute-start.24 = (f32[128,512]{1,0:T(8,128)S(1)}, f32[128,512]{1,0:T(8,128)S(1)}, u32[]{:S(2)}, u32[]{:S(2)}) collective-permute-start(f32[128,512]{1,0:T(8,128)S(1)} %shard_map.63), channel_id=1, source_target_pairs={{1,2},{3,4},{5,6},{7,0},{2,1},{4,3},{6,5},{0,7},{9,10},{11,12},{13... | collective-permute-start | bytes 786440 | tf_op jit(solution)/shard_map/ppermute | solution.py:48
  114.9 12.0 %collective-permute-start.17 = (f32[4,32,512]{2,1,0:T(8,128)S(1)}, f32[4,32,512]{2,1,0:T(8,128)S(1)}, u32[]{:S(2)}, u32[]{:S(2)}) collective-permute-start(f32[4,32,512]{2,1,0:T(8,128)S(1)} %shard_map.58.refs_0_), channel_id=1, source_target_pairs={{8,16},{9,17},{10,18},{11,19},{12,20},{13,21},{14,22},{15,23},{0,1... | collective-permute-start | bytes 786440 | tf_op jit(solution)/shard_map/ppermute | solution.py:60
  115.0 11.9 %collective-permute-start.16 = (f32[4,32,512]{2,1,0:T(8,128)S(1)}, f32[4,32,512]{2,1,0:T(8,128)S(1)}, u32[]{:S(2)}, u32[]{:S(2)}) collective-permute-start(f32[4,32,512]{2,1,0:T(8,128)S(1)} %shard_map.58.refs_0_), channel_id=1, source_target_pairs={{0,8},{16,24},{1,9},{17,25},{2,10},{18,26},{3,11},{19,27},{4,12},{... | collective-permute-start | bytes 786440 | tf_op jit(solution)/shard_map/ppermute | solution.py:60
